TPU v7x, 32 devices: a whole 2x2x4 slice. The times are simulated.
32 devices in a mesh: rows: 4 (over y, x), wide: 8 (over z, core).
Axes of the slice: x: 2, y: 2, z: 4, core: 2. Of those that a mesh axis runs over, the one named last changes fastest.
Arguments:
- tokens: bfloat16 [4, 4096, 768], P('rows', 'wide'), may hold values from -6 to 6
- segments: int32 [4, 4096], P('rows'), may hold values from 0 to 3, never falling along the last dimension, each value on 1 to 2048 neighbouring positions
- ln1_gain: bfloat16 [768], P(('rows', 'wide')), may hold values from 0.25 to 1.75
- ln1_bias: bfloat16 [768], P(('rows', 'wide')), may hold values from -1.75 to 1.75
- ln2_gain: bfloat16 [768], P(('rows', 'wide')), may hold values from 0.25 to 1.75
- ln2_bias: bfloat16 [768], P(('rows', 'wide')), may hold values from -1.75 to 1.75
- q_weight: bfloat16 [768, 768], P(('rows', 'wide')), may hold values from -0.21875 to 0.21875
- q_bias: bfloat16 [768], P(('rows', 'wide')), may hold values from -3 to 3
- kv_weight: bfloat16 [768, 128], P(('rows', 'wide')), may hold values from -0.21875 to 0.21875
- k_bias: bfloat16 [64], replicated, may hold values from -3 to 3
- out_weight: bfloat16 [768, 768], P(('rows', 'wide')), may hold values from -1.75 to 1.75
- out_bias: bfloat16 [768], P(('rows', 'wide')), may hold values from -3 to 3
- up_weight: bfloat16 [768, 3072], P(('rows', 'wide')), may hold values from -0.21875 to 0.21875
- up_bias: bfloat16 [3072], P(('rows', 'wide')), may hold values from -3 to 3
- down_weight: bfloat16 [3072, 768], P(('rows', 'wide')), may hold values from -0.109375 to 0.109375
- cotangent: bfloat16 [4, 4096, 768], P('rows', 'wide'), may hold values from -8 to 8
Outputs:
- layer_out: bfloat16 [4, 4096, 768], P('rows', 'wide')
- input_grad: float32 [4, 4096, 768], P('rows', 'wide')
- grad_ln1_gain: float32 [768], P(('rows', 'wide'))
- grad_ln1_bias: float32 [768], P(('rows', 'wide'))
- grad_ln2_gain: float32 [768], P(('rows', 'wide'))
- grad_ln2_bias: float32 [768], P(('rows', 'wide'))
- grad_q_weight: float32 [768, 768], P(('rows', 'wide'))
- grad_q_bias: float32 [768], P(('rows', 'wide'))
- grad_kv_weight: float32 [768, 128], P(('rows', 'wide'))
- grad_k_bias: float32 [64], replicated
- grad_out_weight: float32 [768, 768], P(('rows', 'wide'))
- grad_out_bias: float32 [768], P(('rows', 'wide'))
- grad_up_weight: float32 [768, 3072], P(('rows', 'wide'))
- grad_up_bias: float32 [3072], P(('rows', 'wide'))
- grad_down_weight: float32 [3072, 768], P(('rows', 'wide'))
Inputs may be any that keep to these rules, and one draw needn't show every extreme that they name: `segments`: along each row segment numbers never fall and start at 0; each document holds 1 to 2048 tokens and some document holds exactly 2048.
All inputs are finite; a program needn't handle non-finite values.
Results may differ from a plain program's by a relative error of at most 0.015.
The roundings to bfloat16 on the way count: a program that leaves them out, or rounds other values in their place, can miss the bound.
Values may be sent and summed in bfloat16 or wider, within the bound.
No kernel may reach another device: no remote copies, remote signals or barrier semaphores. Data moves between devices by JAX's collectives and lax.ppermute only.
A program may use at most 192 MiB of HBM per device.

v0:
```python
import jax
import jax.numpy as jnp
from jax import lax
from jax.sharding import PartitionSpec as P

D = 768
HEADS = 12
HD = 64
ROT = 16
DOC = 2048
GROUPS = 4


norm_eps = 1e-05


def layer_norm(values, scale_vec, shift_vec):
    center = values - jnp.mean(values, axis=-1, keepdims=True)
    spread = jnp.mean(center * center, axis=-1, keepdims=True)
    return center * lax.rsqrt(spread + norm_eps) * scale_vec + shift_vec


def rotate(values, cosine_table, sine_table, direction):
    half_rot = ROT // 2
    lower_part = values[..., :half_rot]
    upper_part = values[..., half_rot:ROT]
    turned_a = lower_part * cosine_table - direction * upper_part * sine_table
    turned_b = upper_part * cosine_table + direction * lower_part * sine_table
    return jnp.concatenate([turned_a, turned_b, values[..., ROT:]], axis=-1)


def rope_tables(relative):
    frequency = 10000.0 ** (-(jnp.arange(ROT // 2, dtype=jnp.float32) * 2.0 / ROT))
    angles = relative.astype(jnp.float32)[:, None] * frequency
    return (jnp.cos(angles), jnp.sin(angles))


def relative_places(segrow):
    places = jnp.arange(segrow.shape[0], dtype=jnp.int32)
    doc_begins = jnp.concatenate([jnp.ones((1,), bool), segrow[1:] != segrow[:-1]])
    return places - lax.cummax(jnp.where(doc_begins, places, 0), axis=0)


def window_len(piece_len):
    return DOC + (piece_len + 127) // 128 * 128


def group_size(pieces, piece_len, head_count):
    size_now = 1
    while size_now * piece_len * head_count < 512 and pieces % (size_now * 2) == 0:
        size_now = size_now * 2
    return size_now


def piece_scores(query_piece, start_at, padded_kv, padded_seg, segrow, window_rows):
    piece_len = query_piece.shape[0]
    window = lax.dynamic_slice_in_dim(padded_kv, start_at + piece_len, window_rows, 0)
    key_part = window[:, :HD]
    value_part = window[:, HD:]
    seg_keys = lax.dynamic_slice_in_dim(padded_seg, start_at + piece_len, window_rows, 0)
    seg_query = lax.dynamic_slice_in_dim(segrow, start_at, piece_len, 0)
    query_places = start_at + jnp.arange(piece_len, dtype=jnp.int32)
    key_places = start_at + piece_len - window_rows + jnp.arange(window_rows, dtype=jnp.int32)
    allowed = (seg_query[:, None] == seg_keys[None, :]) & (
        key_places[None, :] <= query_places[:, None]
    )
    scores = jnp.einsum(
        "phd,wd->hpw", query_piece, key_part, preferred_element_type=jnp.float32
    ) * HD ** (-0.5)
    scores = jnp.where(allowed[None], scores, -1e30)
    return (scores, key_part, value_part)


def piece_forward(query_piece, start_at, padded_kv, padded_seg, segrow, window_rows):
    scores, key_part, value_part = piece_scores(
        query_piece, start_at, padded_kv, padded_seg, segrow, window_rows
    )
    row_peak = jnp.max(scores, axis=-1, keepdims=True)
    exp_terms = jnp.exp(scores - row_peak)
    row_total = jnp.sum(exp_terms, axis=-1, keepdims=True)
    soft_weights = (exp_terms / row_total).astype(jnp.bfloat16)
    attended = jnp.einsum(
        "hpw,wd->phd", soft_weights, value_part, preferred_element_type=jnp.float32
    )
    return (attended.astype(jnp.bfloat16), (row_peak + jnp.log(row_total))[..., 0])


def piece_backward(
    query_piece, start_at, grad_piece, log_total, padded_kv, padded_seg, segrow, window_rows
):
    scores, key_part, value_part = piece_scores(
        query_piece, start_at, padded_kv, padded_seg, segrow, window_rows
    )
    soft_weights = jnp.exp(scores - log_total[..., None])
    grad_values = jnp.einsum(
        "hpw,phd->wd",
        soft_weights.astype(jnp.bfloat16),
        grad_piece,
        preferred_element_type=jnp.float32,
    )
    grad_soft = jnp.einsum(
        "phd,wd->hpw", grad_piece, value_part, preferred_element_type=jnp.float32
    )
    row_delta = jnp.sum(soft_weights * grad_soft, axis=-1, keepdims=True)
    grad_scores = (soft_weights * (grad_soft - row_delta)).astype(jnp.bfloat16)
    grad_query = jnp.einsum(
        "hpw,wd->phd", grad_scores, key_part, preferred_element_type=jnp.float32
    ) * HD ** (-0.5)
    grad_keys = jnp.einsum(
        "hpw,phd->wd", grad_scores, query_piece, preferred_element_type=jnp.float32
    ) * HD ** (-0.5)
    return (grad_query.astype(jnp.bfloat16), jnp.concatenate([grad_keys, grad_values], axis=-1))


def attend(query_pieces, starts, padded_kv, padded_seg, segrow):
    pieces, piece_len, head_count = (
        query_pieces.shape[0],
        query_pieces.shape[1],
        query_pieces.shape[2],
    )
    window_rows = window_len(piece_len)
    per_block = group_size(pieces, piece_len, head_count)
    blocks_query = query_pieces.reshape(pieces // per_block, per_block, piece_len, head_count, HD)
    blocks_start = starts.reshape(pieces // per_block, per_block)

    def one_block(operands):
        query_block, start_block = operands
        return jax.vmap(
            lambda query_piece, start_at: piece_forward(
                query_piece, start_at, padded_kv, padded_seg, segrow, window_rows
            )
        )(query_block, start_block)

    attended, log_totals = lax.map(one_block, (blocks_query, blocks_start))
    return (
        attended.reshape(pieces, piece_len, head_count, HD),
        log_totals.reshape(pieces, head_count, piece_len),
    )


def attend_back(query_pieces, starts, grad_pieces, log_totals, padded_kv, padded_seg, segrow):
    pieces, piece_len, head_count = (
        query_pieces.shape[0],
        query_pieces.shape[1],
        query_pieces.shape[2],
    )
    window_rows = window_len(piece_len)
    per_block = group_size(pieces, piece_len, head_count)
    block_num = pieces // per_block
    blocks_query = query_pieces.reshape(block_num, per_block, piece_len, head_count, HD)
    blocks_start = starts.reshape(block_num, per_block)
    blocks_grad = grad_pieces.reshape(block_num, per_block, piece_len, head_count, HD)
    blocks_log = log_totals.reshape(block_num, per_block, head_count, piece_len)
    buffer_start = jnp.zeros((padded_kv.shape[0], 2 * HD), jnp.float32)

    def one_block(buffer, operands):
        query_block, start_block, grad_block, log_block = operands
        grad_query, grad_windows = jax.vmap(
            lambda query_piece, start_at, grad_piece, log_total: piece_backward(
                query_piece,
                start_at,
                grad_piece,
                log_total,
                padded_kv,
                padded_seg,
                segrow,
                window_rows,
            )
        )(query_block, start_block, grad_block, log_block)

        def add_piece(item_index, accum_buffer):
            offset = start_block[item_index] + piece_len
            region = lax.dynamic_slice_in_dim(accum_buffer, offset, window_rows, 0)
            return lax.dynamic_update_slice_in_dim(
                accum_buffer, region + grad_windows[item_index], offset, 0
            )

        return (lax.fori_loop(0, per_block, add_piece, buffer), grad_query)

    buffer, grad_query = lax.scan(
        one_block, buffer_start, (blocks_query, blocks_start, blocks_grad, blocks_log)
    )
    return (grad_query.reshape(pieces, piece_len, head_count, HD), buffer[window_rows:])


def contract_rows(left, right):
    return lax.dot_general(
        left, right, (((0,), (0,)), ((), ())), preferred_element_type=jnp.float32
    )


def contract_cols(left, right):
    return lax.dot_general(
        left, right, (((1,), (1,)), ((), ())), preferred_element_type=jnp.float32
    )


def shards(
    tokens,
    segments,
    ln1_gain,
    ln1_bias,
    ln2_gain,
    ln2_bias,
    q_weight,
    q_bias,
    kv_weight,
    k_bias,
    out_weight,
    out_bias,
    up_weight,
    up_bias,
    down_weight,
    cotangent,
):
    wide_size = lax.axis_size("wide")
    wide_rank = lax.axis_index("wide")
    blocks_per_group = wide_size // GROUPS
    own_tokens = tokens.shape[1]
    piece_len = own_tokens // blocks_per_group
    block_rank = wide_rank % blocks_per_group
    heads_group = HEADS // GROUPS
    group_width = heads_group * HD
    features = tokens[0].astype(jnp.float32)
    segrow = segments[0]
    own_start = wide_rank * own_tokens
    own_relative = lax.dynamic_slice_in_dim(relative_places(segrow), own_start, own_tokens, 0)
    cosine_table, sine_table = rope_tables(own_relative)
    gathered = (
        lax.all_gather(ln1_gain, ("rows", "wide"), axis=0, tiled=True),
        lax.all_gather(ln1_bias, ("rows", "wide"), axis=0, tiled=True),
        lax.all_gather(ln2_gain, ("rows", "wide"), axis=0, tiled=True),
        lax.all_gather(ln2_bias, ("rows", "wide"), axis=0, tiled=True),
        lax.all_gather(q_weight, ("rows", "wide"), axis=0, tiled=True),
        lax.all_gather(q_bias, ("rows", "wide"), axis=0, tiled=True),
        lax.all_gather(kv_weight, ("rows", "wide"), axis=0, tiled=True),
        lax.all_gather(out_weight, ("rows", "wide"), axis=0, tiled=True),
        lax.all_gather(out_bias, ("rows", "wide"), axis=0, tiled=True),
        lax.all_gather(up_weight, ("rows", "wide"), axis=0, tiled=True),
        lax.all_gather(up_bias, ("rows", "wide"), axis=0, tiled=True),
        lax.all_gather(down_weight, ("rows", "wide"), axis=0, tiled=True),
    )
    (
        gain_one,
        shift_one,
        gain_two,
        shift_two,
        query_weight,
        query_bias,
        pair_weight,
        proj_weight,
        proj_bias,
        hidden_weight,
        hidden_bias,
        back_weight,
    ) = gathered
    normed_one_f, pull_one = jax.vjp(
        layer_norm, features, gain_one.astype(jnp.float32), shift_one.astype(jnp.float32)
    )
    normed_two_f, pull_two = jax.vjp(
        layer_norm, features, gain_two.astype(jnp.float32), shift_two.astype(jnp.float32)
    )
    normed_one = normed_one_f.astype(jnp.bfloat16)
    normed_two = normed_two_f.astype(jnp.bfloat16)
    query_pre = jnp.einsum(
        "td,dgx->gtx",
        normed_one,
        query_weight.reshape(D, GROUPS, group_width),
        preferred_element_type=jnp.float32,
    ) + query_bias.astype(jnp.float32).reshape(GROUPS, 1, group_width)
    query_heads = (
        rotate(
            query_pre.reshape(GROUPS, own_tokens, heads_group, HD),
            cosine_table[None, :, None, :],
            sine_table[None, :, None, :],
            1.0,
        )
        .astype(jnp.bfloat16)
        .reshape(GROUPS, own_tokens, group_width)
    )
    pair_proj = jnp.dot(normed_one, pair_weight, preferred_element_type=jnp.float32)
    key_rot = rotate(
        pair_proj[:, :HD] + k_bias.astype(jnp.float32), cosine_table, sine_table, 1.0
    ).astype(jnp.bfloat16)
    own_pairs = jnp.concatenate([key_rot, pair_proj[:, HD:].astype(jnp.bfloat16)], axis=1)
    window_rows = window_len(piece_len)
    all_pairs = lax.all_gather(own_pairs, "wide", axis=0, tiled=True)
    kv_source = jnp.concatenate([jnp.zeros((window_rows, 2 * HD), jnp.bfloat16), all_pairs], axis=0)
    seg_source = jnp.concatenate([jnp.full((window_rows,), -1, jnp.int32), segrow], axis=0)
    outgoing = query_heads.reshape(GROUPS * blocks_per_group, piece_len, group_width)
    received = lax.all_to_all(outgoing, "wide", split_axis=0, concat_axis=0, tiled=True)
    query_pieces = received.reshape(wide_size, piece_len, heads_group, HD)
    starts = jnp.arange(wide_size, dtype=jnp.int32) * own_tokens + block_rank * piece_len
    attended, log_totals = attend(query_pieces, starts, kv_source, seg_source, segrow)
    returned = lax.all_to_all(
        attended.reshape(wide_size, piece_len, group_width),
        "wide",
        split_axis=0,
        concat_axis=0,
        tiled=True,
    )
    attn_heads = returned.reshape(GROUPS, own_tokens, group_width)
    attn_out = jnp.einsum(
        "gtx,gxe->te",
        attn_heads,
        proj_weight.reshape(GROUPS, group_width, D),
        preferred_element_type=jnp.float32,
    )
    hidden_pre = jnp.dot(
        normed_two, hidden_weight, preferred_element_type=jnp.float32
    ) + hidden_bias.astype(jnp.float32)
    hidden_f, gelu_pull = jax.vjp(
        lambda pre_act: jax.nn.gelu(pre_act, approximate=False), hidden_pre
    )
    hidden = hidden_f.astype(jnp.bfloat16)
    mlp_out = jnp.dot(hidden, back_weight, preferred_element_type=jnp.float32)
    layer_out = (features + attn_out + mlp_out + proj_bias.astype(jnp.float32)).astype(jnp.bfloat16)
    query_weight, pair_weight, proj_weight, hidden_weight, back_weight = (
        lax.all_gather(q_weight, ("rows", "wide"), axis=0, tiled=True),
        lax.all_gather(kv_weight, ("rows", "wide"), axis=0, tiled=True),
        lax.all_gather(out_weight, ("rows", "wide"), axis=0, tiled=True),
        lax.all_gather(up_weight, ("rows", "wide"), axis=0, tiled=True),
        lax.all_gather(down_weight, ("rows", "wide"), axis=0, tiled=True),
    )
    grad_out = cotangent[0]
    grad_float = grad_out.astype(jnp.float32)
    grad_proj = jnp.einsum(
        "gtx,te->gxe", attn_heads, grad_out, preferred_element_type=jnp.float32
    ).reshape(D, D)
    grad_proj_bias = jnp.sum(grad_float, axis=0)
    grad_back = contract_rows(hidden, grad_out)
    grad_heads = jnp.einsum(
        "te,gxe->gtx",
        grad_out,
        proj_weight.reshape(GROUPS, group_width, D),
        preferred_element_type=jnp.float32,
    ).astype(jnp.bfloat16)
    grad_recv = lax.all_to_all(
        grad_heads.reshape(GROUPS * blocks_per_group, piece_len, group_width),
        "wide",
        split_axis=0,
        concat_axis=0,
        tiled=True,
    )
    grad_query, grad_pairs = attend_back(
        query_pieces,
        starts,
        grad_recv.reshape(wide_size, piece_len, heads_group, HD),
        log_totals,
        kv_source,
        seg_source,
        segrow,
    )
    grad_query_heads = lax.all_to_all(
        grad_query.reshape(wide_size, piece_len, group_width),
        "wide",
        split_axis=0,
        concat_axis=0,
        tiled=True,
    ).reshape(GROUPS, own_tokens, group_width)
    pair_sums = lax.psum_scatter(grad_pairs, "wide", scatter_dimension=0, tiled=True)
    grad_key = pair_sums[:, :HD].astype(jnp.bfloat16)
    grad_value = pair_sums[:, HD:].astype(jnp.bfloat16)
    key_pre_grad = rotate(grad_key.astype(jnp.float32), cosine_table, sine_table, -1.0).astype(
        jnp.bfloat16
    )
    query_pre_grad = (
        rotate(
            grad_query_heads.astype(jnp.float32).reshape(GROUPS, own_tokens, heads_group, HD),
            cosine_table[None, :, None, :],
            sine_table[None, :, None, :],
            -1.0,
        )
        .astype(jnp.bfloat16)
        .reshape(GROUPS, own_tokens, group_width)
    )
    pair_grad = jnp.concatenate([key_pre_grad, grad_value], axis=1)
    grouped_weight = query_weight.reshape(D, GROUPS, group_width)
    grad_query_weight = jnp.einsum(
        "td,gtx->dgx", normed_one, query_pre_grad, preferred_element_type=jnp.float32
    ).reshape(D, D)
    grad_query_bias = jnp.sum(query_pre_grad.astype(jnp.float32), axis=1).reshape(D)
    grad_pair_weight = contract_rows(normed_one, pair_grad)
    key_bias_part = jnp.sum(key_pre_grad.astype(jnp.float32), axis=0)
    grad_hidden = contract_cols(grad_out, back_weight)
    grad_pre = gelu_pull(grad_hidden)[0].astype(jnp.bfloat16)
    grad_hidden_weight = contract_rows(normed_two, grad_pre)
    grad_hidden_bias = jnp.sum(grad_pre.astype(jnp.float32), axis=0)
    grad_normed_one = jnp.einsum(
        "gtx,dgx->td", query_pre_grad, grouped_weight, preferred_element_type=jnp.float32
    )
    grad_normed_one = grad_normed_one + contract_cols(pair_grad, pair_weight)
    grad_normed_two = contract_cols(grad_pre, hidden_weight)
    input_one, grad_gain_one, grad_shift_one = pull_one(grad_normed_one)
    input_two, grad_gain_two, grad_shift_two = pull_two(grad_normed_two)
    input_grad = grad_float + input_one + input_two
    summed = (
        lax.psum_scatter(grad_gain_one, ("rows", "wide"), scatter_dimension=0, tiled=True),
        lax.psum_scatter(grad_shift_one, ("rows", "wide"), scatter_dimension=0, tiled=True),
        lax.psum_scatter(grad_gain_two, ("rows", "wide"), scatter_dimension=0, tiled=True),
        lax.psum_scatter(grad_shift_two, ("rows", "wide"), scatter_dimension=0, tiled=True),
        lax.psum_scatter(grad_query_weight, ("rows", "wide"), scatter_dimension=0, tiled=True),
        lax.psum_scatter(grad_query_bias, ("rows", "wide"), scatter_dimension=0, tiled=True),
        lax.psum_scatter(grad_pair_weight, ("rows", "wide"), scatter_dimension=0, tiled=True),
        lax.psum_scatter(grad_proj, ("rows", "wide"), scatter_dimension=0, tiled=True),
        lax.psum_scatter(grad_proj_bias, ("rows", "wide"), scatter_dimension=0, tiled=True),
        lax.psum_scatter(grad_hidden_weight, ("rows", "wide"), scatter_dimension=0, tiled=True),
        lax.psum_scatter(grad_hidden_bias, ("rows", "wide"), scatter_dimension=0, tiled=True),
        lax.psum_scatter(grad_back, ("rows", "wide"), scatter_dimension=0, tiled=True),
    )
    key_bias_sum = lax.psum(key_bias_part, ("rows", "wide"))
    return (
        layer_out[None],
        input_grad[None],
        summed[0],
        summed[1],
        summed[2],
        summed[3],
        summed[4],
        summed[5],
        summed[6],
        key_bias_sum,
        summed[7],
        summed[8],
        summed[9],
        summed[10],
        summed[11],
    )


def solution(mesh):
    return jax.shard_map(
        shards,
        mesh=mesh,
        in_specs=(
            P("rows", "wide", None),
            P("rows", None),
            P(("rows", "wide")),
            P(("rows", "wide")),
            P(("rows", "wide")),
            P(("rows", "wide")),
            P(("rows", "wide"), None),
            P(("rows", "wide")),
            P(("rows", "wide"), None),
            P(),
            P(("rows", "wide"), None),
            P(("rows", "wide")),
            P(("rows", "wide"), None),
            P(("rows", "wide")),
            P(("rows", "wide"), None),
            P("rows", "wide", None),
        ),
        out_specs=(
            P("rows", "wide", None),
            P("rows", "wide", None),
            P(("rows", "wide")),
            P(("rows", "wide")),
            P(("rows", "wide")),
            P(("rows", "wide")),
            P(("rows", "wide"), None),
            P(("rows", "wide")),
            P(("rows", "wide"), None),
            P(),
            P(("rows", "wide"), None),
            P(("rows", "wide")),
            P(("rows", "wide"), None),
            P(("rows", "wide")),
            P(("rows", "wide"), None),
        ),
        check_vma=False,
    )
```

profile of v0, /device:TPU:25, one launch (start us, length us, event | category | flops | bytes accessed | tf_op | source)
XLA Modules:
  0.0 1404.7 jit_solution(12103574381834659398)
XLA Ops:
  10.3 33.7 %all_gather.46 = bf16[768,128]{1,0:T(8,128)(2,1)S(1)} all-gather(bf16[24,128]{1,0:T(8,128)(2,1)} %param.28), channel_id=1, replica_groups=mesh['rows'=4,'wide'=8] {'rows','wide'}, dimensions={0}, use_global_device_ids=true | all-gather | bytes 202752 | tf_op jit(solution)/shard_map/all_gather | solution.py:236
  49.9 44.6 %all-reduce.18 = (bf16[768]{0:T(1024)(128)(2,1)}, bf16[768]{0:T(1024)(128)(2,1)}, bf16[3072]{0:T(1024)(128)(2,1)}, bf16[768]{0:T(1024)(128)(2,1)S(1)}, bf16[768]...) all-reduce(bf16[768]{0:T(1024)(128)(2,1)S(1)} %dynamic-update-slice, ...), channel_id=1, replica_groups=mesh['rows'=4,'wide'=8] {'rows','wide'}, use_global_device_ids=true, to_apply=%add.6 | all-reduce | flops 7680 | bytes 30720
  107.7 6.7 all-to-all-start
  115.6 16.3 %all-gather.6.cloned.1.call-done = bf16[4096,128]{0,1:T(8,128)(2,1)} async-done(((bf16[512,128]{0,1:T(8,128)(2,1)}), bf16[4096,128]{0,1:T(8,128)(2,1)}) %all-gather.6.cloned.1.call-update) | async-done | bytes 1048592 | tf_op jit(solution)/shard_map/all_gather | solution.py:287
  134.5 54.3 %all-gather.10.cloned.1.call-done = bf16[768,768]{1,0:T(8,128)(2,1)} async-done(((bf16[24,768]{1,0:T(8,128)(2,1)}), bf16[768,768]{1,0:T(8,128)(2,1)}) %all-gather.10.cloned.1.call-update) | async-done | bytes 1179664 | tf_op jit(solution)/shard_map/all_gather | solution.py:237
  198.5 117.7 %while.43 = (s32[]{:T(128)}, bf16[8,1,256,3,64]{2,4,3,1,0:T(8,128)(2,1)S(1)}, f32[8,1,3,256]{3,2,1,0:T(4,128)}, s32[8,1]{0,1:T(1,128)}, bf16[6400,128]{0,1:T(8,1...) while((s32[]{:T(128)}, ...), condition=%wide.region_7.8_spmd, body=%wide.region_4.7_spmd.sunk | while | flops 468961024 | bytes 24459524 | solution.py:134
  319.3 306.2 %while.44 = (s32[]{:T(128)}, f32[6400,128]{0,1:T(8,128)}, bf16[8,1,256,3,64]{2,4,3,1,0:T(8,128)(2,1)}, s32[8,1]{0,1:T(1,128)}, s32[4096]{0:T(1024)S(1)}, /*index...) while((s32[]{:T(128)}, f32[6400,128]{0,1:T(8,128)}, ...), condition=%wide.region_10.11_spmd, body=%wide.region_8.10_spmd.sunk | while | flops 1150994176 | bytes 80483224 | solution.py:180
  349.2 6.2 dynamic_update_slice.49
  387.7 6.2 dynamic_update_slice.49
  426.1 6.1 dynamic_update_slice.49
  630.1 34.8 %all_to_all.20 = bf16[8,256,192]{1,2,0:T(8,128)(2,1)S(1)} all-to-all(bf16[8,256,192]{1,2,0:T(8,128)(2,1)S(1)} %bitcast.365), channel_id=1, replica_groups=mesh['rows'=4,'wide'=8] {'wide'}, dimensions={0} | all-to-all | bytes 1572864 | tf_op jit(solution)/shard_map/all_to_all | solution.py:295
  668.3 8.1 all-to-all-start.3
  676.4 20.0 %all-to-all-done.3 = bf16[8,256,192]{1,2,0:T(8,128)(2,1)S(1)} async-done(((bf16[8,256,192]{1,2,0:T(8,128)(2,1)}), bf16[8,256,192]{1,2,0:T(8,128)(2,1)S(1)}, u32[]{:S(2)}, u32[]{:S(2)}) %all-to-all-start.3) | async-done | bytes 786464 | tf_op jit(solution)/shard_map/all_to_all | solution.py:354
  707.5 36.1 %all-gather.12.cloned.1.call-done = bf16[768,3072]{1,0:T(8,128)(2,1)} async-done(((bf16[24,3072]{1,0:T(8,128)(2,1)}), bf16[768,3072]{1,0:T(8,128)(2,1)}) %all-gather.12.cloned.1.call-update) | async-done | bytes 4718608 | tf_op jit(solution)/shard_map/all_gather | solution.py:239
  743.7 19.7 %multiply_convert_fusion = (bf16[512,3072]{1,0:T(8,128)(2,1)}, f32[512,3072]{1,0:T(8,128)}, f32[512,3072]{1,0:T(8,128)}) fusion(f32[3072]{0:T(1024)S(1)} %convert_element_type.178, bf16[768,3072]{1,0:T(8,128)(2,1)} %all-gather.12.cloned.1.call-done, bf16[1,512,768]{2,1,0:T(8,128)(2,1)S(1)} %copy-done.3, f32[768]{0:T(1024)S(1)} %convert_element_type.176, ...), kind=kOutput, calls=%fused_computation.67 | convolution fusion | flops 2522087424 | bytes 21256192 | tf_op jit(solution)/shard_map/dot_general | solution.py:309
  763.3 45.7 %all-gather.14.cloned.1.call-done = bf16[3072,768]{1,0:T(8,128)(2,1)} async-done(((bf16[96,768]{1,0:T(8,128)(2,1)}), bf16[3072,768]{1,0:T(8,128)(2,1)}) %all-gather.14.cloned.1.call-update) | async-done | bytes 4718608 | tf_op jit(solution)/shard_map/all_gather | solution.py:241
  809.0 8.5 convert_reduce_fusion
  825.1 8.2 fusion.90
  848.8 40.1 %all-reduce.17 = (f32[768]{0:T(1024)S(1)}, f32[768]{0:T(1024)S(1)}, f32[768]{0:T(1024)S(1)}, f32[768]{0:T(1024)S(1)}, f32[768]{0:T(1024)S(1)}, /*index=5*/f32[64]{0:T(128)}, f32[768]{0:T(1024)S(1)}, f32[3072]{0:T(1024)S(1)}) all-reduce(f32[768]{0:T(1024)S(1)} %get-tuple-element.526, ...), channel_id=3, replica_groups=mesh['rows'=4,'wide'=8] {'rows','wide'}, use_global_device_ids=true, to_apply=%region_17.18.clone | all-reduce | flops 7744 | bytes 61952
  900.9 10.1 reduce-scatter.13.cloned.1.call-done
  911.0 99.6 %reduce-scatter.19.cloned.1.call-done = f32[24,128]{1,0:T(8,128)} async-done(((f32[768,128]{1,0:T(8,128)}), f32[24,128]{1,0:T(8,128)}) %reduce-scatter.19.cloned.1.call-update) | async-done | bytes 12304
  1010.6 104.4 %reduce-scatter.11.cloned.1.call-done = f32[24,768]{1,0:T(8,128)} async-done(((f32[768,768]{1,0:T(8,128)}), f32[24,768]{1,0:T(8,128)}) %reduce-scatter.11.cloned.1.call-update) | async-done | bytes 73744 | tf_op jit(solution)/shard_map/reduce_scatter | solution.py:402
  1115.0 141.8 %reduce-scatter.15.cloned.1.call-done = f32[24,3072]{1,0:T(8,128)} async-done(((f32[768,3072]{1,0:T(8,128)}), f32[24,3072]{1,0:T(8,128)}) %reduce-scatter.15.cloned.1.call-update) | async-done | bytes 294928 | tf_op jit(solution)/shard_map/reduce_scatter | solution.py:407
  1256.8 141.1 %reduce-scatter.17.cloned.1.call-done = f32[96,768]{1,0:T(8,128)} async-done(((f32[3072,768]{1,0:T(8,128)}), f32[96,768]{1,0:T(8,128)}) %reduce-scatter.17.cloned.1.call-update) | async-done | bytes 294928 | tf_op jit(solution)/shard_map/reduce_scatter | solution.py:409
  (451 shorter events, 421.4 us)
Async XLA Ops:
  7.2 95.4 %copy-start.2 = (bf16[1,512,768]{2,1,0:T(8,128)(2,1)S(1)}, bf16[1,512,768]{2,1,0:T(8,128)(2,1)}, u32[]{:S(2)}) copy-start(bf16[1,512,768]{2,1,0:T(8,128)(2,1)} %param.20) | copy-start | bytes 2359300
  7.2 95.4 %all-gather.8.cloned.1.call-start = ((), (), s32[]{:S(2)}) async-start(), calls=%async_computation.11 | async-start | bytes 1216512 | tf_op jit(solution)/shard_map/all_gather | solution.py:234
  7.9 124.0 %all-gather.6.cloned.1.call-start = ((), (), s32[]{:S(2)}) async-start(), calls=%async_computation.10 | async-start | bytes 1179648 | tf_op jit(solution)/shard_map/all_gather | solution.py:287
  44.0 60.8 %copy-start.15 = (bf16[768,128]{1,0:T(8,128)(2,1)}, bf16[768,128]{1,0:T(8,128)(2,1)S(1)}, u32[]{:S(2)}) copy-start(bf16[768,128]{1,0:T(8,128)(2,1)S(1)} %all_gather.46) | copy-start | bytes 589828
  101.8 87.0 %all-gather.10.cloned.1.call-start = ((), (), s32[]{:S(2)}) async-start(), calls=%async_computation.12 | async-start | bytes 1216512 | tf_op jit(solution)/shard_map/all_gather | solution.py:237
  106.7 82.1 %copy-start.12 = (bf16[1,512,768]{2,1,0:T(8,128)(2,1)S(1)}, bf16[1,512,768]{2,1,0:T(8,128)(2,1)}, u32[]{:S(2)}) copy-start(bf16[1,512,768]{2,1,0:T(8,128)(2,1)} %param.35) | copy-start | bytes 2359300
  107.7 85.0 %all-to-all-start = ((bf16[8,256,192]{1,2,0:T(8,128)(2,1)}), bf16[8,256,192]{1,2,0:T(8,128)(2,1)}, u32[]{:S(2)}, u32[]{:S(2)}) async-start(bf16[8,256,192]{1,2,0:T(8,128)(2,1)} %copy.77), calls=%async_computation | async-start | bytes 1572864 | tf_op jit(solution)/shard_map/all_to_all | solution.py:291
  192.7 123.6 %all-to-all-start.2 = ((bf16[8,256,192]{1,2,0:T(8,128)(2,1)}), bf16[8,256,192]{1,2,0:T(8,128)(2,1)}, u32[]{:S(2)}, u32[]{:S(2)}) async-start(bf16[8,256,192]{1,2,0:T(8,128)(2,1)} %copy.82), calls=%async_computation.2 | async-start | bytes 1572864 | tf_op jit(solution)/shard_map/all_to_all | solution.py:338
  198.3 502.0 %reduce-scatter.9.cloned.1.call-start = ((), (), s32[]{:S(2)}) async-start(), calls=%async_computation.15 | async-start | bytes 2359296 | tf_op jit(solution)/shard_map/reduce_scatter | solution.py:361
  344.5 10.9 copy-start
  383.0 10.8 copy-start
  421.4 10.8 copy-start
  459.8 10.8 copy-start
  498.2 10.7 copy-start
  628.7 115.0 %all-gather.12.cloned.1.call-start = ((), (), s32[]{:S(2)}) async-start(), calls=%async_computation.13 | async-start | bytes 4866048 | tf_op jit(solution)/shard_map/all_gather | solution.py:239
  629.3 179.8 %all-gather.14.cloned.1.call-start = ((), (), s32[]{:S(2)}) async-start(), calls=%async_computation.14 | async-start | bytes 4866048 | tf_op jit(solution)/shard_map/all_gather | solution.py:241
  629.8 281.1 %reduce-scatter.13.cloned.1.call-start = ((), (), s32[]{:S(2)}) async-start(), calls=%async_computation.17 | async-start | bytes 2433024 | tf_op jit(solution)/shard_map/reduce_scatter | solution.py:405
  630.1 35.9 %copy-start.13 = (bf16[1,512,768]{2,1,0:T(8,128)(2,1)S(1)}, bf16[1,512,768]{2,1,0:T(8,128)(2,1)}, u32[]{:S(2)}) copy-start(bf16[1,512,768]{2,1,0:T(8,128)(2,1)} %param.35) | copy-start | bytes 2359300
  668.3 28.1 %all-to-all-start.3 = ((bf16[8,256,192]{1,2,0:T(8,128)(2,1)}), bf16[8,256,192]{1,2,0:T(8,128)(2,1)S(1)}, u32[]{:S(2)}, u32[]{:S(2)}) async-start(bf16[8,256,192]{1,2,0:T(8,128)(2,1)} %bitcast.69), calls=%async_computation.3 | async-start | bytes 1572864 | tf_op jit(solution)/shard_map/all_to_all | solution.py:354
  676.4 334.2 %reduce-scatter.19.cloned.1.call-start = ((), (), s32[]{:S(2)}) async-start(), calls=%async_computation.20 | async-start | bytes 405504
  702.7 412.3 %reduce-scatter.11.cloned.1.call-start = ((), (), s32[]{:S(2)}) async-start(), calls=%async_computation.16 | async-start | bytes 2433024 | tf_op jit(solution)/shard_map/reduce_scatter | solution.py:402
  707.2 101.8 %copy-start.14 = (bf16[1,512,768]{2,1,0:T(8,128)(2,1)S(1)}, bf16[1,512,768]{2,1,0:T(8,128)(2,1)}, u32[]{:S(2)}) copy-start(bf16[1,512,768]{2,1,0:T(8,128)(2,1)} %param.35) | copy-start | bytes 2359300
  707.2 549.5 %reduce-scatter.15.cloned.1.call-start = ((), (), s32[]{:S(2)}) async-start(), calls=%async_computation.18 | async-start | bytes 9732096 | tf_op jit(solution)/shard_map/reduce_scatter | solution.py:407
  824.6 573.3 %reduce-scatter.17.cloned.1.call-start = ((), (), s32[]{:S(2)}) async-start(), calls=%async_computation.19 | async-start | bytes 9732096 | tf_op jit(solution)/shard_map/reduce_scatter | solution.py:409
  (45 other events, 265.9 us)
Sparse Core Ops, SparseCore 0:
  11.0 54.5 all-gather.7
  101.9 29.9 all-gather.5
  134.9 53.8 all-gather.9
  628.8 45.7 reduce-scatter.8
  677.4 66.1 all-gather.11
  746.5 62.4 all-gather.13
  814.9 96.0 reduce-scatter.12
  917.2 93.3 reduce-scatter.18
  1016.5 98.5 reduce-scatter.10
  1122.4 134.3 reduce-scatter.14
  1263.3 134.6 reduce-scatter.16
where the time goes:
time: 1420 us; the launch traced here: 1400 us
  waiting for transfers between devices  672 us (47%)
  matrix products  213 us (15%)
  blocking collectives  153 us (11%)
  local copies, waits for them, and re-layouts  143 us (10%)
  other arithmetic  111 us (8%)
  loops' own time  76 us (5%)
  starting transfers between devices  21.8 us (2%)
  between operations  14.8 us (1%)
    reduce_scatter x1, waiting for transfers between devices, shards(): lax.psum_scatter(grad_hidden_weight, ('rows', 'wide'), scatter_dimension=...  142 us
    reduce_scatter x1, waiting for transfers between devices, shards(): lax.psum_scatter(grad_back, ('rows', 'wide'), scatter_dimension=0, tiled=...  141 us
    reduce_scatter x1, waiting for transfers between devices, shards(): lax.psum_scatter(grad_query_weight, ('rows', 'wide'), scatter_dimension=0...  104 us
    unnamed x12, waiting for transfers between devices  102 us
    unnamed x2, blocking collectives  84.8 us
    all_gather x1, waiting for transfers between devices, shards(): lax.all_gather(out_weight, ('rows', 'wide'), axis=0, tiled=True)  54.3 us
    dynamic_update_slice x8, local copies, waits for them, and re-layouts, add_piece(): lax.dynamic_update_slice_in_dim(accum_buffer, region + grad_windows[item_...  48.1 us
    all_gather x1, waiting for transfers between devices, shards(): lax.all_gather(down_weight, ('rows', 'wide'), axis=0, tiled=True)  45.7 us
  transfers between devices with their start and end apart: 14, of which 10 were waited for; matrix products, arithmetic and copies ran while one was open for 14% of the time, Pallas kernels for 0%

commit v1 on v0

v1 whole, which is shorter than its diff:
```python
import jax
import jax.numpy as jnp
from jax import lax
from jax.experimental import pallas as pl
from jax.experimental.pallas import tpu as pltpu
from jax.sharding import Mesh, PartitionSpec as P

D = 768
HEADS = 12
HD = 64
ROT = 16
DOC = 2048
FF = 3072
MAX_SEGS = 32
norm_eps = 1e-05
BF = jnp.bfloat16
F32 = jnp.float32
HALF = HEADS // 2 * HD
BLK = 256
GROUP = 3


def dot(left, right, dims):
    return lax.dot_general(left, right, (dims, ((), ())), preferred_element_type=F32)


def core_swap(value):
    return lax.ppermute(value, "core", [(0, 1), (1, 0)])


def rows_swap(value, bit):
    return lax.ppermute(value, "rows", [(r, r ^ bit) for r in range(4)])


def chip_shift(value, by, wrap):
    count = lax.axis_size("chip")
    pairs = [(s, (s + by) % count) for s in range(count) if wrap or 0 <= s + by < count]
    return lax.ppermute(value, "chip", pairs)


def square_line():
    return lax.axis_size("rows") == 4 and lax.axis_size("chip") == 4


def place_kernel(lines_ref, flat_ref, cross_ref, low_ref, high_ref, out_ref, sems):
    row, chip = lax.axis_index("rows"), lax.axis_index("chip")
    piece = out_ref.shape[0] // 16
    copies = []
    for turn in range(4):
        for step in range(4):
            source = (lines_ref, flat_ref, cross_ref, low_ref if step < 2 else high_ref)[turn]
            offset = (step if turn < 3 else step % 2) * piece
            spot = ((row ^ turn) * 4 + lax.rem(chip + step, 4)) * piece
            copies.append(
                pltpu.make_async_copy(
                    source.at[pl.ds(offset, piece)],
                    out_ref.at[pl.ds(pl.multiple_of(spot, piece), piece)],
                    sems.at[turn * 4 + step],
                )
            )
    for copy in copies:
        copy.start()
    for copy in copies:
        copy.wait()


def gather_chips(piece):
    if not square_line():
        return lax.all_gather(piece, ("rows", "chip"), axis=0, tiled=True)
    size = piece.shape[0]
    lines = jnp.concatenate([piece] + [chip_shift(piece, -k, True) for k in (1, 2, 3)], axis=0)
    flat, cross = rows_swap(lines, 1), rows_swap(lines, 2)
    low = rows_swap(flat[: 2 * size], 2)
    high = rows_swap(cross[2 * size :], 1)
    return pl.pallas_call(
        place_kernel,
        out_shape=jax.ShapeDtypeStruct((16 * size,) + piece.shape[1:], piece.dtype),
        in_specs=[pl.BlockSpec(memory_space=pl.ANY)] * 5,
        out_specs=pl.BlockSpec(memory_space=pl.ANY),
        scratch_shapes=[pltpu.SemaphoreType.DMA((16,))],
        cost_estimate=pl.CostEstimate(
            flops=0, transcendentals=0, bytes_accessed=64 * size * piece.shape[1]
        ),
        name="place",
    )(lines, flat, cross, low, high)


def reduce_chips(terms):
    if not square_line():
        return lax.psum_scatter(
            terms.astype(F32), ("rows", "chip"), scatter_dimension=0, tiled=True
        )
    row, chip = lax.axis_index("rows"), lax.axis_index("chip")
    size = terms.shape[0] // 16
    grid = terms.reshape((4, 4, size) + terms.shape[1:])

    def plane(bit):
        return lax.dynamic_index_in_dim(grid, row ^ bit, 0, keepdims=False)

    far, flat, cross = plane(3), plane(1), plane(2)
    from_flat = rows_swap(far[:2], 1)
    from_cross = rows_swap(far[2:], 2)
    to_flat = jnp.concatenate(
        [flat[:2], (flat[2:].astype(F32) + from_cross.astype(F32)).astype(BF)], axis=0
    )
    to_cross = jnp.concatenate(
        [(cross[:2].astype(F32) + from_flat.astype(F32)).astype(BF), cross[2:]], axis=0
    )
    got_flat, got_cross = rows_swap(to_flat, 1), rows_swap(to_cross, 2)
    own = plane(0)

    def line(step):
        spot = lax.rem(chip + step, 4)
        pick = [
            lax.dynamic_index_in_dim(part, spot, 0, keepdims=False).astype(F32)
            for part in (own, got_flat, got_cross)
        ]
        return pick[0] + pick[1] + pick[2]

    total = line(0)
    for step in (1, 2, 3):
        total = total + chip_shift(line(step).astype(BF), step, True).astype(F32)
    return total


def sum_everywhere(value):
    if not square_line():
        return lax.psum(value, ("rows", "chip", "core"))
    value = value + core_swap(value)
    for bit in (1, 2):
        value = value + lax.ppermute(value, "chip", [(s, s ^ bit) for s in range(4)])
    for bit in (1, 2):
        value = value + rows_swap(value, bit)
    return value


def by_core(core, own, other, axis):
    return jnp.where(
        core == 0,
        jnp.concatenate([own, other], axis=axis),
        jnp.concatenate([other, own], axis=axis),
    )


def attn_kernel(
    scal_ref, q_ref, g_ref, pos_ref, kv_ref, kvt_ref, o_ref, dq_ref, dkv_ref, s_ref, r_ref
):
    group, block = pl.program_id(0), pl.program_id(1)
    core = scal_ref[0]
    low, high, edge = (scal_ref[1 + 3 * block + i] for i in range(3))
    half_blocks = kv_ref.shape[0] // 2 // BLK

    @pl.when((group == 0) & (block == 0))
    def _():
        dkv_ref[...] = jnp.zeros_like(dkv_ref)

    def spot(key_block):
        per_core = scal_ref[1 + 3 * pl.num_programs(1)]
        pair = key_block // (2 * per_core)
        side = lax.rem(key_block // per_core, 2) ^ core
        place = (pair * 2 + side) * per_core + lax.rem(key_block, per_core)
        return pl.multiple_of(place * BLK, BLK)

    starts, places = pos_ref[0:1, :], pos_ref[1:2, :]
    blank = jnp.zeros((HD, BLK), BF)
    queries, grads = [], []
    for h in range(GROUP):
        query = (q_ref[h * HD : (h + 1) * HD, :].astype(F32) * HD**-0.5).astype(BF)
        grad = g_ref[h * HD : (h + 1) * HD, :]
        queries.append(jnp.concatenate([query, blank], axis=0))
        grads.append(jnp.concatenate([blank, grad], axis=0))
        r_ref[:, h * BLK : (h + 1) * BLK] = queries[h]
        r_ref[:, (GROUP + h) * BLK : (GROUP + h + 1) * BLK] = grads[h]

    def scores(key_block, peaks):
        keys = kv_ref[pl.ds(spot(key_block), BLK), :]
        key_places = key_block * BLK + lax.broadcasted_iota(jnp.int32, (BLK, BLK), 0)
        allowed = (key_places >= starts) & (key_places <= places)
        new = []
        for h in range(GROUP):
            s = dot(keys, queries[h], ((1,), (0,)))
            s = jnp.where(allowed, s, -1e30)
            s_ref[h, pl.ds(pl.multiple_of((key_block - low) * BLK, BLK), BLK), :] = s
            new.append(jnp.maximum(peaks[h], jnp.max(s, axis=0, keepdims=True)))
        return tuple(new)

    peaks = lax.fori_loop(
        low, high, scores, tuple(jnp.full((1, BLK), -1e30, F32) for _ in range(GROUP))
    )

    def expo(key_block, carry):
        values = kvt_ref[HD:, pl.ds(spot(key_block), BLK)]
        new = []
        for h in range(GROUP):
            rows = pl.ds(pl.multiple_of((key_block - low) * BLK, BLK), BLK)
            e = jnp.exp(s_ref[h, rows, :] - peaks[h])
            s_ref[h, rows, :] = e
            total, out = carry[h]
            new.append(
                (
                    total + jnp.sum(e, axis=0, keepdims=True),
                    out + dot(values, e.astype(BF), ((1,), (0,))),
                )
            )
        return tuple(new)

    sums = lax.fori_loop(
        low,
        high,
        expo,
        tuple((jnp.zeros((1, BLK), F32), jnp.zeros((HD, BLK), F32)) for _ in range(GROUP)),
    )
    inverse, delta = [], []
    for h in range(GROUP):
        total, out = sums[h]
        inverse.append(1.0 / total)
        out = out * inverse[h]
        o_ref[h * HD : (h + 1) * HD, :] = out.astype(BF)
        delta.append(jnp.sum(out * grads[h][HD:, :].astype(F32), axis=0, keepdims=True))

    def back(key_block, dqs):
        where = spot(key_block)
        pairs = kv_ref[pl.ds(where, BLK), :]
        keys = kvt_ref[:HD, pl.ds(where, BLK)]
        new, soft, grad_scores = [], [], []
        for h in range(GROUP):
            rows = pl.ds(pl.multiple_of((key_block - low) * BLK, BLK), BLK)
            p = s_ref[h, rows, :] * inverse[h]
            dp = dot(pairs, grads[h], ((1,), (0,)))
            ds = (p * (dp - delta[h])).astype(BF)
            soft.append(p.astype(BF))
            grad_scores.append(ds)
            new.append(dqs[h] + dot(keys, ds, ((1,), (0,))))
        left = jnp.concatenate(grad_scores + soft, axis=1)
        dkv_ref[pl.ds(where, BLK), :] += dot(left, r_ref[...], ((1,), (1,)))
        return tuple(new)

    dqs = lax.fori_loop(
        low, high, back, tuple(jnp.zeros((HD, BLK), F32) for _ in range(GROUP))
    )
    for h in range(GROUP):
        dq_ref[h * HD : (h + 1) * HD, :] = (dqs[h] * HD**-0.5).astype(BF)


def attention(scal, query_t, grad_t, pos, kv, kv_t):
    features, tokens = query_t.shape
    blocks, window = tokens // BLK, kv.shape[0]
    width = GROUP * HD
    tile = pl.BlockSpec((width, BLK), lambda g, b, s: (g, b))
    return pl.pallas_call(
        attn_kernel,
        out_shape=(
            jax.ShapeDtypeStruct((features, tokens), BF),
            jax.ShapeDtypeStruct((features, tokens), BF),
            jax.ShapeDtypeStruct((window, 2 * HD), F32),
        ),
        grid_spec=pltpu.PrefetchScalarGridSpec(
            num_scalar_prefetch=1,
            grid=(features // width, blocks),
            in_specs=[
                tile,
                tile,
                pl.BlockSpec((8, BLK), lambda g, b, s: (0, b)),
                pl.BlockSpec((window, 2 * HD), lambda g, b, s: (0, 0)),
                pl.BlockSpec((2 * HD, window), lambda g, b, s: (0, 0)),
            ],
            out_specs=(
                tile,
                tile,
                pl.BlockSpec((window, 2 * HD), lambda g, b, s: (0, 0)),
            ),
            scratch_shapes=[
                pltpu.VMEM((GROUP, DOC + BLK, BLK), F32),
                pltpu.VMEM((2 * HD, 2 * GROUP * BLK), BF),
            ],
        ),
        compiler_params=pltpu.CompilerParams(
            dimension_semantics=("arbitrary", "arbitrary"), vmem_limit_bytes=40 << 20
        ),
        cost_estimate=pl.CostEstimate(
            flops=12 * features * tokens * DOC * 3 // 4,
            transcendentals=features // HD * tokens * DOC * 3 // 4,
            bytes_accessed=8 * features * tokens,
        ),
        name="attention",
    )(scal, query_t, grad_t, pos, kv, kv_t)


def turn(values, cosine, sine, direction):
    half = ROT // 2
    a, b = values[..., :half, :], values[..., half:ROT, :]
    return jnp.concatenate(
        [
            a * cosine - direction * b * sine,
            b * cosine + direction * a * sine,
            values[..., ROT:, :],
        ],
        axis=-2,
    )


def shards(
    tokens,
    segments,
    ln1_gain,
    ln1_bias,
    ln2_gain,
    ln2_bias,
    q_weight,
    q_bias,
    kv_weight,
    k_bias,
    out_weight,
    out_bias,
    up_weight,
    up_bias,
    down_weight,
    cotangent,
):
    core, chip = lax.axis_index("core"), lax.axis_index("chip")
    chips = lax.axis_size("rows") * lax.axis_size("chip")
    own = tokens.shape[1]
    both = 2 * own
    rows = q_weight.shape[0]
    hidden = up_bias.shape[0]
    back_chips = DOC // both

    def half_columns(array, which):
        return lax.dynamic_slice_in_dim(
            array, which * (array.shape[1] // 2), array.shape[1] // 2, 1
        )

    vectors = jnp.concatenate(
        [
            jnp.stack([ln1_gain, ln1_bias, ln2_gain, ln2_bias, q_bias, out_bias], axis=1),
            up_bias.reshape(rows, hidden // rows),
        ],
        axis=1,
    )
    vectors = jnp.pad(vectors, ((0, 0), (0, 128 - vectors.shape[1])))

    def first(which):
        return jnp.concatenate([half_columns(q_weight, which), kv_weight, vectors], axis=1)

    gathered = gather_chips(by_core(core, first(core), core_swap(first(1 - core)), 0))
    query_weight, pair_weight = gathered[:, :HALF], gathered[:, HALF : HALF + 2 * HD]
    vector_part = gathered[:, HALF + 2 * HD :].astype(F32)
    rows_of = vector_part[:, :6].T
    gain_one, shift_one, gain_two, shift_two = (rows_of[i : i + 1] for i in range(4))
    proj_bias = rows_of[5:6]
    query_bias = lax.dynamic_slice(vector_part, (core * HALF, 4), (HALF, 1))
    hidden_bias = lax.dynamic_index_in_dim(
        vector_part[:, 6 : 6 + hidden // rows].reshape(chips, 2, rows, hidden // rows),
        core,
        1,
        keepdims=False,
    ).reshape(1, FF // 2)

    columns = gather_chips(
        by_core(
            core,
            half_columns(out_weight, core),
            core_swap(half_columns(out_weight, 1 - core)),
            0,
        )
    )
    proj_weight = by_core(
        core,
        lax.dynamic_slice_in_dim(columns, core * HALF, HALF, 0),
        core_swap(lax.dynamic_slice_in_dim(columns, (1 - core) * HALF, HALF, 0)),
        1,
    )
    up_blocks = up_weight.reshape(rows, chips, 2, hidden)

    def up_half(which):
        return lax.dynamic_index_in_dim(up_blocks, which, 2, keepdims=False).reshape(rows, FF // 2)

    hidden_weight = gather_chips(by_core(core, up_half(core), core_swap(up_half(1 - core)), 0))
    back_weight = gather_chips(down_weight)

    own_tokens, own_grad = tokens[0], cotangent[0]
    features = jnp.concatenate([own_tokens, core_swap(own_tokens)], axis=0).astype(F32)
    grad_out = jnp.concatenate([own_grad, core_swap(own_grad)], axis=0)
    center = features - jnp.mean(features, axis=-1, keepdims=True)
    spread = lax.rsqrt(jnp.mean(center * center, axis=-1, keepdims=True) + norm_eps)
    unit = center * spread
    normed_one = (unit * gain_one + shift_one).astype(BF)
    normed_two = (unit * gain_two + shift_two).astype(BF)

    segrow = segments
    ids = lax.broadcasted_iota(jnp.int32, (MAX_SEGS, 1), 0)
    doc_starts = jnp.sum((segrow < ids).astype(jnp.int32), axis=1, keepdims=True)
    first_place, second_place = (chip * 2 + core) * own, (chip * 2 + 1 - core) * own
    span = lax.broadcasted_iota(jnp.int32, (1, own), 1)
    places = jnp.concatenate([first_place + span, second_place + span], axis=1)
    segs = jnp.concatenate(
        [
            lax.dynamic_slice(segrow, (0, first_place), (1, own)),
            lax.dynamic_slice(segrow, (0, second_place), (1, own)),
        ],
        axis=1,
    )
    starts = jnp.sum(jnp.where(segs == ids, doc_starts, 0), axis=0, keepdims=True)
    relative = places - starts
    frequency = 10000.0 ** (-(jnp.arange(ROT // 2, dtype=F32) * 2.0 / ROT))
    angles = relative.astype(F32) * frequency[:, None]
    cosine, sine = jnp.cos(angles), jnp.sin(angles)
    window_start = (chip - back_chips) * both
    pos = jnp.concatenate(
        [starts - window_start, places - window_start, jnp.zeros((6, both), jnp.int32)], axis=0
    )
    firsts, lasts = pos[:, ::BLK], pos[:, BLK - 1 :: BLK]
    scal = jnp.concatenate(
        [
            core.reshape(1),
            jnp.stack([firsts[0] // BLK, lasts[1] // BLK + 1, lasts[0]], axis=1).reshape(-1),
            jnp.full((1,), own // BLK, jnp.int32),
        ]
    ).astype(jnp.int32)

    query_t = dot(query_weight, normed_one, ((0,), (1,))) + query_bias
    query_t = turn(query_t.reshape(HEADS // 2, HD, both), cosine, sine, 1.0).astype(BF)
    query_t = query_t.reshape(HALF, both)
    pair_t = dot(pair_weight, normed_one[:own], ((0,), (1,)))
    key_t = turn(
        pair_t[:HD] + k_bias.astype(F32)[:, None], cosine[:, :own], sine[:, :own], 1.0
    ).astype(BF)
    own_pairs = jnp.concatenate([key_t, pair_t[HD:].astype(BF)], axis=0).T
    behind = jnp.concatenate(
        [chip_shift(own_pairs, k, False)[None] for k in range(back_chips, 0, -1)]
        + [own_pairs[None]],
        axis=0,
    )
    pairs = jnp.stack([behind, core_swap(behind)], axis=1).reshape(-1, 2 * HD)

    grad_t = dot(proj_weight, grad_out, ((1,), (1,))).astype(BF)
    out_t, grad_query_t, grad_pairs = attention(scal, query_t, grad_t, pos, pairs, pairs.T)

    hidden_pre = dot(normed_two, hidden_weight, ((1,), (0,))) + hidden_bias
    hidden_f, gelu_pull = jax.vjp(lambda z: jax.nn.gelu(z, approximate=False), hidden_pre)
    hidden_act = hidden_f.astype(BF)
    grad_back = dot(hidden_act, grad_out, ((0,), (0,))).astype(BF)
    grad_hidden = dot(grad_out, back_weight, ((1,), (1,)))
    grad_pre_f = gelu_pull(grad_hidden)[0]
    grad_pre = grad_pre_f.astype(BF)
    grad_up = dot(normed_two, grad_pre, ((0,), (0,))).astype(BF)
    grad_hidden_bias = jnp.sum(grad_pre.astype(F32), axis=0)
    back_sum = reduce_chips(grad_back)
    up_sum = reduce_chips(grad_up)
    grad_two = dot(grad_pre, hidden_weight, ((1,), (1,)))

    part = dot(out_t, proj_weight, ((0,), (0,))) + dot(hidden_act, back_weight, ((1,), (0,)))
    layer_out = (features[:own] + part[:own] + core_swap(part[own:]) + proj_bias).astype(BF)

    sides = grad_pairs.reshape(back_chips + 1, 2, own, 2 * HD)
    side_sum = sides[:, 0] + core_swap(sides[:, 1])
    pair_sum = side_sum[back_chips]
    for k in range(1, back_chips + 1):
        pair_sum = pair_sum + chip_shift(
            side_sum[back_chips - k].astype(BF), -k, False
        ).astype(F32)
    pair_sum_t = pair_sum.astype(BF).T
    key_pre_t = turn(
        pair_sum_t[:HD].astype(F32), cosine[:, :own], sine[:, :own], -1.0
    ).astype(BF)
    pair_grad_t = jnp.concatenate([key_pre_t, pair_sum_t[HD:]], axis=0)
    query_pre_t = (
        turn(grad_query_t.astype(F32).reshape(HEADS // 2, HD, both), cosine, sine, -1.0)
        .astype(BF)
        .reshape(HALF, both)
    )
    grad_query_weight = dot(normed_one, query_pre_t, ((0,), (1,))).astype(BF)
    grad_pair_weight = dot(normed_one[:own], pair_grad_t, ((0,), (1,))).astype(BF)
    grad_proj = dot(out_t, grad_out, ((1,), (0,))).astype(BF)
    grad_proj = by_core(
        core, half_columns(grad_proj, core), core_swap(half_columns(grad_proj, 1 - core)), 0
    )
    grad_one = dot(query_pre_t, query_weight, ((0,), (1,)))
    grad_one = grad_one + jnp.concatenate(
        [
            dot(pair_grad_t, pair_weight, ((0,), (1,))),
            jnp.zeros((own, D), F32),
        ],
        axis=0,
    )

    scaled = grad_one * gain_one + grad_two * gain_two
    scaled = scaled[:own] + core_swap(scaled[own:])
    own_unit = unit[:own]
    input_grad = own_grad.astype(F32) + spread[:own] * (
        scaled
        - jnp.mean(scaled, axis=-1, keepdims=True)
        - own_unit * jnp.mean(scaled * own_unit, axis=-1, keepdims=True)
    )

    query_bias_part = lax.dynamic_update_slice(
        jnp.zeros((D,), F32), jnp.sum(query_pre_t.astype(F32), axis=1), (core * HALF,)
    )
    table = jnp.stack(
        [
            jnp.sum(grad_one * unit, axis=0),
            jnp.sum(grad_one, axis=0),
            jnp.sum(grad_two * unit, axis=0),
            jnp.sum(grad_two, axis=0),
            query_bias_part,
            jnp.sum(own_grad.astype(F32), axis=0),
        ],
        axis=0,
    )
    two = hidden // (2 * rows)
    up_rows = grad_hidden_bias.reshape(chips, two, 2 * rows).transpose(1, 0, 2).reshape(two, D)
    table = jnp.concatenate([table, up_rows], axis=0)
    table = jnp.pad(table, ((0, 128 - table.shape[0]), (0, 0))).T.astype(BF)
    attn_sum = reduce_chips(
        jnp.concatenate([grad_query_weight, grad_proj, grad_pair_weight, table], axis=1)
    )
    mine = lax.dynamic_slice_in_dim(attn_sum, core * rows, rows, 0)
    theirs = core_swap(lax.dynamic_slice_in_dim(attn_sum, (1 - core) * rows, rows, 0))
    query_out = by_core(core, mine[:, :HALF], theirs[:, :HALF], 1)
    proj_out = by_core(core, mine[:, HALF : 2 * HALF], theirs[:, HALF : 2 * HALF], 1)
    rest = mine[:, 2 * HALF :] + theirs[:, 2 * HALF :]
    pair_out, vector_out = rest[:, : 2 * HD], rest[:, 2 * HD :]
    up_bias_out = attn_sum[:, 2 * HALF + 2 * HD + 6 : 2 * HALF + 2 * HD + 6 + two].T.reshape(hidden)
    key_bias_out = sum_everywhere(jnp.sum(key_pre_t.astype(F32), axis=1))

    mine = lax.dynamic_slice_in_dim(up_sum, core * rows, rows, 0)
    theirs = core_swap(lax.dynamic_slice_in_dim(up_sum, (1 - core) * rows, rows, 0))
    mine, theirs = mine.reshape(rows, chips, 1, hidden), theirs.reshape(rows, chips, 1, hidden)
    up_out = by_core(core, mine, theirs, 2).reshape(rows, FF)
    return (
        layer_out[None],
        input_grad[None],
        vector_out[:, 0],
        vector_out[:, 1],
        vector_out[:, 2],
        vector_out[:, 3],
        query_out,
        vector_out[:, 4],
        pair_out,
        key_bias_out,
        proj_out,
        vector_out[:, 5],
        up_out,
        up_bias_out,
        back_sum,
    )


def solution(mesh):
    devices = mesh.devices.reshape(mesh.shape["rows"], mesh.shape["wide"] // 2, 2)
    every, wide = ("rows", "chip", "core"), ("chip", "core")
    matrix, vector, sequence = P(every, None), P(every), P("rows", wide, None)
    return jax.shard_map(
        shards,
        mesh=Mesh(devices, every),
        in_specs=(
            sequence,
            P("rows", None),
            vector,
            vector,
            vector,
            vector,
            matrix,
            vector,
            matrix,
            P(),
            matrix,
            vector,
            matrix,
            vector,
            matrix,
            sequence,
        ),
        out_specs=(
            sequence,
            sequence,
            vector,
            vector,
            vector,
            vector,
            matrix,
            vector,
            matrix,
            P(),
            matrix,
            vector,
            matrix,
            vector,
            matrix,
        ),
        check_vma=False,
    )
```

time: 1420 us -> 587 us (0.41)
  waiting for transfers between devices: 672 us -> 46.1 us
  Pallas kernels: 0 us -> 277 us
  blocking collectives: 153 us -> 0 us
  matrix products: 213 us -> 68.6 us
  local copies, waits for them, and re-layouts: 143 us -> 53.6 us
  loops' own time: 76 us -> 0 us
  other arithmetic: 111 us -> 45.4 us
  starting transfers between devices: 21.8 us -> 87.1 us
    reduce_scatter x5 -> x0, waiting for transfers between devices: 397 us -> none  [the longest x1 142 us: shards(): lax.psum_scatter(grad_hidden_weight, ('rows', 'wide'), scatter_dimension=...]
    pallas_call x0 -> x5, Pallas kernels: none -> 277 us  [the longest x4 196 us: gather_chips(): pl.pallas_call(place_kernel, out_shape=jax.ShapeDtypeStruct((16 * size,)...]
    all_gather x5 -> x0, waiting for transfers between devices: 152 us -> none  [the longest x1 54.3 us: shards(): lax.all_gather(out_weight, ('rows', 'wide'), axis=0, tiled=True)]
    dot_general x70 -> x15, matrix products: 211 us -> 68.6 us  [dot(): lax.dot_general(left, right, (dims, ((), ())), preferred_element_type=F32)]
    unnamed x12 -> x0, waiting for transfers between devices: 102 us -> none
    ppermute x0 -> x71, starting transfers between devices: none -> 87.1 us  [the longest x30 34.9 us: rows_swap(): return lax.ppermute(value, 'rows', [(r, r ^ bit) for r in range(4)])]
    unnamed x2 -> x0, blocking collectives: 84.8 us -> none
    another operation x2 -> x0, loops' own time: 76 us -> none  [the longest x1 44.4 us: attend_back(): lax.scan(one_block, buffer_start, (blocks_query, blocks_start, blocks_gra...]
  transfers between devices with their start and end apart: 14 -> 71, of which waited for: 10 -> 13; matrix products, arithmetic and copies ran while one was open for 14% -> 26% of each run, Pallas kernels for 0% -> 48%
where the time goes in v1:
time: 587 us; the launch traced here: 581 us
  Pallas kernels  277 us (47%)
  starting transfers between devices  87.1 us (15%)
  matrix products  68.6 us (12%)
  local copies, waits for them, and re-layouts  53.6 us (9%)
  waiting for transfers between devices  46.1 us (8%)
  other arithmetic  45.4 us (8%)
    pallas_call x4, Pallas kernels, gather_chips(): pl.pallas_call(place_kernel, out_shape=jax.ShapeDtypeStruct((16 * size,)...  196 us
    pallas_call x1, Pallas kernels, attention(): pl.pallas_call(attn_kernel, out_shape=(jax.ShapeDtypeStruct((features, to...  81.7 us
    dot_general x15, matrix products, dot(): lax.dot_general(left, right, (dims, ((), ())), preferred_element_type=F32)  68.6 us
    ppermute x30, starting transfers between devices, rows_swap(): return lax.ppermute(value, 'rows', [(r, r ^ bit) for r in range(4)])  34.9 us
    ppermute x14, starting transfers between devices, core_swap(): return lax.ppermute(value, 'core', [(0, 1), (1, 0)])  25.8 us
    ppermute x25, starting transfers between devices, chip_shift(): return lax.ppermute(value, 'chip', pairs)  25.2 us
    ppermute x30, waiting for transfers between devices, rows_swap(): return lax.ppermute(value, 'rows', [(r, r ^ bit) for r in range(4)])  22.8 us
    ppermute x25, waiting for transfers between devices, chip_shift(): return lax.ppermute(value, 'chip', pairs)  19.8 us
  transfers between devices with their start and end apart: 71, of which 13 were waited for; matrix products, arithmetic and copies ran while one was open for 26% of the time, Pallas kernels for 48%

profile of v1, /device:TPU:25, one launch (start us, length us, event | category | flops | bytes accessed | tf_op | source)
XLA Modules:
  0.0 580.8 jit_solution(10090016584900704283)
XLA Ops:
  19.5 3.7 collective-permute-start.10
  43.7 4.1 collective-permute-start
  52.7 4.1 collective-permute-start.18
  57.3 19.1 %place.5 = bf16[768,384]{1,0:T(8,128)(2,1)} custom-call(bf16[192,384]{1,0:T(8,128)(2,1)} %copy-done.30, bf16[192,384]{1,0:T(8,128)(2,1)} %copy-done.38, bf16[192,384]{1,0:T(8,128)(2,1)} %copy-done.39, bf16[96,384]{1,0:T(8,128)(2,1)} %copy-done.47, bf16[96,384]{1,0:T(8,128)(2,1)} %collective-permute-done.16.high_ref), custom_call_target="tpu_custom_call" | custom-call | bytes 1179648 | tf_op jit(solution)/shard_map/place/pallas_call | solution.py:75
  83.4 31.0 %place.4 = bf16[768,640]{1,0:T(8,128)(2,1)} custom-call(bf16[192,640]{1,0:T(8,128)(2,1)} %copy-done.27, bf16[192,640]{1,0:T(8,128)(2,1)} %copy-done.36, bf16[192,640]{1,0:T(8,128)(2,1)} %copy-done.37, bf16[96,640]{1,0:T(8,128)(2,1)} %copy-done.45, bf16[96,640]{1,0:T(8,128)(2,1)} %copy-done.46), custom_call_target="tpu_custom_call" | custom-call | bytes 1966080 | tf_op jit(solution)/shard_map/place/pallas_call | solution.py:75
  142.7 5.3 collective-permute-done.20
  149.0 7.6 %collective-permute-start.21 = (bf16[3,512,128]{1,2,0:T(8,128)(2,1)}, bf16[3,512,128]{1,2,0:T(8,128)(2,1)}, u32[]{:S(2)}, u32[]{:S(2)}) collective-permute-start(bf16[3,512,128]{1,2,0:T(8,128)(2,1)} %get-tuple-element.90), channel_id=1, source_target_pairs={{0,1},{1,0},{2,3},{3,2},{4,5},{5,4},{6,7},{7,6},{8,9},{9,8},{10,11... | collective-permute-start | bytes 1179656 | tf_op jit(solution)/shard_map/ppermute | solution.py:28
  156.5 72.7 %place.7 = bf16[1536,768]{1,0:T(8,128)(2,1)} custom-call(bf16[384,768]{1,0:T(8,128)(2,1)} %copy-done.28, bf16[384,768]{1,0:T(8,128)(2,1)} %collective-permute-done.33.flat_ref, bf16[384,768]{1,0:T(8,128)(2,1)} %collective-permute-done.34.cross_ref, bf16[192,768]{1,0:T(8,128)(2,1)} %collective-permute-done.35.low_ref, ...), custom_call_target="tpu_custom_call" | custom-call | bytes 4718592 | tf_op jit(solution)/shard_map/place/pallas_call | solution.py:75
  229.3 72.7 %place.6 = bf16[768,1536]{1,0:T(8,128)(2,1)} custom-call(bf16[192,1536]{1,0:T(8,128)(2,1)} %pad_maximum_fusion.5.lines_ref, bf16[192,1536]{1,0:T(8,128)(2,1)} %collective-permute-done.26.flat_ref, bf16[192,1536]{1,0:T(8,128)(2,1)} %copy-done.21, bf16[96,1536]{1,0:T(8,128)(2,1)} %collective-permute-done.28.low_ref, ...), custom_call_target="tpu_custom_call" | custom-call | bytes 4718592 | tf_op jit(solution)/shard_map/place/pallas_call | solution.py:75
  302.0 28.3 %multiply_convert_fusion = (bf16[1024,1536]{1,0:T(8,128)(2,1)S(1)}, f32[1024,1536]{1,0:T(8,128)S(1)}, f32[1024,1536]{1,0:T(8,128)S(1)}) fusion(f32[1536]{0:T(1024)} %add.523, bf16[768,1536]{1,0:T(8,128)(2,1)} %place.6, f32[768]{0:T(1024)} %get-tuple-element.28, f32[768]{0:T(1024)} %get-tuple-element.29, f32[1024]{0:T(1024)S(1)} %add_rsqrt_fusion, ...), kind=kOutput, calls=%fused_computation.3 | convolution fusion | flops 2526806016 | bytes 19681280 | tf_op jit(solution)/shard_map/dot_general | solution.py:24
  330.4 4.8 convolution_convert_fusion
  337.9 6.3 %fusion.66 = (bf16[1536]{0:T(1024)(128)(2,1)}, bf16[1024,1536]{1,0:T(8,128)(2,1)S(1)}) fusion(f32[1024,1536]{1,0:T(8,128)S(1)} %get-tuple-element.45, bf16[1536,768]{1,0:T(8,128)(2,1)S(1)} %copy-done.17, bf16[512,768]{1,0:T(8,128)(2,1)} %collective-permute-done.18, bf16[512,768]{1,0:T(8,128)(2,1)S(1)} %bitcast.295, ...), kind=kOutput, calls=%fused_computation.262 | convolution fusion | flops 2444229120 | bytes 19670016 | tf_op jit(solution)/shard_map/dot_general | solution.py:24
  344.3 3.1 convolution_convert_fusion.1
  353.3 7.0 %fusion.67 = f32[1024,768]{1,0:T(8,128)} fusion(bf16[1024,1536]{1,0:T(8,128)(2,1)} %copy-done.60, bf16[1536,768]{1,0:T(8,128)(2,1)} %place.7), kind=kOutput, calls=%fused_computation.263 | convolution fusion | flops 2415919104 | bytes 8650752 | tf_op jit(solution)/shard_map/dot_general | solution.py:24
  364.4 81.7 %attention.1 = (bf16[384,1024]{1,0:T(8,128)(2,1)S(1)}, bf16[384,1024]{1,0:T(8,128)(2,1)S(1)}, f32[3072,128]{1,0:T(8,128)S(1)}) custom-call(s32[14]{0:T(128)S(1)} %pad_add_fusion.3.scal_ref, bf16[384,1024]{1,0:T(8,128)(2,1)S(1)} %bitcast.277, bf16[384,1024]{1,0:T(8,128)(2,1)S(1)} %copy-done, s32[8,1024]{1,0:T(8,128)S(1)} %add_add_fusion.pos_ref, ...), custom_call_target="tpu_custom_call" | custom-call | flops 7247757312 | bytes 3145728 | tf_op jit(solution)/shard_map/attention/pallas_call | solution.py:250
  454.6 3.2 convolution_add_fusion
  470.3 21.4 %collective-permute-done.57 = bf16[4,48,1536]{2,1,0:T(8,128)(2,1)S(1)} collective-permute-done((bf16[4,48,1536]{2,1,0:T(8,128)(2,1)S(1)}, bf16[4,48,1536]{2,1,0:T(8,128)(2,1)S(1)}, u32[]{:S(2)}, u32[]{:S(2)}) %collective-permute-start.57) | collective-permute-done | bytes 589856 | tf_op jit(solution)/shard_map/ppermute | solution.py:32
  503.6 6.2 %fusion.59 = (bf16[768]{0:T(1024)(128)(2,1)S(1)}, bf16[768]{0:T(1024)(128)(2,1)S(1)}, f32[1024,768]{1,0:T(8,128)}, bf16[768]{0:T(1024)(128)(2,1)S(1)}, bf16[768]{0:T(1024)(128)(2,1)S(1)}, /*index=5*/f32[1024,768]{1,0:T(8,128)}) fusion(f32[1024]{0:T(1024)S(1)} %add_rsqrt_fusion, f32[1024]{0:T(1024)S(1)} %broadcast_multiply_fusion.1, ...), kind=kOutput, calls=%fused_computation.256 | convolution fusion | flops 2427712512 | bytes 16535552 | tf_op jit(solution)/shard_map/dot_general | solution.py:24
  517.1 10.8 %collective-permute-start.43 = (bf16[2,48,1024]{2,1,0:T(8,128)(2,1)S(1)}, bf16[2,48,1024]{2,1,0:T(8,128)(2,1)S(1)}, u32[]{:S(2)}, u32[]{:S(2)}) collective-permute-start(bf16[2,48,1024]{2,1,0:T(8,128)(2,1)S(1)} %get-tuple-element.76), channel_id=1, source_target_pairs={{0,16},{8,24},{16,0},{24,8},{1,17},{9,25},{17,1},{25,9},{2,18},{10... | collective-permute-start | bytes 589832 | tf_op jit(solution)/shard_map/ppermute | solution.py:32
  537.2 4.6 collective-permute-done.69
  547.1 2.9 slice.462
  558.5 3.1 fusion.9
  561.6 5.1 collective-permute-done.48
  577.0 3.3 add_bitcast_fusion
  (428 shorter events, 165.9 us)
Async XLA Ops:
  0.7 35.1 %collective-permute-start.30 = (bf16[96,768]{1,0:T(8,128)(2,1)}, bf16[96,768]{1,0:T(8,128)(2,1)}, u32[]{:S(2)}, u32[]{:S(2)}) collective-permute-start(bf16[96,768]{1,0:T(8,128)(2,1)} %param.30), channel_id=1, source_target_pairs={{0,6},{2,0},{4,2},{6,4},{1,7},{3,1},{5,3},{7,5},{8,14},{10,8},{12,... | collective-permute-start | bytes 442376 | tf_op jit(solution)/shard_map/ppermute | solution.py:38
  0.9 37.3 %collective-permute-start.31 = (bf16[96,768]{1,0:T(8,128)(2,1)}, bf16[96,768]{1,0:T(8,128)(2,1)}, u32[]{:S(2)}, u32[]{:S(2)}) collective-permute-start(bf16[96,768]{1,0:T(8,128)(2,1)} %param.30), channel_id=1, source_target_pairs={{0,4},{2,6},{4,0},{6,2},{1,5},{3,7},{5,1},{7,3},{8,12},{10,14},{12... | collective-permute-start | bytes 442376 | tf_op jit(solution)/shard_map/ppermute | solution.py:38
  41.4 35.1 %collective-permute-start.5 = (bf16[192,640]{1,0:T(8,128)(2,1)S(1)}, bf16[192,640]{1,0:T(8,128)(2,1)S(1)}, u32[]{:S(2)}, u32[]{:S(2)}) collective-permute-start(bf16[192,640]{1,0:T(8,128)(2,1)S(1)} %pad_maximum_fusion.13.lines_ref), channel_id=1, source_target_pairs={{0,8},{8,0},{16,24},{24,16},{1,9},{9,1},{17,25},{25,17},{2,10},{10... | collective-permute-start | bytes 737288 | tf_op jit(solution)/shard_map/ppermute | solution.py:32
  42.6 34.2 %collective-permute-start.6 = (bf16[192,640]{1,0:T(8,128)(2,1)S(1)}, bf16[192,640]{1,0:T(8,128)(2,1)S(1)}, u32[]{:S(2)}, u32[]{:S(2)}) collective-permute-start(bf16[192,640]{1,0:T(8,128)(2,1)S(1)} %pad_maximum_fusion.13.lines_ref), channel_id=1, source_target_pairs={{0,16},{8,24},{16,0},{24,8},{1,17},{9,25},{17,1},{25,9},{2,18},{10... | collective-permute-start | bytes 737288 | tf_op jit(solution)/shard_map/ppermute | solution.py:32
  43.7 81.2 %collective-permute-start = (bf16[512,768]{1,0:T(8,128)(2,1)S(1)}, bf16[512,768]{1,0:T(8,128)(2,1)S(1)}, u32[]{:S(2)}, u32[]{:S(2)}) collective-permute-start(bf16[512,768]{1,0:T(8,128)(2,1)S(1)} %bitcast.278), channel_id=1, source_target_pairs={{0,1},{1,0},{2,3},{3,2},{4,5},{5,4},{6,7},{7,6},{8,9},{9,8},{10,11... | collective-permute-start | bytes 2359304 | tf_op jit(solution)/shard_map/ppermute | solution.py:28
  52.7 83.4 %collective-permute-start.18 = (bf16[512,768]{1,0:T(8,128)(2,1)S(1)}, bf16[512,768]{1,0:T(8,128)(2,1)}, u32[]{:S(2)}, u32[]{:S(2)}) collective-permute-start(bf16[512,768]{1,0:T(8,128)(2,1)S(1)} %bitcast.292), channel_id=1, source_target_pairs={{0,1},{1,0},{2,3},{3,2},{4,5},{5,4},{6,7},{7,6},{8,9},{9,8},{10,11... | collective-permute-start | bytes 2359304 | tf_op jit(solution)/shard_map/ppermute | solution.py:28
  56.8 62.8 %collective-permute-start.33 = (bf16[384,768]{1,0:T(8,128)(2,1)}, bf16[384,768]{1,0:T(8,128)(2,1)}, u32[]{:S(2)}, u32[]{:S(2)}) collective-permute-start(bf16[384,768]{1,0:T(8,128)(2,1)} %copy-done.28), channel_id=1, source_target_pairs={{0,8},{8,0},{16,24},{24,16},{1,9},{9,1},{17,25},{25,17},{2,10},{10... | collective-permute-start | bytes 1769480 | tf_op jit(solution)/shard_map/ppermute | solution.py:32
  81.1 40.7 %collective-permute-start.34 = (bf16[384,768]{1,0:T(8,128)(2,1)}, bf16[384,768]{1,0:T(8,128)(2,1)}, u32[]{:S(2)}, u32[]{:S(2)}) collective-permute-start(bf16[384,768]{1,0:T(8,128)(2,1)} %copy-done.28), channel_id=1, source_target_pairs={{0,16},{8,24},{16,0},{24,8},{1,17},{9,25},{17,1},{25,9},{2,18},{10... | collective-permute-start | bytes 1769480 | tf_op jit(solution)/shard_map/ppermute | solution.py:32
  82.4 48.5 %collective-permute-start.26 = (bf16[192,1536]{1,0:T(8,128)(2,1)}, bf16[192,1536]{1,0:T(8,128)(2,1)}, u32[]{:S(2)}, u32[]{:S(2)}) collective-permute-start(bf16[192,1536]{1,0:T(8,128)(2,1)} %pad_maximum_fusion.5.lines_ref), channel_id=1, source_target_pairs={{0,8},{8,0},{16,24},{24,16},{1,9},{9,1},{17,25},{25,17},{2,10},{10... | collective-permute-start | bytes 1769480 | tf_op jit(solution)/shard_map/ppermute | solution.py:32
  125.0 31.6 %collective-permute-start.35 = (bf16[192,768]{1,0:T(8,128)(2,1)S(1)}, bf16[192,768]{1,0:T(8,128)(2,1)}, u32[]{:S(2)}, u32[]{:S(2)}) collective-permute-start(bf16[192,768]{1,0:T(8,128)(2,1)S(1)} %slice.444), channel_id=1, source_target_pairs={{0,16},{8,24},{16,0},{24,8},{1,17},{9,25},{17,1},{25,9},{2,18},{10... | collective-permute-start | bytes 884744 | tf_op jit(solution)/shard_map/ppermute | solution.py:32
  135.1 94.1 %collective-permute-start.28 = (bf16[96,1536]{1,0:T(8,128)(2,1)}, bf16[96,1536]{1,0:T(8,128)(2,1)}, u32[]{:S(2)}, u32[]{:S(2)}) collective-permute-start(bf16[96,1536]{1,0:T(8,128)(2,1)} %slice.441), channel_id=1, source_target_pairs={{0,16},{8,24},{16,0},{24,8},{1,17},{9,25},{17,1},{25,9},{2,18},{10... | collective-permute-start | bytes 884744 | tf_op jit(solution)/shard_map/ppermute | solution.py:32
  136.1 93.2 %collective-permute-start.29 = (bf16[96,1536]{1,0:T(8,128)(2,1)}, bf16[96,1536]{1,0:T(8,128)(2,1)}, u32[]{:S(2)}, u32[]{:S(2)}) collective-permute-start(bf16[96,1536]{1,0:T(8,128)(2,1)} %slice.442), channel_id=1, source_target_pairs={{0,8},{8,0},{16,24},{24,16},{1,9},{9,1},{17,25},{25,17},{2,10},{10... | collective-permute-start | bytes 884744 | tf_op jit(solution)/shard_map/ppermute | solution.py:32
  149.0 211.4 %collective-permute-start.21 = (bf16[3,512,128]{1,2,0:T(8,128)(2,1)}, bf16[3,512,128]{1,2,0:T(8,128)(2,1)}, u32[]{:S(2)}, u32[]{:S(2)}) collective-permute-start(bf16[3,512,128]{1,2,0:T(8,128)(2,1)} %get-tuple-element.90), channel_id=1, source_target_pairs={{0,1},{1,0},{2,3},{3,2},{4,5},{5,4},{6,7},{7,6},{8,9},{9,8},{10,11... | collective-permute-start | bytes 1179656 | tf_op jit(solution)/shard_map/ppermute | solution.py:28
  337.7 124.3 %collective-permute-start.64 = (bf16[2,96,768]{2,1,0:T(8,128)(2,1)}, bf16[2,96,768]{2,1,0:T(8,128)(2,1)}, u32[]{:S(2)}, u32[]{:S(2)}) collective-permute-start(bf16[2,96,768]{2,1,0:T(8,128)(2,1)} %get-tuple-element.56), channel_id=1, source_target_pairs={{0,16},{8,24},{16,0},{24,8},{1,17},{9,25},{17,1},{25,9},{2,18},{10... | collective-permute-start | bytes 884744 | tf_op jit(solution)/shard_map/ppermute | solution.py:32
  337.9 124.2 %collective-permute-start.66 = (bf16[2,96,768]{2,1,0:T(8,128)(2,1)}, bf16[2,96,768]{2,1,0:T(8,128)(2,1)}, u32[]{:S(2)}, u32[]{:S(2)}) collective-permute-start(bf16[2,96,768]{2,1,0:T(8,128)(2,1)} %get-tuple-element.58), channel_id=1, source_target_pairs={{0,8},{8,0},{16,24},{24,16},{1,9},{9,1},{17,25},{25,17},{2,10},{10... | collective-permute-start | bytes 884744 | tf_op jit(solution)/shard_map/ppermute | solution.py:32
  349.9 114.2 %collective-permute-start.56 = (bf16[2,48,1536]{2,1,0:T(8,128)(2,1)}, bf16[2,48,1536]{2,1,0:T(8,128)(2,1)}, u32[]{:S(2)}, u32[]{:S(2)}) collective-permute-start(bf16[2,48,1536]{2,1,0:T(8,128)(2,1)} %get-tuple-element.62), channel_id=1, source_target_pairs={{0,16},{8,24},{16,0},{24,8},{1,17},{9,25},{17,1},{25,9},{2,18},{10... | collective-permute-start | bytes 884744 | tf_op jit(solution)/shard_map/ppermute | solution.py:32
  351.1 113.0 %collective-permute-start.58 = (bf16[2,48,1536]{2,1,0:T(8,128)(2,1)}, bf16[2,48,1536]{2,1,0:T(8,128)(2,1)}, u32[]{:S(2)}, u32[]{:S(2)}) collective-permute-start(bf16[2,48,1536]{2,1,0:T(8,128)(2,1)} %get-tuple-element.64), channel_id=1, source_target_pairs={{0,8},{8,0},{16,24},{24,16},{1,9},{9,1},{17,25},{25,17},{2,10},{10... | collective-permute-start | bytes 884744 | tf_op jit(solution)/shard_map/ppermute | solution.py:32
  462.1 96.4 %collective-permute-start.37 = (f32[512,768]{1,0:T(8,128)}, f32[512,768]{1,0:T(8,128)}, u32[]{:S(2)}, u32[]{:S(2)}) collective-permute-start(f32[512,768]{1,0:T(8,128)} %slice.447), channel_id=1, source_target_pairs={{0,1},{1,0},{2,3},{3,2},{4,5},{5,4},{6,7},{7,6},{8,9},{9,8},{10,11... | collective-permute-start | bytes 4718600 | tf_op jit(solution)/shard_map/ppermute | solution.py:28
  464.1 32.2 %collective-permute-start.65 = (bf16[4,96,768]{2,1,0:T(8,128)(2,1)S(1)}, bf16[4,96,768]{2,1,0:T(8,128)(2,1)S(1)}, u32[]{:S(2)}, u32[]{:S(2)}) collective-permute-start(bf16[4,96,768]{2,1,0:T(8,128)(2,1)S(1)} %pad_maximum_fusion.8), channel_id=1, source_target_pairs={{0,8},{8,0},{16,24},{24,16},{1,9},{9,1},{17,25},{25,17},{2,10},{10... | collective-permute-start | bytes 1769480 | tf_op jit(solution)/shard_map/ppermute | solution.py:32
  465.6 26.1 %collective-permute-start.57 = (bf16[4,48,1536]{2,1,0:T(8,128)(2,1)S(1)}, bf16[4,48,1536]{2,1,0:T(8,128)(2,1)S(1)}, u32[]{:S(2)}, u32[]{:S(2)}) collective-permute-start(bf16[4,48,1536]{2,1,0:T(8,128)(2,1)S(1)} %pad_maximum_fusion.6), channel_id=1, source_target_pairs={{0,8},{8,0},{16,24},{24,16},{1,9},{9,1},{17,25},{25,17},{2,10},{10... | collective-permute-start | bytes 1769480 | tf_op jit(solution)/shard_map/ppermute | solution.py:32
  467.3 25.7 %collective-permute-start.59 = (bf16[4,48,1536]{2,1,0:T(8,128)(2,1)S(1)}, bf16[4,48,1536]{2,1,0:T(8,128)(2,1)S(1)}, u32[]{:S(2)}, u32[]{:S(2)}) collective-permute-start(bf16[4,48,1536]{2,1,0:T(8,128)(2,1)S(1)} %pad_maximum_fusion.7), channel_id=1, source_target_pairs={{0,16},{8,24},{16,0},{24,8},{1,17},{9,25},{17,1},{25,9},{2,18},{10... | collective-permute-start | bytes 1769480 | tf_op jit(solution)/shard_map/ppermute | solution.py:32
  468.6 27.7 %collective-permute-start.67 = (bf16[4,96,768]{2,1,0:T(8,128)(2,1)S(1)}, bf16[4,96,768]{2,1,0:T(8,128)(2,1)S(1)}, u32[]{:S(2)}, u32[]{:S(2)}) collective-permute-start(bf16[4,96,768]{2,1,0:T(8,128)(2,1)S(1)} %pad_maximum_fusion.9), channel_id=1, source_target_pairs={{0,16},{8,24},{16,0},{24,8},{1,17},{9,25},{17,1},{25,9},{2,18},{10... | collective-permute-start | bytes 1769480 | tf_op jit(solution)/shard_map/ppermute | solution.py:32
  496.3 31.6 %collective-permute-start.61 = (bf16[48,1536]{1,0:T(8,128)(2,1)}, bf16[48,1536]{1,0:T(8,128)(2,1)}, u32[]{:S(2)}, u32[]{:S(2)}) collective-permute-start(bf16[48,1536]{1,0:T(8,128)(2,1)} %get-tuple-element.51), channel_id=1, source_target_pairs={{0,4},{2,6},{4,0},{6,2},{1,5},{3,7},{5,1},{7,3},{8,12},{10,14},{12... | collective-permute-start | bytes 442376 | tf_op jit(solution)/shard_map/ppermute | solution.py:38
  498.7 29.2 %collective-permute-start.62 = (bf16[48,1536]{1,0:T(8,128)(2,1)}, bf16[48,1536]{1,0:T(8,128)(2,1)}, u32[]{:S(2)}, u32[]{:S(2)}) collective-permute-start(bf16[48,1536]{1,0:T(8,128)(2,1)} %get-tuple-element.50), channel_id=1, source_target_pairs={{0,6},{2,0},{4,2},{6,4},{1,7},{3,1},{5,3},{7,5},{8,14},{10,8},{12,... | collective-permute-start | bytes 442376 | tf_op jit(solution)/shard_map/ppermute | solution.py:38
  (111 other events, 1592.2 us)

commit v2 on v1

v2 whole, which is shorter than its diff:
```python
import functools
import math

import jax
import jax.numpy as jnp
from jax import lax
from jax.experimental import pallas as pl
from jax.experimental.pallas import tpu as pltpu
from jax.sharding import Mesh, PartitionSpec as P

D = 768
HEADS = 12
HD = 64
ROT = 16
DOC = 2048
FF = 3072
MAX_SEGS = 32
norm_eps = 1e-05
BF = jnp.bfloat16
F32 = jnp.float32
HALF = HEADS // 2 * HD
BLK = 256
GROUP = 6


def dot(left, right, dims):
    return lax.dot_general(left, right, (dims, ((), ())), preferred_element_type=F32)


def core_swap(value):
    return lax.ppermute(value, "core", [(0, 1), (1, 0)])


def rows_swap(value, bit):
    return lax.ppermute(value, "rows", [(r, r ^ bit) for r in range(4)])


def chip_shift(value, by, wrap):
    count = lax.axis_size("chip")
    pairs = [(s, (s + by) % count) for s in range(count) if wrap or 0 <= s + by < count]
    return lax.ppermute(value, "chip", pairs)


def square_line():
    return lax.axis_size("rows") == 4 and lax.axis_size("chip") == 4


def place_kernel(parts, lines_ref, flat_ref, cross_ref, far_ref, *rest):
    outs, sems = rest[:-1], rest[-1]
    row, chip = lax.axis_index("rows"), lax.axis_index("chip")
    size = lines_ref.shape[0] // 4
    copies = []
    for turn, source in enumerate((lines_ref, flat_ref, cross_ref, far_ref)):
        for step in range(4):
            place = (row ^ turn) * 4 + lax.rem(chip + step, 4)
            for first, count, out, stride, offset in parts:
                copies.append(
                    pltpu.make_async_copy(
                        source.at[pl.ds(step * size + first, count)],
                        outs[out].at[pl.ds(pl.multiple_of(place * stride + offset, 8), count)],
                        sems.at[len(copies)],
                    )
                )
    for copy in copies:
        copy.start()
    for copy in copies:
        copy.wait()


def gather_line(piece):
    return [piece] + [chip_shift(piece, -k, True) for k in (1, 2, 3)]


def gather_rows(lines):
    return lines, rows_swap(lines, 1), rows_swap(lines, 2), rows_swap(lines, 3)


def gather_place(lines, parts, shapes):
    return pl.pallas_call(
        functools.partial(place_kernel, parts),
        out_shape=tuple(jax.ShapeDtypeStruct(shape, BF) for shape in shapes),
        in_specs=[pl.BlockSpec(memory_space=pl.ANY)] * 4,
        out_specs=tuple(pl.BlockSpec(memory_space=pltpu.VMEM) for _ in shapes),
        scratch_shapes=[pltpu.SemaphoreType.DMA((16 * len(parts),))],
        cost_estimate=pl.CostEstimate(
            flops=0, transcendentals=0, bytes_accessed=4 * sum(a * b for a, b in shapes)
        ),
        name="place",
    )(*lines)


def gather_whole(piece):
    return lax.all_gather(piece, ("rows", "chip"), axis=0, tiled=True)


def reduce_first(terms):
    row = lax.axis_index("rows")
    grid = terms.reshape((4, 4, terms.shape[0] // 16) + terms.shape[1:])
    planes = [lax.dynamic_index_in_dim(grid, row ^ bit, 0, keepdims=False) for bit in range(4)]
    return planes, (rows_swap(planes[3][:2], 1), rows_swap(planes[3][2:], 2))


def reduce_second(planes, arrived):
    _, flat, cross, _ = planes
    from_flat, from_cross = arrived
    to_flat = jnp.concatenate(
        [flat[:2], (flat[2:].astype(F32) + from_cross.astype(F32)).astype(BF)], axis=0
    )
    to_cross = jnp.concatenate(
        [(cross[:2].astype(F32) + from_flat.astype(F32)).astype(BF), cross[2:]], axis=0
    )
    return rows_swap(to_flat, 1), rows_swap(to_cross, 2)


def reduce_third(planes, arrived):
    chip = lax.axis_index("chip")

    def line(step):
        spot = lax.rem(chip + step, 4)
        pick = [
            lax.dynamic_index_in_dim(part, spot, 0, keepdims=False).astype(F32)
            for part in (planes[0], *arrived)
        ]
        return pick[0] + pick[1] + pick[2]

    return line(0), [chip_shift(line(step).astype(BF), step, True) for step in (1, 2, 3)]


def reduce_last(own, arrived):
    return own + arrived[0].astype(F32) + arrived[1].astype(F32) + arrived[2].astype(F32)


def reduce_whole(terms):
    return lax.psum_scatter(terms.astype(F32), ("rows", "chip"), scatter_dimension=0, tiled=True)


def after(value, *others):
    return lax.optimization_barrier((value, others))[0]


def sum_everywhere(value):
    if not square_line():
        return lax.psum(value, ("rows", "chip", "core"))
    value = value + core_swap(value)
    for bit in (1, 2):
        value = value + lax.ppermute(value, "chip", [(s, s ^ bit) for s in range(4)])
    for bit in (1, 2):
        value = value + rows_swap(value, bit)
    return value


def by_core(core, own, other, axis):
    return jnp.where(
        core == 0,
        jnp.concatenate([own, other], axis=axis),
        jnp.concatenate([other, own], axis=axis),
    )


def vector_kernel(v_ref, rows_ref, bias_ref):
    core = lax.axis_index("core")
    count = v_ref.shape[0]
    lane = lax.broadcasted_iota(jnp.int32, (128, D), 0)
    place = lax.broadcasted_iota(jnp.int32, (128, D), 1)
    pick = jnp.where(lane == lax.rem(place, 24), 1.0, 0.0).astype(BF)
    spread = dot(v_ref[...], pick, ((1,), (0,)))
    row = lax.broadcasted_iota(jnp.int32, (count, D), 0)
    spot = lax.broadcasted_iota(jnp.int32, (count, D), 1)
    own = jnp.where(row // 16 == spot // 24, spread, 0.0).astype(BF)
    kind = lax.rem(lax.broadcasted_iota(jnp.int32, (8, count), 1), 16)
    which = lax.broadcasted_iota(jnp.int32, (8, count), 0)
    rows_ref[...] = dot(jnp.where(kind == which, 1.0, 0.0).astype(BF), own, ((1,), (0,)))
    bias_ref[...] = jnp.zeros_like(bias_ref)
    start = (2 * (spot // 48) + core) * 16 + 6 + lax.rem(spot, 48) // 24
    for k in range(2):
        bias_ref[k : k + 1, :] = jnp.sum(
            jnp.where(row == start + 2 * k, spread, 0.0), axis=0, keepdims=True
        )


def turn(values, cosine, sine, direction):
    half = ROT // 2
    a, b = values[:half, :], values[half:ROT, :]
    return jnp.concatenate(
        [a * cosine - direction * b * sine, b * cosine + direction * a * sine, values[ROT:, :]],
        axis=0,
    )


def standard(tokens):
    values = tokens.astype(F32)
    center = values - jnp.mean(values, axis=-1, keepdims=True)
    spread = lax.rsqrt(jnp.mean(center * center, axis=-1, keepdims=True) + norm_eps)
    return center * spread, spread


def front_kernel(
    own_ref, other_ref, w_ref, rows_ref, kbias_ref, cos_ref, sin_ref,
    h1_ref, h2_ref, h2t_ref, q_ref, pairs_ref, keep_ref, send_ref,
):
    core = lax.axis_index("core")
    count = own_ref.shape[0]
    gain_one, shift_one, gain_two, shift_two = (rows_ref[i : i + 1, :] for i in range(4))
    for part, ref in enumerate((own_ref, other_ref)):
        unit, _ = standard(ref[...])
        spot = pl.ds(part * count, count)
        h1_ref[spot, :] = (unit * gain_one + shift_one).astype(BF)
        normed = (unit * gain_two + shift_two).astype(BF)
        h2_ref[spot, :] = normed
        h2t_ref[:, part * count : (part + 1) * count] = normed.T
    pair = dot(w_ref[:, 2 * HALF :], h1_ref[:count, :], ((0,), (1,)))
    key = turn(
        pair[:HD] + kbias_ref[...], cos_ref[:, :count], sin_ref[:, :count], 1.0
    ).astype(BF)
    pairs_ref[...] = jnp.concatenate([key, pair[HD:].astype(BF)], axis=0).T
    query = dot(w_ref[:, :HALF], h1_ref[...], ((0,), (1,)))
    bias = jnp.where(core == 0, rows_ref[4:5, :HALF], rows_ref[4:5, HALF:])
    query = query + jnp.broadcast_to(bias, (8, HALF)).T[:, :1]
    for h in range(HEADS // 2):
        q_ref[h * HD : (h + 1) * HD, :] = turn(
            query[h * HD : (h + 1) * HD, :], cos_ref[...], sin_ref[...], 1.0
        ).astype(BF)
    for index, ref in ((core, keep_ref), (1 - core, send_ref)):
        spot = pl.ds(pl.multiple_of(index * HALF, HALF), HALF)
        ref[...] = w_ref[spot, HALF : 2 * HALF]


def front(own, other, weights, rows, k_bias, cosine, sine):
    both = 2 * own.shape[0]
    return pl.pallas_call(
        front_kernel,
        out_shape=(
            jax.ShapeDtypeStruct((both, D), BF),
            jax.ShapeDtypeStruct((both, D), BF),
            jax.ShapeDtypeStruct((D, both), BF),
            jax.ShapeDtypeStruct((HALF, both), BF),
            jax.ShapeDtypeStruct((own.shape[0], 2 * HD), BF),
            jax.ShapeDtypeStruct((HALF, HALF), BF),
            jax.ShapeDtypeStruct((HALF, HALF), BF),
        ),
        compiler_params=pltpu.CompilerParams(vmem_limit_bytes=48 << 20),
        cost_estimate=pl.CostEstimate(
            flops=2 * both * D * (HALF + 2 * HD), transcendentals=both, bytes_accessed=8 * both * D
        ),
        name="front",
    )(own, other, weights, rows, k_bias, cosine, sine)


def attn_kernel(
    scal_ref, q_ref, grad_ref, keep_ref, got_ref, pos_ref, cos_ref, sin_ref, mine_ref, theirs_ref,
    o_ref, dq_ref, dmine_ref, dtheirs_ref,
    kv_ref, kvt_ref, dkv_ref, g_ref, s_ref, r_ref, rt_ref,
):
    block = pl.program_id(0)
    core = scal_ref[0]
    low, high, edge = (scal_ref[1 + 3 * block + i] for i in range(3))
    wide = GROUP * BLK
    half = kv_ref.shape[0] // 2
    own_blocks = pl.num_programs(0) // 2

    @pl.when(block == 0)
    def _():
        dkv_ref[...] = jnp.zeros_like(dkv_ref)
        for part, ref in enumerate((mine_ref, theirs_ref)):
            kv_ref[part * half : (part + 1) * half, :] = ref[...]
            kvt_ref[: 2 * HD, part * half : (part + 1) * half] = ref[...].T
        kvt_ref[2 * HD :, :] = jnp.ones((16, 2 * half), BF)

    def spot(key_block):
        side = lax.rem(key_block // own_blocks, 2) ^ core
        place = (key_block // (2 * own_blocks)) * own_blocks + lax.rem(key_block, own_blocks)
        return pl.multiple_of(side * half + place * BLK, BLK)

    def slot(key_block):
        return pl.ds(pl.multiple_of((key_block - low) * BLK, BLK), BLK)

    near = pl.ds(pl.multiple_of(core * HALF, HALF), HALF)
    away = pl.ds(pl.multiple_of((1 - core) * HALF, HALF), HALF)
    g_ref[...] = (
        dot(keep_ref[...], grad_ref[:, near], ((1,), (1,)))
        + dot(got_ref[...], grad_ref[:, away], ((1,), (1,)))
    ).astype(BF)
    starts = jnp.concatenate([pos_ref[0:1, :]] * GROUP, axis=1)
    places = jnp.concatenate([pos_ref[1:2, :]] * GROUP, axis=1)
    blank = jnp.zeros((HD, BLK), BF)
    for h in range(GROUP):
        query = (q_ref[h * HD : (h + 1) * HD, :].astype(F32) * HD**-0.5).astype(BF)
        grad = g_ref[h * HD : (h + 1) * HD, :]
        query = jnp.concatenate([query, blank], axis=0)
        grad = jnp.concatenate([blank, grad], axis=0)
        r_ref[0, :, h * BLK : (h + 1) * BLK] = query
        r_ref[1, :, h * BLK : (h + 1) * BLK] = grad
        rt_ref[h * BLK : (h + 1) * BLK, :] = query.T
        rt_ref[(GROUP + h) * BLK : (GROUP + h + 1) * BLK, :] = grad.T

    def scores(masked, key_block, peak):
        keys = kv_ref[pl.ds(spot(key_block), BLK), :]
        s = dot(keys, r_ref[0], ((1,), (0,)))
        if masked:
            key_places = key_block * BLK + lax.broadcasted_iota(jnp.int32, (BLK, wide), 0)
            s = jnp.where((key_places >= starts) & (key_places <= places), s, -1e30)
        s_ref[slot(key_block), :] = s
        return jnp.maximum(peak, jnp.max(s, axis=0, keepdims=True))

    clear = jnp.minimum((edge + BLK - 1) // BLK, high - 1)
    peak = jnp.full((1, wide), -1e30, F32)
    peak = lax.fori_loop(low, clear, functools.partial(scores, True), peak)
    peak = lax.fori_loop(clear, high - 1, functools.partial(scores, False), peak)
    peak = scores(True, high - 1, peak)

    def expo(key_block, out):
        values = kvt_ref[HD:, pl.ds(spot(key_block), BLK)]
        e = jnp.exp(s_ref[slot(key_block), :] - peak)
        s_ref[slot(key_block), :] = e
        return out + dot(values, e.astype(BF), ((1,), (0,)))

    out = lax.fori_loop(low, high, expo, jnp.zeros((HD + 16, wide), F32))
    inverse = 1.0 / out[HD : HD + 1, :]
    out = out[:HD] * inverse
    deltas = []
    for h in range(GROUP):
        part = out[:, h * BLK : (h + 1) * BLK]
        o_ref[h * HD : (h + 1) * HD, :] = part.astype(BF)
        deltas.append(
            jnp.sum(part * g_ref[h * HD : (h + 1) * HD, :].astype(F32), axis=0, keepdims=True)
        )
    delta = jnp.concatenate(deltas, axis=1)

    def back(key_block, dq):
        where = spot(key_block)
        pairs = kv_ref[pl.ds(where, BLK), :]
        keys = kvt_ref[:HD, pl.ds(where, BLK)]
        p = s_ref[slot(key_block), :] * inverse
        dp = dot(pairs, r_ref[1], ((1,), (0,)))
        ds = (p * (dp - delta)).astype(BF)
        left = jnp.concatenate([ds, p.astype(BF)], axis=1)
        dkv_ref[pl.ds(where, BLK), :] += dot(left, rt_ref[...], ((1,), (0,)))
        return dq + dot(keys, ds, ((1,), (0,)))

    dq = lax.fori_loop(low, high, back, jnp.zeros((HD, wide), F32)) * HD**-0.5
    for h in range(GROUP):
        part = dq[:, h * BLK : (h + 1) * BLK].astype(BF).astype(F32)
        dq_ref[h * HD : (h + 1) * HD, :] = turn(part, cos_ref[...], sin_ref[...], -1.0).astype(BF)

    @pl.when(block == pl.num_programs(0) - 1)
    def _():
        dmine_ref[...] = dkv_ref[:half, :]
        dtheirs_ref[...] = dkv_ref[half:, :]


def attention(scal, query_t, grad_out, keep, got, pos, cosine, sine, mine, theirs):
    features, tokens = query_t.shape
    blocks, half = tokens // BLK, mine.shape[0]
    tile = pl.BlockSpec((features, BLK), lambda b, s: (0, b))
    small = pl.BlockSpec((8, BLK), lambda b, s: (0, b))

    def whole(rows, columns):
        return pl.BlockSpec((rows, columns), lambda b, s: (0, 0))

    return pl.pallas_call(
        attn_kernel,
        out_shape=(
            jax.ShapeDtypeStruct((features, tokens), BF),
            jax.ShapeDtypeStruct((features, tokens), BF),
            jax.ShapeDtypeStruct((half, 2 * HD), F32),
            jax.ShapeDtypeStruct((half, 2 * HD), F32),
        ),
        grid_spec=pltpu.PrefetchScalarGridSpec(
            num_scalar_prefetch=1,
            grid=(blocks,),
            in_specs=[
                tile,
                pl.BlockSpec((BLK, D), lambda b, s: (b, 0)),
                whole(HALF, HALF),
                whole(HALF, HALF),
                small,
                small,
                small,
                whole(half, 2 * HD),
                whole(half, 2 * HD),
            ],
            out_specs=(tile, tile, whole(half, 2 * HD), whole(half, 2 * HD)),
            scratch_shapes=[
                pltpu.VMEM((2 * half, 2 * HD), BF),
                pltpu.VMEM((2 * HD + 16, 2 * half), BF),
                pltpu.VMEM((2 * half, 2 * HD), F32),
                pltpu.VMEM((features, BLK), BF),
                pltpu.VMEM((DOC + BLK, GROUP * BLK), F32),
                pltpu.VMEM((2, 2 * HD, GROUP * BLK), BF),
                pltpu.VMEM((2 * GROUP * BLK, 2 * HD), BF),
            ],
        ),
        compiler_params=pltpu.CompilerParams(
            dimension_semantics=("arbitrary",), vmem_limit_bytes=48 << 20
        ),
        cost_estimate=pl.CostEstimate(
            flops=12 * features * tokens * DOC * 3 // 4,
            transcendentals=features // HD * tokens * DOC * 3 // 4,
            bytes_accessed=8 * features * tokens,
        ),
        name="attention",
    )(scal, query_t, grad_out, keep, got, pos, cosine, sine, mine, theirs)


def heads_kernel(
    o_ref, dq_ref, h1_ref, grad_ref, w_ref, keep_ref, got_ref,
    part_ref, dh_ref, gq_ref, keep_out_ref, send_out_ref, sums_ref,
):
    core = lax.axis_index("core")
    near = pl.ds(pl.multiple_of(core * HALF, HALF), HALF)
    away = pl.ds(pl.multiple_of((1 - core) * HALF, HALF), HALF)
    keep_out_ref[...] = dot(o_ref[...], grad_ref[:, near], ((1,), (0,))).astype(BF)
    send_out_ref[...] = dot(o_ref[...], grad_ref[:, away], ((1,), (0,))).astype(BF)
    gq_ref[...] = dot(dq_ref[...], h1_ref[...], ((1,), (0,))).T.astype(BF)
    heads = o_ref[...].T
    part_ref[:, near] = dot(heads, keep_ref[...], ((1,), (0,)))
    part_ref[:, away] = dot(heads, got_ref[...], ((1,), (0,)))
    dh_ref[...] = dot(dq_ref[...].T, w_ref[...], ((1,), (1,)))
    ones = jnp.ones((8, dq_ref.shape[1]), BF)
    sums_ref[...] = jnp.zeros_like(sums_ref)
    sums_ref[0:8, near] = dot(ones, dq_ref[...], ((1,), (1,)))
    count = grad_ref.shape[0] // 2
    sums_ref[8:16, :] = dot(ones[:, :count], grad_ref[:count, :], ((1,), (0,)))


def after_heads(out_t, dq_t, normed, grad_out, query_weight, keep, got):
    both = normed.shape[0]
    return pl.pallas_call(
        heads_kernel,
        out_shape=(
            jax.ShapeDtypeStruct((both, D), F32),
            jax.ShapeDtypeStruct((both, D), F32),
            jax.ShapeDtypeStruct((D, HALF), BF),
            jax.ShapeDtypeStruct((HALF, HALF), BF),
            jax.ShapeDtypeStruct((HALF, HALF), BF),
            jax.ShapeDtypeStruct((16, D), F32),
        ),
        compiler_params=pltpu.CompilerParams(vmem_limit_bytes=48 << 20),
        cost_estimate=pl.CostEstimate(
            flops=8 * both * D * HALF, transcendentals=0, bytes_accessed=12 * both * D
        ),
        name="after_heads",
    )(out_t, dq_t, normed, grad_out, query_weight, keep, got)


def pairs_kernel(
    own_ref, near_ref, far_ref, h1_ref, w_ref, cos_ref, sin_ref, gw_ref, dh_ref, gbias_ref
):
    total = own_ref[...] + near_ref[...].astype(F32) + far_ref[...].astype(F32)
    total = total.astype(BF).astype(F32).T
    key = turn(total[:HD], cos_ref[...], sin_ref[...], -1.0)
    grad = jnp.concatenate([key, total[HD:]], axis=0).astype(BF)
    gw_ref[...] = dot(grad, h1_ref[...], ((1,), (0,))).T.astype(BF)
    dh_ref[...] = dot(grad.T, w_ref[...], ((1,), (1,)))
    ones = jnp.ones((8, grad.shape[1]), BF)
    gbias_ref[...] = dot(ones, grad, ((1,), (1,)))


def after_pairs(own, near, far, normed, pair_weight, cosine, sine):
    count = own.shape[0]

    def whole(rows, columns):
        return pl.BlockSpec((rows, columns), lambda i: (0, 0))

    return pl.pallas_call(
        pairs_kernel,
        out_shape=(
            jax.ShapeDtypeStruct((D, 2 * HD), BF),
            jax.ShapeDtypeStruct((count, D), F32),
            jax.ShapeDtypeStruct((8, 2 * HD), F32),
        ),
        grid=(1,),
        in_specs=[
            whole(count, 2 * HD),
            whole(count, 2 * HD),
            whole(count, 2 * HD),
            whole(count, D),
            whole(D, 2 * HD),
            whole(8, count),
            whole(8, count),
        ],
        out_specs=(whole(D, 2 * HD), whole(count, D), whole(8, 2 * HD)),
        compiler_params=pltpu.CompilerParams(vmem_limit_bytes=32 << 20),
        cost_estimate=pl.CostEstimate(
            flops=8 * count * D * HD, transcendentals=0, bytes_accessed=8 * count * D
        ),
        name="after_pairs",
    )(own, near, far, normed, pair_weight, cosine, sine)


def ffn_units(step, h_ref, ht_ref, g_ref, up_ref, bias_ref, down_ref, grad_ref, act_ref, dz_ref):
    spot = pl.ds(pl.multiple_of(step * BLK, BLK), BLK)
    up, down = up_ref[:, spot], down_ref[spot, :]
    z = dot(h_ref[...], up, ((1,), (0,))) + bias_ref[:, spot]
    below = 0.5 * (1.0 + lax.erf(z * 0.5**0.5))
    slope = below + z * (jnp.exp(-0.5 * z * z) * (0.5 / math.pi) ** 0.5)
    act = (z * below).astype(BF)
    grad = (dot(g_ref[...], down, ((1,), (1,))) * slope).astype(BF)
    grad_ref[:, spot] = dot(ht_ref[...], grad, ((1,), (0,))).astype(BF)
    grad_ref[spot, D : 2 * D] = dot(act, g_ref[...], ((0,), (0,))).astype(BF)
    act_ref[:, spot] = act
    dz_ref[:, spot] = grad
    return jnp.sum(grad.astype(F32), axis=0, keepdims=True), spot


def ffn_first_kernel(
    h_ref, ht_ref, g_ref, up_ref, bias_ref, down_ref, part_ref,
    out_ref, dh_ref, grad_ref, gbias_ref,
    act_ref, dz_ref,
):
    step = pl.program_id(0)
    units = up_ref.shape[1] // BLK

    @pl.when(step < units)
    def _():
        gbias, spot = ffn_units(
            step, h_ref, ht_ref, g_ref, up_ref, bias_ref, down_ref, grad_ref, act_ref, dz_ref
        )
        gbias_ref[:, spot] = gbias

    @pl.when(step >= units)
    def _():
        spot = pl.ds(pl.multiple_of((step - units) * BLK, BLK), BLK)
        out_ref[...] = part_ref[...] + dot(act_ref[spot, :], down_ref[...], ((1,), (0,)))
        dh_ref[...] = dot(dz_ref[spot, :], up_ref[...], ((1,), (1,)))


def ffn_second_kernel(
    h_ref, ht_ref, g_ref, up_ref, bias_ref, down_ref,
    part_ref, dh_in_ref, x_ref, one_ref, pair_ref, rows_ref, sums_ref, bias0_ref, gpair_ref,
    keep_ref, send_ref, tkeep_ref, tsend_ref, grad_ref,
    act_ref, dz_ref, table_ref,
):
    step = pl.program_id(0)
    units = up_ref.shape[1] // BLK
    blocks = pl.num_programs(0) - units

    @pl.when(step == 0)
    def _():
        table_ref[...] = jnp.zeros_like(table_ref)
        table_ref[4:5, :] = sums_ref[0:1, :]
        table_ref[5:6, :] = sums_ref[8:9, :]
        table_ref[6:7, :] = bias0_ref[...]
        grad_ref[:, 2 * D : 2 * D + 2 * HD] = gpair_ref[...]

    @pl.when(step < units)
    def _():
        gbias, spot = ffn_units(
            step, h_ref, ht_ref, g_ref, up_ref, bias_ref, down_ref, grad_ref, act_ref, dz_ref
        )
        table_ref[7:8, spot] = gbias

    def tokens(first):
        spot = pl.ds(pl.multiple_of((step - units) * BLK, BLK), BLK)
        out = part_ref[...] + dot(act_ref[spot, :], down_ref[...], ((1,), (0,)))
        two = dh_in_ref[...] + dot(dz_ref[spot, :], up_ref[...], ((1,), (1,)))
        one = one_ref[...]
        if first:
            one = one + pair_ref[...]
        unit, _ = standard(x_ref[...])
        scaled = one * rows_ref[0:1, :] + two * rows_ref[2:3, :]
        for ref, value in (
            ((keep_ref, out), (tkeep_ref, scaled)) if first else ((send_ref, out), (tsend_ref, scaled))
        ):
            ref[...] = value
        for i, value in enumerate((one * unit, one, two * unit, two)):
            table_ref[i : i + 1, :] += jnp.sum(value, axis=0, keepdims=True)

    @pl.when((step >= units) & (step < units + blocks // 2))
    def _():
        tokens(True)

    @pl.when(step >= units + blocks // 2)
    def _():
        tokens(False)

    @pl.when(step == pl.num_programs(0) - 1)
    def _():
        grad_ref[:, 2 * D + 2 * HD :] = table_ref[...].T.astype(BF)


def feed_forward(normed, normed_t, grad_out, up, bias, down, part, more=None):
    tokens, width = normed.shape
    hidden = up.shape[1]
    units, blocks = hidden // BLK, tokens // BLK

    def whole(rows, columns):
        return pl.BlockSpec((rows, columns), lambda i: (0, 0))

    def block(first, last):
        return pl.BlockSpec((BLK, width), lambda i: (jnp.clip(i - units - first, 0, last - first), 0))

    every, own, other = block(0, blocks - 1), block(0, blocks // 2 - 1), block(blocks // 2, blocks - 1)
    in_specs = [
        whole(tokens, width),
        whole(width, tokens),
        whole(tokens, width),
        whole(width, hidden),
        whole(1, hidden),
        whole(hidden, width),
        every,
    ]
    rows = jax.ShapeDtypeStruct((tokens, width), F32)
    side = jax.ShapeDtypeStruct((tokens // 2, width), F32)
    scratch = [pltpu.VMEM((tokens, hidden), BF), pltpu.VMEM((tokens, hidden), BF)]
    if more is None:
        kernel, operands = ffn_first_kernel, ()
        shapes = (
            rows,
            rows,
            jax.ShapeDtypeStruct((width, 2 * width), BF),
            jax.ShapeDtypeStruct((1, hidden), F32),
        )
        out_specs = (every, every, whole(width, 2 * width), whole(1, hidden))
    else:
        kernel, operands = ffn_second_kernel, more
        in_specs += [
            every,
            every,
            every,
            own,
            whole(8, width),
            whole(16, width),
            whole(1, hidden),
            whole(width, 2 * HD),
        ]
        wide = 2 * width + 2 * HD + 128
        shapes = (side, side, side, side, jax.ShapeDtypeStruct((width, wide), BF))
        out_specs = (own, other, own, other, whole(width, wide))
        scratch.append(pltpu.VMEM((128, width), F32))
    return pl.pallas_call(
        kernel,
        out_shape=shapes,
        grid=(units + blocks,),
        in_specs=in_specs,
        out_specs=out_specs,
        scratch_shapes=scratch,
        compiler_params=pltpu.CompilerParams(
            dimension_semantics=("arbitrary",), vmem_limit_bytes=56 << 20
        ),
        cost_estimate=pl.CostEstimate(
            flops=12 * tokens * width * hidden,
            transcendentals=2 * tokens * hidden,
            bytes_accessed=8 * width * hidden + 20 * tokens * width,
        ),
        name="ffn",
    )(normed, normed_t, grad_out, up, bias, down, part, *operands)


def shards(
    tokens,
    segments,
    ln1_gain,
    ln1_bias,
    ln2_gain,
    ln2_bias,
    q_weight,
    q_bias,
    kv_weight,
    k_bias,
    out_weight,
    out_bias,
    up_weight,
    up_bias,
    down_weight,
    cotangent,
):
    core, chip = lax.axis_index("core"), lax.axis_index("chip")
    chips = lax.axis_size("rows") * lax.axis_size("chip")
    own = tokens.shape[1]
    both = 2 * own
    rows = q_weight.shape[0]
    hidden = up_bias.shape[0]
    half = hidden // 2
    back_chips = DOC // both
    own_tokens, own_grad = tokens[0], cotangent[0]

    def half_columns(array, which):
        return lax.dynamic_slice_in_dim(
            array, which * (array.shape[1] // 2), array.shape[1] // 2, 1
        )

    def first(which):
        return jnp.concatenate(
            [half_columns(q_weight, which), half_columns(out_weight, which), kv_weight], axis=1
        )

    up_blocks = up_weight.reshape(rows, chips, 2, 2, half)

    def up_half(which):
        block = lax.dynamic_index_in_dim(up_blocks, which, 2, keepdims=False)
        return block.transpose(0, 2, 1, 3).reshape(rows, FF // 2)

    flat = (ln1_gain, ln1_bias, ln2_gain, ln2_bias, q_bias, out_bias)
    if square_line():
        wide = 2 * HALF + 2 * HD
        line = jnp.concatenate(
            [vector.reshape(1, rows) for vector in flat] + [up_bias.reshape(hidden // rows, rows)]
        )
        line = jnp.pad(line, ((0, 16 - line.shape[0]), (0, wide - rows)))
        mine = jnp.concatenate([first(core), line], axis=0)
        theirs = jnp.concatenate([first(1 - core), line], axis=0)
        attn_line = jnp.concatenate(gather_line(by_core(core, mine, core_swap(theirs), 0)))
        attn_rows = gather_rows(attn_line)
        up_piece = by_core(core, up_half(core), core_swap(up_half(1 - core)), 0)
        ff_piece = jnp.concatenate([up_piece[:, :D], up_piece[:, D:], down_weight], axis=0)
        ff_line = gather_line(after(ff_piece, attn_line))
        other_tokens = core_swap(own_tokens)
        features = jnp.concatenate([own_tokens, other_tokens], axis=0)
        grad_out = jnp.concatenate([own_grad, core_swap(own_grad)], axis=0)
        attn_rows, ff_line, grad_out, features = lax.optimization_barrier(
            (attn_rows, ff_line, grad_out, features)
        )
        step = rows + 16
        weights, vectors = gather_place(
            attn_rows,
            (
                (0, rows, 0, 2 * rows, 0),
                (step, rows, 0, 2 * rows, rows),
                (rows, 16, 1, 32, 0),
                (step + rows, 16, 1, 32, 16),
            ),
            ((D, wide), (32 * chips, wide)),
        )
        vector_rows, hidden_bias = pl.pallas_call(
            vector_kernel,
            grid=(1,),
            in_specs=[pl.BlockSpec((32 * chips, 128), lambda i: (0, 0))],
            out_specs=(
                pl.BlockSpec((8, D), lambda i: (0, 0)),
                pl.BlockSpec((8, D), lambda i: (0, 0)),
            ),
            out_shape=(jax.ShapeDtypeStruct((8, D), F32), jax.ShapeDtypeStruct((8, D), F32)),
            name="vectors",
        )(vectors)
    else:
        weights = gather_whole(by_core(core, first(core), core_swap(first(1 - core)), 0))
        every = ("rows", "chip", "core")
        table = lax.all_gather(jnp.stack(flat), every, axis=1, tiled=True).astype(F32)
        vector_rows = jnp.pad(table, ((0, 2), (0, 0)))
        bias = gather_whole(up_bias).astype(F32).reshape(chips, 2, half)
        hidden_bias = jnp.pad(bias.transpose(1, 0, 2).reshape(2, D), ((0, 6), (0, 0)))

    if not square_line():
        other_tokens = core_swap(own_tokens)
        features = jnp.concatenate([own_tokens, other_tokens], axis=0)
        grad_out = jnp.concatenate([own_grad, core_swap(own_grad)], axis=0)

    ids = lax.broadcasted_iota(jnp.int32, (MAX_SEGS, 1), 0)
    doc_starts = jnp.sum((segments < ids).astype(jnp.int32), axis=1, keepdims=True)
    first_place, second_place = (chip * 2 + core) * own, (chip * 2 + 1 - core) * own
    span = lax.broadcasted_iota(jnp.int32, (1, own), 1)
    places = jnp.concatenate([first_place + span, second_place + span], axis=1)
    segs = jnp.concatenate(
        [
            lax.dynamic_slice(segments, (0, first_place), (1, own)),
            lax.dynamic_slice(segments, (0, second_place), (1, own)),
        ],
        axis=1,
    )
    starts = jnp.sum(jnp.where(segs == ids, doc_starts, 0), axis=0, keepdims=True)
    relative = places - starts
    frequency = 10000.0 ** (-(jnp.arange(ROT // 2, dtype=F32) * 2.0 / ROT))
    angles = relative.astype(F32) * frequency[:, None]
    cosine, sine = jnp.cos(angles), jnp.sin(angles)
    window_start = (chip - back_chips) * both
    pos = jnp.concatenate(
        [starts - window_start, places - window_start, jnp.zeros((6, both), jnp.int32)], axis=0
    )
    firsts, lasts = pos[:, ::BLK], pos[:, BLK - 1 :: BLK]
    scal = jnp.concatenate(
        [
            core.reshape(1),
            jnp.stack([firsts[0] // BLK, lasts[1] // BLK + 1, lasts[0]], axis=1).reshape(-1),
        ]
    ).astype(jnp.int32)


    normed_one, normed_two, normed_two_t, query_t, own_pairs, keep, send = front(
        own_tokens, other_tokens, weights, vector_rows, k_bias.astype(F32)[:, None], cosine, sine
    )
    got = core_swap(send)
    if square_line():
        ff_line = jnp.concatenate(ff_line)
    mine = jnp.concatenate(
        [chip_shift(own_pairs, k, False) for k in range(back_chips, 0, -1)] + [own_pairs], axis=0
    )
    theirs = core_swap(mine)

    if square_line():
        ff_rows = gather_rows(after(ff_line, attn_rows))

    out_t, grad_query_t, pair_mine, pair_theirs = attention(
        scal, query_t, grad_out, keep, got, pos, cosine, sine, mine, theirs
    )
    if square_line():
        (out_t, grad_query_t, pair_mine, pair_theirs), ff_rows = lax.optimization_barrier(
            ((out_t, grad_query_t, pair_mine, pair_theirs), ff_rows)
        )
    part, grad_one, grad_query, proj_keep, proj_send, sums = after_heads(
        out_t, grad_query_t, normed_one, grad_out, weights[:, :HALF], keep, got
    )
    pair_got = core_swap(pair_theirs)
    if square_line():
        part, grad_one, grad_query, proj_keep, proj_send, sums = after(
            (part, grad_one, grad_query, proj_keep, proj_send, sums), pair_got
        )
    grad_proj = by_core(core, proj_keep, core_swap(proj_send), 0)
    attn_terms = jnp.concatenate([grad_query, grad_proj], axis=1)

    pair_sum = (pair_mine + pair_got).reshape(back_chips + 1, own, 2 * HD)
    arrived = [
        chip_shift(pair_sum[back_chips - k].astype(BF), -k, False) for k in range(1, back_chips + 1)
    ]
    pair_weight = weights[:, 2 * HALF : 2 * HALF + 2 * HD]
    grad_pair, grad_one_pair, key_bias = after_pairs(
        pair_sum[back_chips], *arrived, normed_one, pair_weight, cosine, sine
    )

    if square_line():
        ups_downs = gather_place(
            ff_rows,
            tuple((i * 2 * rows, 2 * rows, i, 2 * rows, 0) for i in range(4)),
            ((D, D),) * 4,
        )
    else:
        up_whole = gather_whole(by_core(core, up_half(core), core_swap(up_half(1 - core)), 0))
        down_whole = gather_whole(down_weight).reshape(chips, 2, half, D)
        down_whole = down_whole.transpose(1, 0, 2, 3).reshape(2, D, D)
        ups_downs = (up_whole[:, :D], up_whole[:, D:], down_whole[0], down_whole[1])
    first = (normed_two, normed_two_t, grad_out, ups_downs[0], hidden_bias[0:1], ups_downs[2])
    second = (normed_two, normed_two_t, grad_out, ups_downs[1], hidden_bias[1:2], ups_downs[3])
    if square_line():
        attn_planes, attn_one = reduce_first(attn_terms)
    part, dh, terms0, gbias = feed_forward(*first, part)
    if square_line():
        part, dh, terms0, gbias = after((part, dh, terms0, gbias), attn_one, arrived)
        attn_two = reduce_second(attn_planes, attn_one)
        planes0, one0 = reduce_first(terms0)
    more = (dh, features, grad_one, grad_one_pair, vector_rows, sums, gbias, grad_pair)
    second_out = feed_forward(*second, part, more)
    if square_line():
        second_out = after(second_out, attn_two, one0)
    part, part_send, scaled, scaled_send, terms1 = second_out
    part_got, scaled_got = core_swap(part_send), core_swap(scaled_send)

    def finish(part_got, scaled_got):
        layer_out = own_tokens.astype(F32) + part + part_got + vector_rows[5:6]
        total = scaled + scaled_got
        unit, spread = standard(own_tokens)
        input_grad = own_grad.astype(F32) + spread * (
            total
            - jnp.mean(total, axis=-1, keepdims=True)
            - unit * jnp.mean(total * unit, axis=-1, keepdims=True)
        )
        return layer_out.astype(BF), input_grad

    def split(value):
        return (
            lax.dynamic_slice_in_dim(value, core * rows, rows, 0),
            core_swap(lax.dynamic_slice_in_dim(value, (1 - core) * rows, rows, 0)),
        )

    if square_line():
        two0 = reduce_second(planes0, one0)
        planes1, one1 = reduce_first(terms1)
        attn_own, attn_three = reduce_third(attn_planes, attn_two)
        one1, part_got, scaled_got, attn_three = lax.optimization_barrier(
            (one1, part_got, scaled_got, attn_three)
        )
        two1 = reduce_second(planes1, one1)
        own0, three0 = reduce_third(planes0, two0)
        layer_out, input_grad = finish(part_got, scaled_got)
        attn_sum = reduce_last(attn_own, attn_three)
        mine, theirs = split(attn_sum)
        two1, layer_out, input_grad, three0, theirs = lax.optimization_barrier(
            (two1, layer_out, input_grad, three0, theirs)
        )
        own1, three1 = reduce_third(planes1, two1)
        sum0 = reduce_last(own0, three0)
        up_first = split(sum0[:, :D])
        query_out = by_core(core, mine[:, :HALF], theirs[:, :HALF], 1)
        proj_out = by_core(core, mine[:, HALF:], theirs[:, HALF:], 1)
        key_bias_out = sum_everywhere(key_bias[0, :HD])
        own1 = after(own1, query_out, proj_out, up_first, key_bias_out)
        sum1 = reduce_last(own1, three1)
    else:
        layer_out, input_grad = finish(part_got, scaled_got)
        sum0, sum1 = reduce_whole(terms0), reduce_whole(terms1)
        mine, theirs = split(reduce_whole(attn_terms))
        query_out = by_core(core, mine[:, :HALF], theirs[:, :HALF], 1)
        proj_out = by_core(core, mine[:, HALF:], theirs[:, HALF:], 1)
        up_first = split(sum0[:, :D])
        key_bias_out = sum_everywhere(key_bias[0, :HD])
    mine, theirs = split(jnp.concatenate([sum1[:, :D], sum1[:, 2 * D :]], axis=1))
    up_second = (mine[:, :D], theirs[:, :D])
    rest = mine[:, D:] + theirs[:, D:]
    pair_out, vector_out = rest[:, : 2 * HD], rest[:, 2 * HD :]
    up_bias_out = sum1[:, 2 * D + 2 * HD + 6 : 2 * D + 2 * HD + 8].T.reshape(hidden)

    def blocks(first_half, second_half):
        return jnp.stack(
            [value.reshape(rows, chips, half) for value in (first_half, second_half)], axis=2
        ).reshape(rows, chips, 1, hidden)

    mine, theirs = blocks(up_first[0], up_second[0]), blocks(up_first[1], up_second[1])
    up_out = by_core(core, mine, theirs, 2).reshape(rows, FF)
    down_out = jnp.concatenate([sum0[:, D:], sum1[:, D : 2 * D]], axis=0)
    return (
        layer_out[None],
        input_grad[None],
        vector_out[:, 0],
        vector_out[:, 1],
        vector_out[:, 2],
        vector_out[:, 3],
        query_out,
        vector_out[:, 4],
        pair_out,
        key_bias_out,
        proj_out,
        vector_out[:, 5],
        up_out,
        up_bias_out,
        down_out,
    )


def solution(mesh):
    devices = mesh.devices.reshape(mesh.shape["rows"], mesh.shape["wide"] // 2, 2)
    every, wide = ("rows", "chip", "core"), ("chip", "core")
    matrix, vector, sequence = P(every, None), P(every), P("rows", wide, None)
    return jax.shard_map(
        shards,
        mesh=Mesh(devices, every),
        in_specs=(
            sequence,
            P("rows", None),
            vector,
            vector,
            vector,
            vector,
            matrix,
            vector,
            matrix,
            P(),
            matrix,
            vector,
            matrix,
            vector,
            matrix,
            sequence,
        ),
        out_specs=(
            sequence,
            sequence,
            vector,
            vector,
            vector,
            vector,
            matrix,
            vector,
            matrix,
            P(),
            matrix,
            vector,
            matrix,
            vector,
            matrix,
        ),
        check_vma=False,
    )
```

time: 587 us -> 283 us (0.48)
  Pallas kernels: 277 us -> 101 us
  matrix products: 68.6 us -> 0 us
  local copies, waits for them, and re-layouts: 53.6 us -> 24.1 us
  starting transfers between devices: 87.1 us -> 66.9 us
  other arithmetic: 45.4 us -> 25.3 us
  waiting for transfers between devices: 46.1 us -> 60.5 us
    pallas_call x4 -> x8, Pallas kernels: 196 us -> 58.4 us  [the longest x2 35.3 us: feed_forward(): pl.pallas_call(kernel, out_shape=shapes, grid=(units + blocks,), in_specs...]
    dot_general x15 -> x0, matrix products: 68.6 us -> none  [dot(): lax.dot_general(left, right, (dims, ((), ())), preferred_element_type=F32)]
    pallas_call x1, Pallas kernels: 81.7 us -> 42.2 us  [attention(): pl.pallas_call(attn_kernel, out_shape=(jax.ShapeDtypeStruct((features, to...]
    ppermute x25 -> x19, waiting for transfers between devices: 19.8 us -> 45.3 us  [chip_shift(): return lax.ppermute(value, 'chip', pairs)]
    ppermute x30 -> x20, waiting for transfers between devices: 22.8 us -> 10.8 us  [rows_swap(): return lax.ppermute(value, 'rows', [(r, r ^ bit) for r in range(4)])]
    ppermute x30 -> x20, starting transfers between devices: 34.9 us -> 24.8 us  [rows_swap(): return lax.ppermute(value, 'rows', [(r, r ^ bit) for r in range(4)])]
    ppermute x14, starting transfers between devices: 25.8 us -> 16 us  [core_swap(): return lax.ppermute(value, 'core', [(0, 1), (1, 0)])]
    convert_element_type x12 -> x6, other arithmetic: 13.1 us -> 3.97 us  [the longest x3 2.54 us: reduce_third(): line(step).astype(BF)]
  transfers between devices with their start and end apart: 71 -> 55, of which waited for: 13 -> 20; matrix products, arithmetic and copies ran while one was open for 26% -> 13% of each run, Pallas kernels for 48% -> 32%
where the time goes in v2:
time: 283 us; the launch traced here: 279 us
  Pallas kernels  101 us (36%)
  starting transfers between devices  66.9 us (24%)
  waiting for transfers between devices  60.5 us (21%)
  other arithmetic  25.3 us (9%)
  local copies, waits for them, and re-layouts  24.1 us (9%)
    ppermute x19, waiting for transfers between devices, chip_shift(): return lax.ppermute(value, 'chip', pairs)  45.3 us
    pallas_call x1, Pallas kernels, attention(): pl.pallas_call(attn_kernel, out_shape=(jax.ShapeDtypeStruct((features, to...  42.2 us
    pallas_call x2, Pallas kernels, feed_forward(): pl.pallas_call(kernel, out_shape=shapes, grid=(units + blocks,), in_specs...  35.3 us
    ppermute x19, starting transfers between devices, chip_shift(): return lax.ppermute(value, 'chip', pairs)  26.2 us
    ppermute x20, starting transfers between devices, rows_swap(): return lax.ppermute(value, 'rows', [(r, r ^ bit) for r in range(4)])  24.8 us
    ppermute x14, starting transfers between devices, core_swap(): return lax.ppermute(value, 'core', [(0, 1), (1, 0)])  16 us
    ppermute x20, waiting for transfers between devices, rows_swap(): return lax.ppermute(value, 'rows', [(r, r ^ bit) for r in range(4)])  10.8 us
    unnamed x74, local copies, waits for them, and re-layouts  8.84 us
  transfers between devices with their start and end apart: 55, of which 20 were waited for; matrix products, arithmetic and copies ran while one was open for 13% of the time, Pallas kernels for 32%

profile of v2, /device:TPU:25, one launch (start us, length us, event | category | flops | bytes accessed | tf_op | source)
XLA Modules:
  0.0 279.0 jit_solution(13892201234419085672)
XLA Ops:
  9.6 3.3 %collective-permute-done.4 = bf16[80,896]{1,0:T(8,128)(2,1)S(1)} collective-permute-done((bf16[80,896]{1,0:T(8,128)(2,1)S(1)}, bf16[80,896]{1,0:T(8,128)(2,1)S(1)}, u32[]{:S(2)}, u32[]{:S(2)}) %collective-permute-start.4) | collective-permute-done | bytes 143392 | tf_op jit(solution)/shard_map/ppermute | solution.py:41
  12.9 9.1 %collective-permute-done.3 = bf16[80,896]{1,0:T(8,128)(2,1)S(1)} collective-permute-done((bf16[80,896]{1,0:T(8,128)(2,1)S(1)}, bf16[80,896]{1,0:T(8,128)(2,1)S(1)}, u32[]{:S(2)}, u32[]{:S(2)}) %collective-permute-start.3) | collective-permute-done | bytes 143392 | tf_op jit(solution)/shard_map/ppermute | solution.py:41
  24.8 6.3 %collective-permute-done.9 = bf16[192,768]{1,0:T(8,128)(2,1)S(1)} collective-permute-done((bf16[192,768]{1,0:T(8,128)(2,1)S(1)}, bf16[192,768]{1,0:T(8,128)(2,1)S(1)}, u32[]{:S(2)}, u32[]{:S(2)}) %collective-permute-start.9) | collective-permute-done | bytes 294944 | tf_op jit(solution)/shard_map/ppermute | solution.py:41
  38.4 10.2 %collective-permute-done.10 = bf16[192,768]{1,0:T(8,128)(2,1)S(1)} collective-permute-done((bf16[192,768]{1,0:T(8,128)(2,1)S(1)}, bf16[192,768]{1,0:T(8,128)(2,1)S(1)}, u32[]{:S(2)}, u32[]{:S(2)}) %collective-permute-start.10) | collective-permute-done | bytes 294944 | tf_op jit(solution)/shard_map/ppermute | solution.py:41
  49.4 3.5 %place.2 = (bf16[768,896]{1,0:T(8,128)(2,1)}, bf16[512,896]{1,0:T(8,128)(2,1)}) custom-call(bf16[320,896]{1,0:T(8,128)(2,1)} %copy-done.20, bf16[320,896]{1,0:T(8,128)(2,1)} %collective-permute-done.5.flat_ref, bf16[320,896]{1,0:T(8,128)(2,1)} %collective-permute-done.6.cross_ref, bf16[320,896]{1,0:T(8,128)(2,1)} %collective-permute-done.7.far_ref), custom_call_target="tpu_custom_call" | custom-call | bytes 4587520 | tf_op jit(solution)/shard_map/place/pallas_call | solution.py:79
  57.5 3.9 %front.1 = (bf16[1024,768]{1,0:T(8,128)(2,1)S(1)}, bf16[1024,768]{1,0:T(8,128)(2,1)}, bf16[768,1024]{1,0:T(8,128)(2,1)}, bf16[384,1024]{1,0:T(8,128)(2,1)S(1)}, ...) custom-call(bf16[512,768]{1,0:T(8,128)(2,1)S(1)} %bitcast.235, ...), custom_call_target="tpu_custom_call" | custom-call | flops 805306368 | bytes 6291456 | tf_op jit(solution)/shard_map/front/pallas_call | solution.py:230
  68.7 2.6 collective-permute-done.14
  78.0 42.2 %attention.1 = (bf16[384,1024]{1,0:T(8,128)(2,1)S(1)}, bf16[384,1024]{1,0:T(8,128)(2,1)S(1)}, f32[1536,128]{1,0:T(8,128)S(1)}, f32[1536,128]{1,0:T(8,128)}) custom-call(s32[13]{0:T(128)S(1)} %pad_add_fusion.2.scal_ref, bf16[384,1024]{1,0:T(8,128)(2,1)S(1)} %copy-done.8, bf16[1024,768]{1,0:T(8,128)(2,1)} %pad_maximum_fusion.grad_ref.g_ref, ...), custom_call_target="tpu_custom_call" | custom-call | flops 7247757312 | bytes 3145728 | tf_op jit(solution)/shard_map/attention/pallas_call | solution.py:360
  126.7 7.4 %collective-permute-start.24 = (bf16[512,128]{1,0:T(8,128)(2,1)S(1)}, bf16[512,128]{1,0:T(8,128)(2,1)S(1)}, u32[]{:S(2)}, u32[]{:S(2)}) collective-permute-start(bf16[512,128]{1,0:T(8,128)(2,1)S(1)} %get-tuple-element.233), channel_id=1, source_target_pairs={{2,0},{4,2},{6,4},{3,1},{5,3},{7,5},{10,8},{12,10},{14,12},{11,9},... | collective-permute-start | bytes 393224 | tf_op jit(solution)/shard_map/ppermute | solution.py:41
  134.1 3.1 %collective-permute-start.25 = (bf16[512,128]{1,0:T(8,128)(2,1)S(1)}, bf16[512,128]{1,0:T(8,128)(2,1)S(1)}, u32[]{:S(2)}, u32[]{:S(2)}) collective-permute-start(bf16[512,128]{1,0:T(8,128)(2,1)S(1)} %get-tuple-element.232), channel_id=1, source_target_pairs={{4,0},{6,2},{5,1},{7,3},{12,8},{14,10},{13,9},{15,11},{20,16},{22,... | collective-permute-start | bytes 393224 | tf_op jit(solution)/shard_map/ppermute | solution.py:41
  137.3 7.5 %after_heads.1 = (f32[1024,768]{1,0:T(8,128)}, f32[1024,768]{1,0:T(8,128)}, bf16[768,384]{1,0:T(8,128)(2,1)S(1)}, bf16[384,384]{1,0:T(8,128)(2,1)S(1)}, bf16[384...) custom-call(bf16[384,1024]{1,0:T(8,128)(2,1)S(1)} %copy-done.13, bf16[384,1024]{1,0:T(8,128)(2,1)S(1)} %copy-done.15, ...), custom_call_target="tpu_custom_call" | custom-call | flops 2415919104 | bytes 9437184 | tf_op jit(solution)/shard_map/after_heads/pallas_call | solution.py:428
  150.8 5.1 %place.3 = (bf16[768,768]{1,0:T(8,128)(2,1)}, bf16[768,768]{1,0:T(8,128)(2,1)}, bf16[768,768]{1,0:T(8,128)(2,1)}, bf16[768,768]{1,0:T(8,128)(2,1)}) custom-call(bf16[768,768]{1,0:T(8,128)(2,1)} %pad_maximum_fusion.2.lines_ref, bf16[768,768]{1,0:T(8,128)(2,1)} %collective-permute-done.17.flat_ref, bf16[768,768]{1,0:T(8,128)(2,1)} %collective-permute-done.18.cross_ref, ...), custom_call_target="tpu_custom_call" | custom-call | bytes 9437184 | tf_op jit(solution)/shard_map/place/pallas_call | solution.py:79
  158.0 7.1 %collective-permute-start.23 = (bf16[2,48,768]{2,1,0:T(8,128)(2,1)S(1)}, bf16[2,48,768]{2,1,0:T(8,128)(2,1)S(1)}, u32[]{:S(2)}, u32[]{:S(2)}) collective-permute-start(bf16[2,48,768]{2,1,0:T(8,128)(2,1)S(1)} %get-tuple-element.229), channel_id=1, source_target_pairs={{0,16},{8,24},{16,0},{24,8},{1,17},{9,25},{17,1},{25,9},{2,18},{10... | collective-permute-start | bytes 442376 | tf_op jit(solution)/shard_map/ppermute | solution.py:35
  165.1 16.0 %ffn.2 = (f32[1024,768]{1,0:T(8,128)}, f32[1024,768]{1,0:T(8,128)}, bf16[768,1536]{1,0:T(8,128)(2,1)}, f32[1,768]{1,0:T(1,128)}) custom-call(bf16[1024,768]{1,0:T(8,128)(2,1)} %get-tuple-element.111.h_ref, bf16[768,1024]{1,0:T(8,128)(2,1)} %get-tuple-element.112.ht_ref, bf16[1024,768]{1,0:T(8,128)(2,1)} %pad_maximum_fusion.grad_ref.g_ref, ...), custom_call_target="tpu_custom_call" | custom-call | flops 7247757312 | bytes 20447232 | tf_op jit(solution)/shard_map/ffn/pallas_call | solution.py:631
  185.9 19.3 %ffn.3 = (f32[512,768]{1,0:T(8,128)}, f32[512,768]{1,0:T(8,128)}, f32[512,768]{1,0:T(8,128)}, f32[512,768]{1,0:T(8,128)}, bf16[768,1792]{1,0:T(8,128)(2,1)}) custom-call(bf16[1024,768]{1,0:T(8,128)(2,1)} %get-tuple-element.111.h_ref, bf16[768,1024]{1,0:T(8,128)(2,1)} %get-tuple-element.112.ht_ref, bf16[1024,768]{1,0:T(8,128)(2,1)} %pad_maximum_fusion.grad_ref.g_ref, ...), custom_call_target="tpu_custom_call" | custom-call | flops 7247757312 | bytes 20447232 | tf_op jit(solution)/shard_map/ffn/pallas_call | solution.py:631
  205.2 2.9 %collective-permute-start.32 = (f32[512,768]{1,0:T(8,128)}, f32[512,768]{1,0:T(8,128)S(1)}, u32[]{:S(2)}, u32[]{:S(2)}) collective-permute-start(f32[512,768]{1,0:T(8,128)} %get-tuple-element.170), channel_id=1, source_target_pairs={{0,1},{1,0},{2,3},{3,2},{4,5},{5,4},{6,7},{7,6},{8,9},{9,8},{10,11... | collective-permute-start | bytes 4718600 | tf_op jit(solution)/shard_map/ppermute | solution.py:31
  222.0 5.2 %collective-permute-done.40 = bf16[4,48,1536]{2,1,0:T(8,128)(2,1)} collective-permute-done((bf16[4,48,1536]{2,1,0:T(8,128)(2,1)}, bf16[4,48,1536]{2,1,0:T(8,128)(2,1)}, u32[]{:S(2)}, u32[]{:S(2)}) %collective-permute-start.40) | collective-permute-done | bytes 589856 | tf_op jit(solution)/shard_map/ppermute | solution.py:35
  232.1 2.6 collective-permute-done.36
  245.8 3.1 %collective-permute-start.44 = (f32[24,768]{1,0:T(8,128)S(1)}, f32[24,768]{1,0:T(8,128)S(1)}, u32[]{:S(2)}, u32[]{:S(2)}) collective-permute-start(f32[24,768]{1,0:T(8,128)S(1)} %constant_dynamic-slice_fusion.3), channel_id=1, source_target_pairs={{0,1},{1,0},{2,3},{3,2},{4,5},{5,4},{6,7},{7,6},{8,9},{9,8},{10,11... | collective-permute-start | bytes 221192 | tf_op jit(solution)/shard_map/ppermute | solution.py:31
  249.8 3.1 %collective-permute-done.37 = bf16[4,48,1792]{2,1,0:T(8,128)(2,1)S(1)} collective-permute-done((bf16[4,48,1792]{2,1,0:T(8,128)(2,1)S(1)}, bf16[4,48,1792]{2,1,0:T(8,128)(2,1)S(1)}, u32[]{:S(2)}, u32[]{:S(2)}) %collective-permute-start.37) | collective-permute-done | bytes 688160 | tf_op jit(solution)/shard_map/ppermute | solution.py:35
  254.0 3.7 %collective-permute-start.52 = (bf16[48,1792]{1,0:T(8,128)(2,1)S(1)}, bf16[48,1792]{1,0:T(8,128)(2,1)S(1)}, u32[]{:S(2)}, u32[]{:S(2)}) collective-permute-start(bf16[48,1792]{1,0:T(8,128)(2,1)S(1)} %get-tuple-element.204), channel_id=1, source_target_pairs={{0,4},{2,6},{4,0},{6,2},{1,5},{3,7},{5,1},{7,3},{8,12},{10,14},{12... | collective-permute-start | bytes 516104 | tf_op jit(solution)/shard_map/ppermute | solution.py:41
  258.9 4.3 %collective-permute-start.45 = (f32[24,768]{1,0:T(8,128)S(1)}, f32[24,768]{1,0:T(8,128)S(1)}, u32[]{:S(2)}, u32[]{:S(2)}) collective-permute-start(f32[24,768]{1,0:T(8,128)S(1)} %get-tuple-element.242), channel_id=1, source_target_pairs={{0,1},{1,0},{2,3},{3,2},{4,5},{5,4},{6,7},{7,6},{8,9},{9,8},{10,11... | collective-permute-start | bytes 221192 | tf_op jit(solution)/shard_map/ppermute | solution.py:31
  265.4 3.5 %collective-permute-done.52 = bf16[48,1792]{1,0:T(8,128)(2,1)S(1)} collective-permute-done((bf16[48,1792]{1,0:T(8,128)(2,1)S(1)}, bf16[48,1792]{1,0:T(8,128)(2,1)S(1)}, u32[]{:S(2)}, u32[]{:S(2)}) %collective-permute-start.52) | collective-permute-done | bytes 172064 | tf_op jit(solution)/shard_map/ppermute | solution.py:41
  268.9 3.1 %collective-permute-done.51 = bf16[48,1792]{1,0:T(8,128)(2,1)S(1)} collective-permute-done((bf16[48,1792]{1,0:T(8,128)(2,1)S(1)}, bf16[48,1792]{1,0:T(8,128)(2,1)S(1)}, u32[]{:S(2)}, u32[]{:S(2)}) %collective-permute-start.51) | collective-permute-done | bytes 172064 | tf_op jit(solution)/shard_map/ppermute | solution.py:41
  (283 shorter events, 99.0 us)
Async XLA Ops:
  0.7 33.0 %collective-permute-start = (bf16[512,768]{1,0:T(8,128)(2,1)}, bf16[512,768]{1,0:T(8,128)(2,1)S(1)}, u32[]{:S(2)}, u32[]{:S(2)}) collective-permute-start(bf16[512,768]{1,0:T(8,128)(2,1)} %bitcast.233), channel_id=1, source_target_pairs={{0,1},{1,0},{2,3},{3,2},{4,5},{5,4},{6,7},{7,6},{8,9},{9,8},{10,11... | collective-permute-start | bytes 2359304 | tf_op jit(solution)/shard_map/ppermute | solution.py:31
  7.0 27.6 %collective-permute-start.12 = (bf16[512,768]{1,0:T(8,128)(2,1)S(1)}, bf16[512,768]{1,0:T(8,128)(2,1)}, u32[]{:S(2)}, u32[]{:S(2)}) collective-permute-start(bf16[512,768]{1,0:T(8,128)(2,1)S(1)} %bitcast.240), channel_id=1, source_target_pairs={{0,1},{1,0},{2,3},{3,2},{4,5},{5,4},{6,7},{7,6},{8,9},{9,8},{10,11... | collective-permute-start | bytes 2359304 | tf_op jit(solution)/shard_map/ppermute | solution.py:31
  22.3 26.3 %collective-permute-start.5 = (bf16[320,896]{1,0:T(8,128)(2,1)S(1)}, bf16[320,896]{1,0:T(8,128)(2,1)}, u32[]{:S(2)}, u32[]{:S(2)}) collective-permute-start(bf16[320,896]{1,0:T(8,128)(2,1)S(1)} %pad_maximum_fusion.8.lines_ref), channel_id=1, source_target_pairs={{0,8},{8,0},{16,24},{24,16},{1,9},{9,1},{17,25},{25,17},{2,10},{10... | collective-permute-start | bytes 1720328 | tf_op jit(solution)/shard_map/ppermute | solution.py:35
  23.6 25.0 %collective-permute-start.6 = (bf16[320,896]{1,0:T(8,128)(2,1)S(1)}, bf16[320,896]{1,0:T(8,128)(2,1)}, u32[]{:S(2)}, u32[]{:S(2)}) collective-permute-start(bf16[320,896]{1,0:T(8,128)(2,1)S(1)} %pad_maximum_fusion.8.lines_ref), channel_id=1, source_target_pairs={{0,16},{8,24},{16,0},{24,8},{1,17},{9,25},{17,1},{25,9},{2,18},{10... | collective-permute-start | bytes 1720328 | tf_op jit(solution)/shard_map/ppermute | solution.py:35
  31.1 18.3 %collective-permute-start.7 = (bf16[320,896]{1,0:T(8,128)(2,1)S(1)}, bf16[320,896]{1,0:T(8,128)(2,1)}, u32[]{:S(2)}, u32[]{:S(2)}) collective-permute-start(bf16[320,896]{1,0:T(8,128)(2,1)S(1)} %pad_maximum_fusion.8.lines_ref), channel_id=1, source_target_pairs={{0,24},{8,16},{16,8},{24,0},{1,25},{9,17},{17,9},{25,1},{2,26},{10... | collective-permute-start | bytes 1720328 | tf_op jit(solution)/shard_map/ppermute | solution.py:35
  33.6 15.0 %collective-permute-start.10 = (bf16[192,768]{1,0:T(8,128)(2,1)S(1)}, bf16[192,768]{1,0:T(8,128)(2,1)S(1)}, u32[]{:S(2)}, u32[]{:S(2)}) collective-permute-start(bf16[192,768]{1,0:T(8,128)(2,1)S(1)} %pad_maximum_fusion.11), channel_id=1, source_target_pairs={{0,4},{2,6},{4,0},{6,2},{1,5},{3,7},{5,1},{7,3},{8,12},{10,14},{12... | collective-permute-start | bytes 884744 | tf_op jit(solution)/shard_map/ppermute | solution.py:41
  66.1 56.6 %collective-permute-start.17 = (bf16[768,768]{1,0:T(8,128)(2,1)}, bf16[768,768]{1,0:T(8,128)(2,1)}, u32[]{:S(2)}, u32[]{:S(2)}) collective-permute-start(bf16[768,768]{1,0:T(8,128)(2,1)} %pad_maximum_fusion.2.lines_ref), channel_id=1, source_target_pairs={{0,8},{8,0},{16,24},{24,16},{1,9},{9,1},{17,25},{25,17},{2,10},{10... | collective-permute-start | bytes 3538952 | tf_op jit(solution)/shard_map/ppermute | solution.py:35
  66.8 55.9 %collective-permute-start.18 = (bf16[768,768]{1,0:T(8,128)(2,1)}, bf16[768,768]{1,0:T(8,128)(2,1)}, u32[]{:S(2)}, u32[]{:S(2)}) collective-permute-start(bf16[768,768]{1,0:T(8,128)(2,1)} %pad_maximum_fusion.2.lines_ref), channel_id=1, source_target_pairs={{0,16},{8,24},{16,0},{24,8},{1,17},{9,25},{17,1},{25,9},{2,18},{10... | collective-permute-start | bytes 3538952 | tf_op jit(solution)/shard_map/ppermute | solution.py:35
  67.1 55.6 %collective-permute-start.19 = (bf16[768,768]{1,0:T(8,128)(2,1)}, bf16[768,768]{1,0:T(8,128)(2,1)}, u32[]{:S(2)}, u32[]{:S(2)}) collective-permute-start(bf16[768,768]{1,0:T(8,128)(2,1)} %pad_maximum_fusion.2.lines_ref), channel_id=1, source_target_pairs={{0,24},{8,16},{16,8},{24,0},{1,25},{9,17},{17,9},{25,1},{2,26},{10... | collective-permute-start | bytes 3538952 | tf_op jit(solution)/shard_map/ppermute | solution.py:35
  126.7 18.1 %collective-permute-start.24 = (bf16[512,128]{1,0:T(8,128)(2,1)S(1)}, bf16[512,128]{1,0:T(8,128)(2,1)S(1)}, u32[]{:S(2)}, u32[]{:S(2)}) collective-permute-start(bf16[512,128]{1,0:T(8,128)(2,1)S(1)} %get-tuple-element.233), channel_id=1, source_target_pairs={{2,0},{4,2},{6,4},{3,1},{5,3},{7,5},{10,8},{12,10},{14,12},{11,9},... | collective-permute-start | bytes 393224 | tf_op jit(solution)/shard_map/ppermute | solution.py:41
  156.0 25.2 %collective-permute-start.49 = (f32[64]{0:T(128)S(1)}, f32[64]{0:T(128)S(1)}, u32[]{:S(2)}, u32[]{:S(2)}) collective-permute-start(f32[64]{0:T(128)S(1)} %add.473), channel_id=1, source_target_pairs={{0,8},{8,0},{16,24},{24,16},{1,9},{9,1},{17,25},{25,17},{2,10},{10... | collective-permute-start | bytes 776 | tf_op jit(solution)/shard_map/ppermute | solution.py:35
  157.6 23.6 %collective-permute-start.22 = (bf16[2,48,768]{2,1,0:T(8,128)(2,1)S(1)}, bf16[2,48,768]{2,1,0:T(8,128)(2,1)S(1)}, u32[]{:S(2)}, u32[]{:S(2)}) collective-permute-start(bf16[2,48,768]{2,1,0:T(8,128)(2,1)S(1)} %get-tuple-element.228), channel_id=1, source_target_pairs={{0,8},{8,0},{16,24},{24,16},{1,9},{9,1},{17,25},{25,17},{2,10},{10... | collective-permute-start | bytes 442376 | tf_op jit(solution)/shard_map/ppermute | solution.py:35
  158.0 23.3 %collective-permute-start.23 = (bf16[2,48,768]{2,1,0:T(8,128)(2,1)S(1)}, bf16[2,48,768]{2,1,0:T(8,128)(2,1)S(1)}, u32[]{:S(2)}, u32[]{:S(2)}) collective-permute-start(bf16[2,48,768]{2,1,0:T(8,128)(2,1)S(1)} %get-tuple-element.229), channel_id=1, source_target_pairs={{0,16},{8,24},{16,0},{24,8},{1,17},{9,25},{17,1},{25,9},{2,18},{10... | collective-permute-start | bytes 442376 | tf_op jit(solution)/shard_map/ppermute | solution.py:35
  181.2 33.7 %collective-permute-start.50 = (f32[64]{0:T(128)S(1)}, f32[64]{0:T(128)S(1)}, u32[]{:S(2)}, u32[]{:S(2)}) collective-permute-start(f32[64]{0:T(128)S(1)} %add.474), channel_id=1, source_target_pairs={{0,16},{8,24},{16,0},{24,8},{1,17},{9,25},{17,1},{25,9},{2,18},{10... | collective-permute-start | bytes 776 | tf_op jit(solution)/shard_map/ppermute | solution.py:35
  181.4 23.7 %collective-permute-start.26 = (bf16[4,48,768]{2,1,0:T(8,128)(2,1)S(1)}, bf16[4,48,768]{2,1,0:T(8,128)(2,1)S(1)}, u32[]{:S(2)}, u32[]{:S(2)}) collective-permute-start(bf16[4,48,768]{2,1,0:T(8,128)(2,1)S(1)} %pad_maximum_fusion.12), channel_id=1, source_target_pairs={{0,8},{8,0},{16,24},{24,16},{1,9},{9,1},{17,25},{25,17},{2,10},{10... | collective-permute-start | bytes 884744 | tf_op jit(solution)/shard_map/ppermute | solution.py:35
  182.2 23.0 %collective-permute-start.27 = (bf16[4,48,768]{2,1,0:T(8,128)(2,1)S(1)}, bf16[4,48,768]{2,1,0:T(8,128)(2,1)S(1)}, u32[]{:S(2)}, u32[]{:S(2)}) collective-permute-start(bf16[4,48,768]{2,1,0:T(8,128)(2,1)S(1)} %pad_maximum_fusion.13), channel_id=1, source_target_pairs={{0,16},{8,24},{16,0},{24,8},{1,17},{9,25},{17,1},{25,9},{2,18},{10... | collective-permute-start | bytes 884744 | tf_op jit(solution)/shard_map/ppermute | solution.py:35
  185.0 20.2 %collective-permute-start.28 = (bf16[2,48,1536]{2,1,0:T(8,128)(2,1)S(1)}, bf16[2,48,1536]{2,1,0:T(8,128)(2,1)S(1)}, u32[]{:S(2)}, u32[]{:S(2)}) collective-permute-start(bf16[2,48,1536]{2,1,0:T(8,128)(2,1)S(1)} %get-tuple-element.216), channel_id=1, source_target_pairs={{0,8},{8,0},{16,24},{24,16},{1,9},{9,1},{17,25},{25,17},{2,10},{10... | collective-permute-start | bytes 884744 | tf_op jit(solution)/shard_map/ppermute | solution.py:35
  185.8 19.4 %collective-permute-start.29 = (bf16[2,48,1536]{2,1,0:T(8,128)(2,1)S(1)}, bf16[2,48,1536]{2,1,0:T(8,128)(2,1)S(1)}, u32[]{:S(2)}, u32[]{:S(2)}) collective-permute-start(bf16[2,48,1536]{2,1,0:T(8,128)(2,1)S(1)} %get-tuple-element.218), channel_id=1, source_target_pairs={{0,16},{8,24},{16,0},{24,8},{1,17},{9,25},{17,1},{25,9},{2,18},{10... | collective-permute-start | bytes 884744 | tf_op jit(solution)/shard_map/ppermute | solution.py:35
  205.2 33.6 %collective-permute-start.32 = (f32[512,768]{1,0:T(8,128)}, f32[512,768]{1,0:T(8,128)S(1)}, u32[]{:S(2)}, u32[]{:S(2)}) collective-permute-start(f32[512,768]{1,0:T(8,128)} %get-tuple-element.170), channel_id=1, source_target_pairs={{0,1},{1,0},{2,3},{3,2},{4,5},{5,4},{6,7},{7,6},{8,9},{9,8},{10,11... | collective-permute-start | bytes 4718600 | tf_op jit(solution)/shard_map/ppermute | solution.py:31
  208.1 30.7 %collective-permute-start.33 = (f32[512,768]{1,0:T(8,128)}, f32[512,768]{1,0:T(8,128)}, u32[]{:S(2)}, u32[]{:S(2)}) collective-permute-start(f32[512,768]{1,0:T(8,128)} %get-tuple-element.171), channel_id=1, source_target_pairs={{0,1},{1,0},{2,3},{3,2},{4,5},{5,4},{6,7},{7,6},{8,9},{9,8},{10,11... | collective-permute-start | bytes 4718600 | tf_op jit(solution)/shard_map/ppermute | solution.py:31
  212.3 15.0 %collective-permute-start.40 = (bf16[4,48,1536]{2,1,0:T(8,128)(2,1)}, bf16[4,48,1536]{2,1,0:T(8,128)(2,1)}, u32[]{:S(2)}, u32[]{:S(2)}) collective-permute-start(bf16[4,48,1536]{2,1,0:T(8,128)(2,1)} %pad_maximum_fusion.7), channel_id=1, source_target_pairs={{0,16},{8,24},{16,0},{24,8},{1,17},{9,25},{17,1},{25,9},{2,18},{10... | collective-permute-start | bytes 1769480 | tf_op jit(solution)/shard_map/ppermute | solution.py:35
  215.3 14.4 %collective-permute-start.39 = (bf16[4,48,1536]{2,1,0:T(8,128)(2,1)}, bf16[4,48,1536]{2,1,0:T(8,128)(2,1)}, u32[]{:S(2)}, u32[]{:S(2)}) collective-permute-start(bf16[4,48,1536]{2,1,0:T(8,128)(2,1)} %pad_maximum_fusion.6), channel_id=1, source_target_pairs={{0,8},{8,0},{16,24},{24,16},{1,9},{9,1},{17,25},{25,17},{2,10},{10... | collective-permute-start | bytes 1769480 | tf_op jit(solution)/shard_map/ppermute | solution.py:35
  221.3 15.5 %collective-permute-start.30 = (bf16[2,48,1792]{2,1,0:T(8,128)(2,1)S(1)}, bf16[2,48,1792]{2,1,0:T(8,128)(2,1)S(1)}, u32[]{:S(2)}, u32[]{:S(2)}) collective-permute-start(bf16[2,48,1792]{2,1,0:T(8,128)(2,1)S(1)} %get-tuple-element.212), channel_id=1, source_target_pairs={{0,8},{8,0},{16,24},{24,16},{1,9},{9,1},{17,25},{25,17},{2,10},{10... | collective-permute-start | bytes 1032200 | tf_op jit(solution)/shard_map/ppermute | solution.py:35
  254.0 14.9 %collective-permute-start.52 = (bf16[48,1792]{1,0:T(8,128)(2,1)S(1)}, bf16[48,1792]{1,0:T(8,128)(2,1)S(1)}, u32[]{:S(2)}, u32[]{:S(2)}) collective-permute-start(bf16[48,1792]{1,0:T(8,128)(2,1)S(1)} %get-tuple-element.204), channel_id=1, source_target_pairs={{0,4},{2,6},{4,0},{6,2},{1,5},{3,7},{5,1},{7,3},{8,12},{10,14},{12... | collective-permute-start | bytes 516104 | tf_op jit(solution)/shard_map/ppermute | solution.py:41
  (67 other events, 481.9 us)

commit v3 on v2

v3 whole, which is shorter than its diff:
```python
import functools
import math

import jax
import jax.numpy as jnp
from jax import lax
from jax.experimental import pallas as pl
from jax.experimental.pallas import tpu as pltpu
from jax.sharding import Mesh, PartitionSpec as P

D = 768
HEADS = 12
HD = 64
ROT = 16
DOC = 2048
FF = 3072
MAX_SEGS = 32
norm_eps = 1e-05
BF = jnp.bfloat16
F32 = jnp.float32
HALF = HEADS // 2 * HD
BLK = 256
GROUP = 6


def dot(left, right, dims):
    return lax.dot_general(left, right, (dims, ((), ())), preferred_element_type=F32)


def core_swap(value):
    return lax.ppermute(value, "core", [(0, 1), (1, 0)])


def rows_swap(value, bit):
    return lax.ppermute(value, "rows", [(r, r ^ bit) for r in range(4)])


def chip_shift(value, by, wrap):
    count = lax.axis_size("chip")
    pairs = [(s, (s + by) % count) for s in range(count) if wrap or 0 <= s + by < count]
    return lax.ppermute(value, "chip", pairs)


def square_line():
    return lax.axis_size("rows") == 4 and lax.axis_size("chip") == 4


def place_copies(parts, sources, outs, sems):
    row, chip = lax.axis_index("rows"), lax.axis_index("chip")
    size = sources[0].shape[0] // 4
    copies = []
    for first, count, out in parts:
        for turn, source in enumerate(sources):
            for step in range(4):
                place = (row ^ turn) * 4 + lax.rem(chip + step, 4)
                copies.append(
                    pltpu.make_async_copy(
                        source.at[pl.ds(step * size + first, count)],
                        outs[out].at[pl.ds(pl.multiple_of(place * count, 8), count)],
                        sems.at[len(copies)],
                    )
                )
    return copies


def gather_line(piece):
    return [piece] + [chip_shift(piece, -k, True) for k in (1, 2, 3)]


def gather_rows(lines):
    return lines, rows_swap(lines, 1), rows_swap(lines, 2), rows_swap(lines, 3)


def gather_whole(piece):
    return lax.all_gather(piece, ("rows", "chip"), axis=0, tiled=True)


def reduce_first(terms):
    row = lax.axis_index("rows")
    grid = terms.reshape((4, 4, terms.shape[0] // 16) + terms.shape[1:])
    planes = [lax.dynamic_index_in_dim(grid, row ^ bit, 0, keepdims=False) for bit in range(4)]
    return planes, (rows_swap(planes[3][:2], 1), rows_swap(planes[3][2:], 2))


def reduce_rows(terms):
    row = lax.axis_index("rows")
    grid = terms.reshape((4, 4, terms.shape[0] // 16) + terms.shape[1:])
    planes = [lax.dynamic_index_in_dim(grid, row ^ bit, 0, keepdims=False) for bit in range(4)]
    return planes[0], [rows_swap(planes[bit], bit) for bit in (3, 1, 2)]


def reduce_second(planes, arrived):
    _, flat, cross, _ = planes
    from_flat, from_cross = arrived
    to_flat = jnp.concatenate(
        [flat[:2], (flat[2:].astype(F32) + from_cross.astype(F32)).astype(BF)], axis=0
    )
    to_cross = jnp.concatenate(
        [(cross[:2].astype(F32) + from_flat.astype(F32)).astype(BF), cross[2:]], axis=0
    )
    return rows_swap(to_flat, 1), rows_swap(to_cross, 2)


def reduce_third(own, arrived):
    chip = lax.axis_index("chip")

    def line(step):
        spot = lax.rem(chip + step, 4)
        pick = [
            lax.dynamic_index_in_dim(part, spot, 0, keepdims=False).astype(F32)
            for part in (own, *arrived)
        ]
        return sum(pick[1:], pick[0])

    return line(0), [chip_shift(line(step).astype(BF), step, True) for step in (1, 2, 3)]


def reduce_last(own, arrived):
    return own + arrived[0].astype(F32) + arrived[1].astype(F32) + arrived[2].astype(F32)


def reduce_whole(terms):
    return lax.psum_scatter(terms.astype(F32), ("rows", "chip"), scatter_dimension=0, tiled=True)


def after(value, *others):
    return lax.optimization_barrier((value, others))[0]


def line_swap(value, bit):
    return lax.ppermute(value, "chip", [(s, s ^ bit) for s in range(4)])


def by_core(core, own, other, axis):
    return jnp.where(
        core == 0,
        jnp.concatenate([own, other], axis=axis),
        jnp.concatenate([other, own], axis=axis),
    )


def pack_kernel(q_ref, out_ref, kv_ref, vectors_ref, mine_ref, theirs_ref):
    core = lax.axis_index("core")
    rows = q_ref.shape[0]
    pick = lax.broadcasted_iota(jnp.int32, (16, 128), 0) == lax.broadcasted_iota(
        jnp.int32, (16, 128), 1
    )
    columns = dot(vectors_ref[...], jnp.where(pick, 1.0, 0.0).astype(BF), ((0,), (0,))).astype(BF)
    for which, ref in ((core, mine_ref), (1 - core, theirs_ref)):
        spot = pl.ds(pl.multiple_of(which * HALF, HALF), HALF)
        ref[:, :HALF] = q_ref[:, spot]
        ref[:, HALF : 2 * HALF] = out_ref[:, spot]
        ref[:, 2 * HALF : 2 * HALF + 2 * HD] = kv_ref[...]
        ref[:, 2 * HALF + 2 * HD :] = columns


def pack(q_weight, out_weight, kv_weight, vectors):
    rows = q_weight.shape[0]
    side = jax.ShapeDtypeStruct((rows, 2 * HALF + 2 * HD + 128), BF)
    return pl.pallas_call(
        pack_kernel,
        out_shape=(side, side),
        cost_estimate=pl.CostEstimate(flops=0, transcendentals=0, bytes_accessed=8 * rows * D),
        name="pack",
    )(q_weight, out_weight, kv_weight, vectors)


def turn(values, cosine, sine, direction):
    half = ROT // 2
    a, b = values[:half, :], values[half:ROT, :]
    return jnp.concatenate(
        [a * cosine - direction * b * sine, b * cosine + direction * a * sine, values[ROT:, :]],
        axis=0,
    )


def standard(tokens):
    values = tokens.astype(F32)
    center = values - jnp.mean(values, axis=-1, keepdims=True)
    spread = lax.rsqrt(jnp.mean(center * center, axis=-1, keepdims=True) + norm_eps)
    return center * spread, spread


def front_rest(
    own_ref, other_ref, kbias_ref, cos_ref, sin_ref, w_ref, rows_ref,
    h1_ref, h2_ref, h2t_ref, q_ref, pairs_ref, keep_ref, send_ref,
):
    core = lax.axis_index("core")
    count = own_ref.shape[0]
    gain_one, shift_one, gain_two, shift_two = (rows_ref[i : i + 1, :] for i in range(4))

    def norm(part, ref):
        unit, _ = standard(ref[...])
        spot = pl.ds(part * count, count)
        h1_ref[spot, :] = (unit * gain_one + shift_one).astype(BF)
        normed = (unit * gain_two + shift_two).astype(BF)
        h2_ref[spot, :] = normed
        h2t_ref[:, part * count : (part + 1) * count] = normed.T

    norm(0, own_ref)
    pair = dot(w_ref[:, 2 * HALF : 2 * HALF + 2 * HD], h1_ref[:count, :], ((0,), (1,)))
    key = turn(
        pair[:HD] + kbias_ref[...], cos_ref[:, :count], sin_ref[:, :count], 1.0
    ).astype(BF)
    pairs_ref[...] = jnp.concatenate([key, pair[HD:].astype(BF)], axis=0).T
    norm(1, other_ref)
    query = dot(w_ref[:, :HALF], h1_ref[...], ((0,), (1,)))
    bias = jnp.where(core == 0, rows_ref[4:5, :HALF], rows_ref[4:5, HALF:])
    query = query + jnp.broadcast_to(bias, (8, HALF)).T[:, :1]
    for h in range(HEADS // 2):
        q_ref[h * HD : (h + 1) * HD, :] = turn(
            query[h * HD : (h + 1) * HD, :], cos_ref[...], sin_ref[...], 1.0
        ).astype(BF)
    for index, ref in ((core, keep_ref), (1 - core, send_ref)):
        spot = pl.ds(pl.multiple_of(index * HALF, HALF), HALF)
        ref[...] = w_ref[spot, HALF : 2 * HALF]


def front_kernel(
    lines_ref, flat_ref, cross_ref, far_ref, own_ref, other_ref, kbias_ref, cos_ref, sin_ref,
    w_ref, rows_ref, bias_ref, h1_ref, h2_ref, h2t_ref, q_ref, pairs_ref, keep_ref, send_ref, sems,
):
    core = lax.axis_index("core")
    copies = place_copies(
        ((0, w_ref.shape[0] // 16, 0),), (lines_ref, flat_ref, cross_ref, far_ref), (w_ref,), sems
    )
    for copy in copies:
        copy.start()
    for copy in copies:
        copy.wait()
    table = w_ref[:, 2 * HALF + 2 * HD :].astype(F32).T
    rows_ref[...] = table[:8, :]
    half = lax.rem(lax.broadcasted_iota(jnp.int32, (1, D), 1), 48) // 24
    for k in range(2):
        low, high = table[6 + 2 * k : 7 + 2 * k, :], table[7 + 2 * k : 8 + 2 * k, :]
        first = jnp.where(half == 0, low, pltpu.roll(jnp.broadcast_to(high, (8, D)), 24, 1)[:1])
        second = jnp.where(
            half == 1, high, pltpu.roll(jnp.broadcast_to(low, (8, D)), D - 24, 1)[:1]
        )
        bias_ref[k : k + 1, :] = jnp.where(core == 0, first, second)
    bias_ref[2:8, :] = jnp.zeros((6, D), F32)
    front_rest(
        own_ref, other_ref, kbias_ref, cos_ref, sin_ref, w_ref, rows_ref,
        h1_ref, h2_ref, h2t_ref, q_ref, pairs_ref, keep_ref, send_ref,
    )


def front_plain_kernel(
    w_ref, rows_ref, own_ref, other_ref, kbias_ref, cos_ref, sin_ref, *outs
):
    front_rest(own_ref, other_ref, kbias_ref, cos_ref, sin_ref, w_ref, rows_ref, *outs)


def front(pieces, own, other, k_bias, cosine, sine):
    both = 2 * own.shape[0]
    placed = len(pieces) == 4
    wide = pieces[0].shape[1]
    shapes = (
        jax.ShapeDtypeStruct((both, D), BF),
        jax.ShapeDtypeStruct((both, D), BF),
        jax.ShapeDtypeStruct((D, both), BF),
        jax.ShapeDtypeStruct((HALF, both), BF),
        jax.ShapeDtypeStruct((own.shape[0], 2 * HD), BF),
        jax.ShapeDtypeStruct((HALF, HALF), BF),
        jax.ShapeDtypeStruct((HALF, HALF), BF),
    )
    here = pl.BlockSpec(memory_space=pltpu.VMEM)
    if placed:
        shapes = (
            jax.ShapeDtypeStruct((D, wide), BF),
            jax.ShapeDtypeStruct((8, D), F32),
            jax.ShapeDtypeStruct((8, D), F32),
        ) + shapes
    return pl.pallas_call(
        front_kernel if placed else front_plain_kernel,
        out_shape=shapes,
        in_specs=[pl.BlockSpec(memory_space=pl.ANY) if placed else here] * len(pieces) + [here] * 5,
        out_specs=tuple(here for _ in shapes),
        scratch_shapes=[pltpu.SemaphoreType.DMA((16,))] if placed else [],
        compiler_params=pltpu.CompilerParams(vmem_limit_bytes=48 << 20),
        cost_estimate=pl.CostEstimate(
            flops=2 * both * D * (HALF + 2 * HD), transcendentals=both, bytes_accessed=8 * both * D
        ),
        name="front",
    )(*pieces, own, other, k_bias, cosine, sine)


def attn_kernel(
    scal_ref, q_ref, grad_ref, keep_in_ref, got_in_ref, pos_ref, cos_ref, sin_ref, mine_ref, theirs_ref,
    o_ref, dq_ref, dmine_ref, dtheirs_ref,
    keep_ref, got_ref, kv_ref, kvt_ref, dkv_ref, g_ref, s_ref, r_ref, rt_ref, sems,
):
    block = pl.program_id(0)
    core = scal_ref[0]
    low, high, edge = (scal_ref[1 + 3 * block + i] for i in range(3))
    wide = GROUP * BLK
    half = kv_ref.shape[0] // 2
    own_blocks = pl.num_programs(0) // 2

    @pl.when(block == 0)
    def _():
        dkv_ref[...] = jnp.zeros_like(dkv_ref)
        copies = [
            pltpu.make_async_copy(source, target, sems.at[i])
            for i, (source, target) in enumerate(
                (
                    (mine_ref, kv_ref.at[pl.ds(0, half)]),
                    (theirs_ref, kv_ref.at[pl.ds(half, half)]),
                    (keep_in_ref, keep_ref),
                    (got_in_ref, got_ref),
                )
            )
        ]
        for copy in copies:
            copy.start()
        for copy in copies:
            copy.wait()
        for part in range(2):
            kvt_ref[: 2 * HD, part * half : (part + 1) * half] = kv_ref[
                part * half : (part + 1) * half, :
            ].T
        kvt_ref[2 * HD :, :] = jnp.ones((16, 2 * half), BF)

    def spot(key_block):
        side = lax.rem(key_block // own_blocks, 2) ^ core
        place = (key_block // (2 * own_blocks)) * own_blocks + lax.rem(key_block, own_blocks)
        return pl.multiple_of(side * half + place * BLK, BLK)

    first, pairs_end, single = low // 2, high // 2, lax.rem(high, 2)
    last = pairs_end - 1 + single
    clear = jnp.clip((edge + 2 * BLK - 1) // (2 * BLK), first, last)

    def slot(key_block, size):
        return pl.ds(pl.multiple_of((key_block - 2 * first) * BLK, BLK), size)

    def over_keys(body, carry):
        def double(masked):
            return lambda i, c: body(masked, 2 * i, 2 * BLK, c)

        carry = lax.fori_loop(first, clear, double(True), carry)
        carry = lax.fori_loop(clear, last, double(False), carry)
        carry = lax.fori_loop(last, pairs_end, double(True), carry)
        return lax.fori_loop(
            0, single, lambda i, c: body(True, 2 * pairs_end + i, BLK, c), carry
        )

    def over_all(body, carry):
        carry = lax.fori_loop(first, pairs_end, lambda i, c: body(2 * i, 2 * BLK, c), carry)
        return lax.fori_loop(0, single, lambda i, c: body(2 * pairs_end + i, BLK, c), carry)

    near = pl.ds(pl.multiple_of(core * HALF, HALF), HALF)
    away = pl.ds(pl.multiple_of((1 - core) * HALF, HALF), HALF)
    g_ref[...] = (
        dot(keep_ref[...], grad_ref[:, near], ((1,), (1,)))
        + dot(got_ref[...], grad_ref[:, away], ((1,), (1,)))
    ).astype(BF)
    starts = jnp.concatenate([pos_ref[0:1, :]] * GROUP, axis=1)
    places = jnp.concatenate([pos_ref[1:2, :]] * GROUP, axis=1)
    blank = jnp.zeros((HD, BLK), BF)
    for h in range(GROUP):
        query = (q_ref[h * HD : (h + 1) * HD, :].astype(F32) * HD**-0.5).astype(BF)
        grad = g_ref[h * HD : (h + 1) * HD, :]
        query = jnp.concatenate([query, blank], axis=0)
        grad = jnp.concatenate([blank, grad], axis=0)
        r_ref[0, :, h * BLK : (h + 1) * BLK] = query
        r_ref[1, :, h * BLK : (h + 1) * BLK] = grad
        rt_ref[h * BLK : (h + 1) * BLK, :] = query.T
        rt_ref[(GROUP + h) * BLK : (GROUP + h + 1) * BLK, :] = grad.T

    def scores(masked, key_block, size, peak):
        keys = kv_ref[pl.ds(spot(key_block), size), :]
        s = dot(keys, r_ref[0], ((1,), (0,)))
        if masked:
            key_places = key_block * BLK + lax.broadcasted_iota(jnp.int32, (size, wide), 0)
            s = jnp.where((key_places >= starts) & (key_places <= places), s, -1e30)
        s_ref[slot(key_block, size), :] = s
        return jnp.maximum(peak, jnp.max(s, axis=0, keepdims=True))

    peak = over_keys(scores, jnp.full((1, wide), -1e30, F32))

    def expo(key_block, size, out):
        values = kvt_ref[HD:, pl.ds(spot(key_block), size)]
        e = jnp.exp(s_ref[slot(key_block, size), :] - peak)
        s_ref[slot(key_block, size), :] = e
        return out + dot(values, e.astype(BF), ((1,), (0,)))

    out = over_all(expo, jnp.zeros((HD + 16, wide), F32))
    inverse = 1.0 / out[HD : HD + 1, :]
    out = out[:HD] * inverse
    deltas = []
    for h in range(GROUP):
        part = out[:, h * BLK : (h + 1) * BLK]
        o_ref[h * HD : (h + 1) * HD, :] = part.astype(BF)
        deltas.append(
            jnp.sum(part * g_ref[h * HD : (h + 1) * HD, :].astype(F32), axis=0, keepdims=True)
        )
    delta = jnp.concatenate(deltas, axis=1)

    def back(key_block, size, dq):
        where = spot(key_block)
        pairs = kv_ref[pl.ds(where, size), :]
        keys = kvt_ref[:HD, pl.ds(where, size)]
        p = s_ref[slot(key_block, size), :] * inverse
        dp = dot(pairs, r_ref[1], ((1,), (0,)))
        ds = (p * (dp - delta)).astype(BF)
        left = jnp.concatenate([ds, p.astype(BF)], axis=1)
        dkv_ref[pl.ds(where, size), :] += dot(left, rt_ref[...], ((1,), (0,)))
        return dq + dot(keys, ds, ((1,), (0,)))

    dq = over_all(back, jnp.zeros((HD, wide), F32)) * HD**-0.5
    for h in range(GROUP):
        part = dq[:, h * BLK : (h + 1) * BLK].astype(BF).astype(F32)
        dq_ref[h * HD : (h + 1) * HD, :] = turn(part, cos_ref[...], sin_ref[...], -1.0).astype(BF)

    @pl.when(block == pl.num_programs(0) - 1)
    def _():
        dmine_ref[...] = dkv_ref[:half, :]
        dtheirs_ref[...] = dkv_ref[half:, :]


def attention(scal, query_t, grad_out, keep, got, pos, cosine, sine, mine, theirs):
    features, tokens = query_t.shape
    blocks, half = tokens // BLK, mine.shape[0]
    tile = pl.BlockSpec((features, BLK), lambda b, s: (0, b))
    small = pl.BlockSpec((8, BLK), lambda b, s: (0, b))

    def whole(rows, columns):
        return pl.BlockSpec((rows, columns), lambda b, s: (0, 0))

    return pl.pallas_call(
        attn_kernel,
        out_shape=(
            jax.ShapeDtypeStruct((features, tokens), BF),
            jax.ShapeDtypeStruct((features, tokens), BF),
            jax.ShapeDtypeStruct((half, 2 * HD), F32),
            jax.ShapeDtypeStruct((half, 2 * HD), F32),
        ),
        grid_spec=pltpu.PrefetchScalarGridSpec(
            num_scalar_prefetch=1,
            grid=(blocks,),
            in_specs=[
                tile,
                pl.BlockSpec((BLK, D), lambda b, s: (b, 0)),
                pl.BlockSpec(memory_space=pltpu.HBM),
                pl.BlockSpec(memory_space=pltpu.HBM),
                small,
                small,
                small,
                pl.BlockSpec(memory_space=pltpu.HBM),
                pl.BlockSpec(memory_space=pltpu.HBM),
            ],
            out_specs=(tile, tile, whole(half, 2 * HD), whole(half, 2 * HD)),
            scratch_shapes=[
                pltpu.VMEM((HALF, HALF), BF),
                pltpu.VMEM((HALF, HALF), BF),
                pltpu.VMEM((2 * half, 2 * HD), BF),
                pltpu.VMEM((2 * HD + 16, 2 * half), BF),
                pltpu.VMEM((2 * half, 2 * HD), F32),
                pltpu.VMEM((features, BLK), BF),
                pltpu.VMEM((DOC + 2 * BLK, GROUP * BLK), F32),
                pltpu.VMEM((2, 2 * HD, GROUP * BLK), BF),
                pltpu.VMEM((2 * GROUP * BLK, 2 * HD), BF),
                pltpu.SemaphoreType.DMA((4,)),
            ],
        ),
        compiler_params=pltpu.CompilerParams(
            dimension_semantics=("arbitrary",), vmem_limit_bytes=48 << 20
        ),
        cost_estimate=pl.CostEstimate(
            flops=12 * features * tokens * DOC * 3 // 4,
            transcendentals=features // HD * tokens * DOC * 3 // 4,
            bytes_accessed=8 * features * tokens,
        ),
        name="attention",
    )(scal, query_t, grad_out, keep, got, pos, cosine, sine, mine, theirs)


def heads_kernel(
    o_ref, dq_ref, h1_ref, grad_ref, gq_ref, keep_out_ref, send_out_ref, sums_ref
):
    core = lax.axis_index("core")
    near = pl.ds(pl.multiple_of(core * HALF, HALF), HALF)
    away = pl.ds(pl.multiple_of((1 - core) * HALF, HALF), HALF)
    send_out_ref[...] = dot(o_ref[...], grad_ref[:, away], ((1,), (0,))).astype(BF)
    keep_out_ref[...] = dot(o_ref[...], grad_ref[:, near], ((1,), (0,))).astype(BF)
    gq_ref[...] = dot(dq_ref[...], h1_ref[...], ((1,), (0,))).T.astype(BF)
    ones = jnp.ones((8, dq_ref.shape[1]), BF)
    sums_ref[...] = jnp.zeros_like(sums_ref)
    sums_ref[0:8, near] = dot(ones, dq_ref[...], ((1,), (1,)))
    count = grad_ref.shape[0] // 2
    sums_ref[8:16, :] = dot(ones[:, :count], grad_ref[:count, :], ((1,), (0,)))


def after_heads(out_t, dq_t, normed, grad_out):
    both = normed.shape[0]
    return pl.pallas_call(
        heads_kernel,
        out_shape=(
            jax.ShapeDtypeStruct((D, HALF), BF),
            jax.ShapeDtypeStruct((HALF, HALF), BF),
            jax.ShapeDtypeStruct((HALF, HALF), BF),
            jax.ShapeDtypeStruct((16, D), F32),
        ),
        compiler_params=pltpu.CompilerParams(vmem_limit_bytes=48 << 20),
        cost_estimate=pl.CostEstimate(
            flops=4 * both * D * HALF, transcendentals=0, bytes_accessed=6 * both * D
        ),
        name="after_heads",
    )(out_t, dq_t, normed, grad_out)


def pairs_kernel(
    own_ref, near_ref, far_ref, h1_ref, w_ref, cos_ref, sin_ref, gw_ref, dh_ref, gbias_ref
):
    total = own_ref[...] + near_ref[...].astype(F32) + far_ref[...].astype(F32)
    total = total.astype(BF).astype(F32).T
    key = turn(total[:HD], cos_ref[...], sin_ref[...], -1.0)
    grad = jnp.concatenate([key, total[HD:]], axis=0).astype(BF)
    gw_ref[...] = dot(grad, h1_ref[...], ((1,), (0,))).T.astype(BF)
    dh_ref[...] = dot(grad.T, w_ref[:, 2 * HALF : 2 * HALF + 2 * HD], ((1,), (1,)))
    ones = jnp.ones((8, grad.shape[1]), BF)
    gbias_ref[...] = dot(ones, grad, ((1,), (1,)))


def after_pairs(pairs, near, far, normed, weights, cosine, sine):
    count = near.shape[0]

    def whole(rows, columns):
        return pl.BlockSpec((rows, columns), lambda i: (0, 0))

    return pl.pallas_call(
        pairs_kernel,
        out_shape=(
            jax.ShapeDtypeStruct((D, 2 * HD), BF),
            jax.ShapeDtypeStruct((count, D), F32),
            jax.ShapeDtypeStruct((8, 2 * HD), F32),
        ),
        grid=(1,),
        in_specs=[
            pl.BlockSpec((count, 2 * HD), lambda i: (pairs.shape[0] // count - 1, 0)),
            whole(count, 2 * HD),
            whole(count, 2 * HD),
            whole(count, D),
            whole(D, weights.shape[1]),
            whole(8, count),
            whole(8, count),
        ],
        out_specs=(whole(D, 2 * HD), whole(count, D), whole(8, 2 * HD)),
        compiler_params=pltpu.CompilerParams(vmem_limit_bytes=32 << 20),
        cost_estimate=pl.CostEstimate(
            flops=8 * count * D * HD, transcendentals=0, bytes_accessed=8 * count * D
        ),
        name="after_pairs",
    )(pairs, near, far, normed, weights, cosine, sine)


def ffn_units(
    placed, h_ref, ht_ref, g_ref, bias_ref, up_ref, down_ref, grad_ref, act_ref, dz_ref
):
    for copy in placed:
        copy.start()
    for copy in placed[: len(placed) // 2]:
        copy.wait()
    z = dot(h_ref[...], up_ref[...], ((1,), (0,))) + bias_ref[...]
    below = 0.5 * (1.0 + lax.erf(z * 0.5**0.5))
    slope = below + z * (jnp.exp(-0.5 * z * z) * (0.5 / math.pi) ** 0.5)
    act = (z * below).astype(BF)
    grad_ref[:, D : 2 * D] = dot(act, g_ref[...], ((0,), (0,))).astype(BF)
    act_ref[...] = act
    for copy in placed[len(placed) // 2 :]:
        copy.wait()
    grad = (dot(g_ref[...], down_ref[...], ((1,), (1,))) * slope).astype(BF)
    dz_ref[...] = grad
    grad_ref[:, :D] = dot(ht_ref[...], grad, ((1,), (0,))).astype(BF)
    return jnp.sum(grad.astype(F32), axis=0, keepdims=True)


def ffn_weights(parts, rest):
    if parts is None:
        return (), rest[0], rest[1], rest[2:]
    up_ref, down_ref, sems = rest[-3:]
    return place_copies(parts, rest[:4], (up_ref, down_ref), sems), up_ref, down_ref, rest[4:-3]


def ffn_first_kernel(parts, h_ref, ht_ref, g_ref, bias_ref, *rest):
    placed, up_ref, down_ref, rest = ffn_weights(parts, rest)
    out_ref, dh_ref, grad_ref, gbias_ref, act_ref, dz_ref = rest
    step = pl.program_id(0)

    @pl.when(step == 0)
    def _():
        gbias_ref[...] = ffn_units(
            placed, h_ref, ht_ref, g_ref, bias_ref, up_ref, down_ref, grad_ref, act_ref, dz_ref
        )

    @pl.when(step > 0)
    def _():
        spot = pl.ds(pl.multiple_of((step - 1) * BLK, BLK), BLK)
        out_ref[...] = dot(act_ref[spot, :], down_ref[...], ((1,), (0,)))
        dh_ref[...] = dot(dz_ref[spot, :], up_ref[...], ((1,), (1,)))


def ffn_second_kernel(parts, h_ref, ht_ref, g_ref, bias_ref, *rest):
    placed, up_ref, down_ref, rest = ffn_weights(parts, rest)
    (
        mlp_ref, dh_in_ref, x_ref, o_ref, dq_ref, w_ref, out_keep_ref, out_got_ref,
        pair_ref, rows_ref, sums_ref, bias0_ref, gpair_ref,
        keep_ref, send_ref, tkeep_ref, tsend_ref, grad_ref,
        act_ref, dz_ref, table_ref,
    ) = rest
    step = pl.program_id(0)
    core = lax.axis_index("core")
    blocks = pl.num_programs(0) - 1

    @pl.when(step == 0)
    def _():
        table_ref[...] = jnp.zeros_like(table_ref)
        table_ref[4:5, :] = sums_ref[0:1, :]
        table_ref[5:6, :] = sums_ref[8:9, :]
        table_ref[6:7, :] = bias0_ref[...]
        grad_ref[:, 2 * D : 2 * D + 2 * HD] = gpair_ref[...]
        table_ref[7:8, :] = ffn_units(
            placed, h_ref, ht_ref, g_ref, bias_ref, up_ref, down_ref, grad_ref, act_ref, dz_ref
        )

    def tokens(first):
        spot = pl.ds(pl.multiple_of((step - 1) * BLK, BLK), BLK)
        heads = o_ref[...].T
        near = dot(heads, out_keep_ref[...], ((1,), (0,)))
        away = dot(heads, out_got_ref[...], ((1,), (0,)))
        low, high = jnp.where(core == 0, near, away), jnp.where(core == 0, away, near)
        out = mlp_ref[...] + dot(act_ref[spot, :], down_ref[...], ((1,), (0,)))
        out = out + jnp.concatenate([low, high], axis=1)
        two = dh_in_ref[...] + dot(dz_ref[spot, :], up_ref[...], ((1,), (1,)))
        one = dot(dq_ref[...].T, w_ref[:, :HALF], ((1,), (1,)))
        if first:
            one = one + pair_ref[...]
        unit, _ = standard(x_ref[...])
        scaled = one * rows_ref[0:1, :] + two * rows_ref[2:3, :]
        refs = (keep_ref, tkeep_ref) if first else (send_ref, tsend_ref)
        refs[0][...], refs[1][...] = out, scaled
        for i, value in enumerate((one * unit, one, two * unit, two)):
            table_ref[i : i + 1, :] += jnp.sum(value, axis=0, keepdims=True)

    @pl.when((step > 0) & (step <= blocks // 2))
    def _():
        tokens(True)

    @pl.when(step > blocks // 2)
    def _():
        tokens(False)

    @pl.when(step == pl.num_programs(0) - 1)
    def _():
        grad_ref[:, 2 * D + 2 * HD :] = table_ref[...].T.astype(BF)


def feed_forward(normed, normed_t, grad_out, bias, parts, held, *more):
    tokens, width = normed.shape
    hidden = bias.shape[1]
    blocks = tokens // BLK

    def whole(rows, columns):
        return pl.BlockSpec((rows, columns), lambda i: (0, 0))

    def block(first, last):
        return pl.BlockSpec((BLK, width), lambda i: (jnp.clip(i - 1 - first, 0, last - first), 0))

    every, own, other = block(0, blocks - 1), block(0, blocks // 2 - 1), block(blocks // 2, blocks - 1)
    across = pl.BlockSpec((HALF, BLK), lambda i: (0, jnp.maximum(i - 1, 0)))
    in_specs = [
        whole(tokens, width),
        whole(width, tokens),
        whole(tokens, width),
        whole(1, hidden),
    ]
    in_specs += (
        [whole(width, hidden), whole(hidden, width)]
        if parts is None
        else [pl.BlockSpec(memory_space=pl.ANY)] * 4
    )
    rows = jax.ShapeDtypeStruct((tokens, width), F32)
    side = jax.ShapeDtypeStruct((tokens // 2, width), F32)
    scratch = [pltpu.VMEM((tokens, hidden), BF), pltpu.VMEM((tokens, hidden), BF)]
    if not more:
        kernel = ffn_first_kernel
        shapes = (
            rows,
            rows,
            jax.ShapeDtypeStruct((width, 2 * width), BF),
            jax.ShapeDtypeStruct((1, hidden), F32),
        )
        out_specs = (every, every, whole(width, 2 * width), whole(1, hidden))
    else:
        kernel = ffn_second_kernel
        in_specs += [
            every,
            every,
            every,
            across,
            across,
            whole(width, more[5].shape[1]),
            whole(HALF, HALF),
            whole(HALF, HALF),
            own,
            whole(8, width),
            whole(16, width),
            whole(1, hidden),
            whole(width, 2 * HD),
        ]
        wide = 2 * width + 2 * HD + 128
        shapes = (side, side, side, side, jax.ShapeDtypeStruct((width, wide), BF))
        out_specs = (own, other, own, other, whole(width, wide))
        scratch.append(pltpu.VMEM((128, width), F32))
    if parts is not None:
        scratch += [
            pltpu.VMEM((width, hidden), BF),
            pltpu.VMEM((hidden, width), BF),
            pltpu.SemaphoreType.DMA((32,)),
        ]
    return pl.pallas_call(
        functools.partial(kernel, parts),
        out_shape=shapes,
        grid=(1 + blocks,),
        in_specs=in_specs,
        out_specs=out_specs,
        scratch_shapes=scratch,
        compiler_params=pltpu.CompilerParams(
            dimension_semantics=("arbitrary",), vmem_limit_bytes=56 << 20
        ),
        cost_estimate=pl.CostEstimate(
            flops=12 * tokens * width * hidden,
            transcendentals=2 * tokens * hidden,
            bytes_accessed=8 * width * hidden + 20 * tokens * width,
        ),
        name="ffn",
    )(normed, normed_t, grad_out, bias, *held, *more)


def shards(
    tokens,
    segments,
    ln1_gain,
    ln1_bias,
    ln2_gain,
    ln2_bias,
    q_weight,
    q_bias,
    kv_weight,
    k_bias,
    out_weight,
    out_bias,
    up_weight,
    up_bias,
    down_weight,
    cotangent,
):
    core, chip = lax.axis_index("core"), lax.axis_index("chip")
    chips = lax.axis_size("rows") * lax.axis_size("chip")
    own = tokens.shape[1]
    both = 2 * own
    rows = q_weight.shape[0]
    hidden = up_bias.shape[0]
    half = hidden // 2
    back_chips = DOC // both
    own_tokens, own_grad = tokens[0], cotangent[0]

    def half_columns(array, which):
        return lax.dynamic_slice_in_dim(
            array, which * (array.shape[1] // 2), array.shape[1] // 2, 1
        )

    def first(which):
        return jnp.concatenate(
            [half_columns(q_weight, which), half_columns(out_weight, which), kv_weight], axis=1
        )

    up_blocks = up_weight

    def up_half(which):
        block = up_blocks.reshape(rows, chips, 2, 2, half)
        block = lax.dynamic_index_in_dim(block, which, 2, keepdims=False)
        return block.transpose(0, 2, 1, 3).reshape(rows, FF // 2)

    flat = (ln1_gain, ln1_bias, ln2_gain, ln2_bias, q_bias, out_bias)
    if square_line():
        vectors = jnp.concatenate(
            [vector.reshape(1, rows) for vector in flat] + [up_bias.reshape(hidden // rows, rows)]
        )
        vectors = jnp.pad(vectors, ((0, 16 - vectors.shape[0]), (0, 0)))
        mine, theirs = pack(q_weight, out_weight, kv_weight, vectors)
        attn_piece = by_core(core, mine, core_swap(theirs), 0)
        segments, up_blocks = after((segments, up_blocks), attn_piece)
        attn_line = jnp.concatenate(gather_line(attn_piece))
        attn_rows = gather_rows(attn_line)
        up_piece = by_core(core, up_half(core), core_swap(up_half(1 - core)), 0)
        ff_piece = jnp.concatenate([up_piece[:, :D], up_piece[:, D:], down_weight], axis=0)
        ff_line = gather_line(after(ff_piece, attn_line))
        other_tokens = core_swap(own_tokens)
        features = jnp.concatenate([own_tokens, other_tokens], axis=0)
        grad_out = jnp.concatenate([own_grad, core_swap(own_grad)], axis=0)
        attn_rows, grad_out, features = lax.optimization_barrier((attn_rows, grad_out, features))
    else:
        weights = gather_whole(by_core(core, first(core), core_swap(first(1 - core)), 0))
        every = ("rows", "chip", "core")
        table = lax.all_gather(jnp.stack(flat), every, axis=1, tiled=True).astype(F32)
        vector_rows = jnp.pad(table, ((0, 2), (0, 0)))
        bias = gather_whole(up_bias).astype(F32).reshape(chips, 2, half)
        hidden_bias = jnp.pad(bias.transpose(1, 0, 2).reshape(2, D), ((0, 6), (0, 0)))

    if not square_line():
        other_tokens = core_swap(own_tokens)
        features = jnp.concatenate([own_tokens, other_tokens], axis=0)
        grad_out = jnp.concatenate([own_grad, core_swap(own_grad)], axis=0)

    ids = lax.broadcasted_iota(jnp.int32, (MAX_SEGS, 1), 0)
    doc_starts = jnp.sum((segments < ids).astype(jnp.int32), axis=1, keepdims=True)
    first_place, second_place = (chip * 2 + core) * own, (chip * 2 + 1 - core) * own
    span = lax.broadcasted_iota(jnp.int32, (1, own), 1)
    places = jnp.concatenate([first_place + span, second_place + span], axis=1)
    segs = jnp.concatenate(
        [
            lax.dynamic_slice(segments, (0, first_place), (1, own)),
            lax.dynamic_slice(segments, (0, second_place), (1, own)),
        ],
        axis=1,
    )
    starts = jnp.sum(jnp.where(segs == ids, doc_starts, 0), axis=0, keepdims=True)
    relative = places - starts
    frequency = 10000.0 ** (-(jnp.arange(ROT // 2, dtype=F32) * 2.0 / ROT))
    angles = relative.astype(F32) * frequency[:, None]
    cosine, sine = jnp.cos(angles), jnp.sin(angles)
    window_start = (chip - back_chips) * both
    pos = jnp.concatenate(
        [starts - window_start, places - window_start, jnp.zeros((6, both), jnp.int32)], axis=0
    )
    firsts, lasts = pos[:, ::BLK], pos[:, BLK - 1 :: BLK]
    scal = jnp.concatenate(
        [
            core.reshape(1),
            jnp.stack([firsts[0] // BLK, lasts[1] // BLK + 1, lasts[0]], axis=1).reshape(-1),
        ]
    ).astype(jnp.int32)


    bias_column = k_bias.astype(F32)[:, None]
    if square_line():
        weights, vector_rows, hidden_bias, *fronts = front(
            attn_rows, own_tokens, other_tokens, bias_column, cosine, sine
        )
    else:
        fronts = front(
            (weights, vector_rows), own_tokens, other_tokens, bias_column, cosine, sine
        )
    normed_one, normed_two, normed_two_t, query_t, own_pairs, keep, send = fronts
    got = core_swap(send)
    mine = jnp.concatenate(
        [chip_shift(own_pairs, k, False) for k in range(back_chips, 0, -1)] + [own_pairs], axis=0
    )
    theirs = core_swap(mine)
    if square_line():
        ff_rows = gather_rows(after(jnp.concatenate(ff_line), attn_rows))

    heads = attention(scal, query_t, grad_out, keep, got, pos, cosine, sine, mine, theirs)
    if square_line():
        heads, ff_rows = lax.optimization_barrier((heads, ff_rows))
    out_t, grad_query_t, pair_mine, pair_theirs = heads
    pair_got = core_swap(pair_theirs)
    grad_query, proj_keep, proj_send, sums = after_heads(
        out_t, grad_query_t, normed_one, grad_out
    )
    proj_got = core_swap(proj_send)
    if square_line():
        pair_got, proj_got = after((pair_got, proj_got), sums)
        parts = [((i * 2 * rows, 2 * rows, 0), ((2 + i) * 2 * rows, 2 * rows, 1)) for i in range(2)]
        held = [ff_rows, ff_rows]
    else:
        up_whole = gather_whole(by_core(core, up_half(core), core_swap(up_half(1 - core)), 0))
        down_whole = gather_whole(down_weight).reshape(chips, 2, half, D)
        down_whole = down_whole.transpose(1, 0, 2, 3).reshape(2, D, D)
        parts = [None, None]
        held = [(up_whole[:, i * D : (i + 1) * D], down_whole[i]) for i in range(2)]
    pair_sum = pair_mine + pair_got
    arrived = [
        chip_shift(
            pair_sum[(back_chips - k) * own : (back_chips - k + 1) * own].astype(BF), -k, False
        )
        for k in range(1, back_chips + 1)
    ]
    grad_proj = by_core(core, proj_keep, proj_got, 0)
    attn_terms = jnp.concatenate([grad_query, grad_proj], axis=1)
    if square_line():
        attn_plane, attn_one = reduce_rows(attn_terms)
    grad_pair, grad_one_pair, key_bias = after_pairs(
        pair_sum, *arrived, normed_one, weights, cosine, sine
    )
    key_bias = key_bias[0, :HD]

    inputs = (normed_two, normed_two_t, grad_out)
    if square_line():
        other_bias = core_swap(key_bias)
    first = feed_forward(*inputs, hidden_bias[0:1], parts[0], held[0])
    if square_line():
        first, other_bias = lax.optimization_barrier((after(first, attn_one), other_bias))
        key_bias = key_bias + other_bias
    mlp, grad_two, terms0, bias0 = first
    if square_line():
        plane0, one0 = reduce_rows(terms0)
        other_bias = line_swap(key_bias, 1)
    part, part_send, scaled, scaled_send, terms1 = second = feed_forward(
        *inputs,
        hidden_bias[1:2],
        parts[1],
        held[1],
        mlp,
        grad_two,
        features,
        out_t,
        grad_query_t,
        weights,
        keep,
        got,
        grad_one_pair,
        vector_rows,
        sums,
        bias0,
        grad_pair,
    )
    part, part_send, scaled, scaled_send, terms1 = second
    if square_line():
        (part, part_send, scaled, scaled_send), one0, other_bias = lax.optimization_barrier(
            ((part, part_send, scaled, scaled_send), one0, other_bias)
        )
        key_bias = key_bias + other_bias
    part_got, scaled_got = core_swap(part_send), core_swap(scaled_send)

    def finish(part_got, scaled_got):
        layer_out = own_tokens.astype(F32) + part + part_got + vector_rows[5:6]
        total = scaled + scaled_got
        unit, spread = standard(own_tokens)
        input_grad = own_grad.astype(F32) + spread * (
            total
            - jnp.mean(total, axis=-1, keepdims=True)
            - unit * jnp.mean(total * unit, axis=-1, keepdims=True)
        )
        return layer_out.astype(BF), input_grad

    def split(value):
        return (
            lax.dynamic_slice_in_dim(value, core * rows, rows, 0),
            core_swap(lax.dynamic_slice_in_dim(value, (1 - core) * rows, rows, 0)),
        )

    def blocks(first_half, second_half):
        return jnp.stack(
            [value.reshape(rows, chips, half) for value in (first_half, second_half)], axis=2
        ).reshape(rows, chips, 1, hidden)

    if square_line():
        plane1, one1 = reduce_rows(terms1)
        other_bias = line_swap(after(key_bias, part_got), 2)
        own0, three0 = reduce_third(plane0, after(one0, part_got, scaled_got))
        layer_out, input_grad = finish(part_got, scaled_got)
        three0, layer_out, input_grad, other_bias = lax.optimization_barrier(
            (three0, layer_out, input_grad, other_bias)
        )
        key_bias = key_bias + other_bias
        attn_own, attn_three = reduce_third(attn_plane, after(attn_one, three0))
        sum0 = reduce_last(own0, three0)
        one1, attn_three, sum0 = lax.optimization_barrier((one1, attn_three, sum0))
        own1, three1 = reduce_third(plane1, one1)
        other_bias = rows_swap(after(key_bias, one1), 1)
        key_bias = key_bias + other_bias
        attn_split = split(reduce_last(attn_own, after(attn_three, other_bias)))
        up_split = split(after(sum0, other_bias)[:, :D])
        key_bias_out = key_bias + rows_swap(key_bias, 2)
        mine, theirs = attn_split
        query_out = by_core(core, mine[:, :HALF], theirs[:, :HALF], 1)
        proj_out = by_core(core, mine[:, HALF:], theirs[:, HALF:], 1)
        three1, up_split, query_out, proj_out, key_bias_out = lax.optimization_barrier(
            (three1, up_split, query_out, proj_out, key_bias_out)
        )
        sum1 = reduce_last(own1, three1)
    else:
        layer_out, input_grad = finish(part_got, scaled_got)
        sum0, sum1 = reduce_whole(terms0), reduce_whole(terms1)
        up_split = split(sum0[:, :D])
        mine, theirs = split(reduce_whole(attn_terms))
        query_out = by_core(core, mine[:, :HALF], theirs[:, :HALF], 1)
        proj_out = by_core(core, mine[:, HALF:], theirs[:, HALF:], 1)
        key_bias_out = lax.psum(key_bias, ("rows", "chip", "core"))
    mine, theirs = split(jnp.concatenate([sum1[:, :D], sum1[:, 2 * D :]], axis=1))
    rest = mine[:, D:] + theirs[:, D:]
    pair_out, vector_out = rest[:, : 2 * HD], rest[:, 2 * HD :]
    up_bias_out = sum1[:, 2 * D + 2 * HD + 6 : 2 * D + 2 * HD + 8].T.reshape(hidden)
    up_out = by_core(
        core, blocks(up_split[0], mine[:, :D]), blocks(up_split[1], theirs[:, :D]), 2
    ).reshape(rows, FF)
    down_out = jnp.concatenate([sum0[:, D:], sum1[:, D : 2 * D]], axis=0)
    return (
        layer_out[None],
        input_grad[None],
        vector_out[:, 0],
        vector_out[:, 1],
        vector_out[:, 2],
        vector_out[:, 3],
        query_out,
        vector_out[:, 4],
        pair_out,
        key_bias_out,
        proj_out,
        vector_out[:, 5],
        up_out,
        up_bias_out,
        down_out,
    )


def solution(mesh):
    devices = mesh.devices.reshape(mesh.shape["rows"], mesh.shape["wide"] // 2, 2)
    every, wide = ("rows", "chip", "core"), ("chip", "core")
    matrix, vector, sequence = P(every, None), P(every), P("rows", wide, None)
    return jax.shard_map(
        shards,
        mesh=Mesh(devices, every),
        in_specs=(
            sequence,
            P("rows", None),
            vector,
            vector,
            vector,
            vector,
            matrix,
            vector,
            matrix,
            P(),
            matrix,
            vector,
            matrix,
            vector,
            matrix,
            sequence,
        ),
        out_specs=(
            sequence,
            sequence,
            vector,
            vector,
            vector,
            vector,
            matrix,
            vector,
            matrix,
            P(),
            matrix,
            vector,
            matrix,
            vector,
            matrix,
        ),
        check_vma=False,
    )
```

time: 283 us -> 254 us (0.90)
  Pallas kernels: 101 us -> 80.3 us
  waiting for transfers between devices: 60.5 us -> 52.4 us
    ppermute x19, waiting for transfers between devices: 45.3 us -> 30.4 us  [chip_shift(): return lax.ppermute(value, 'chip', pairs)]
    ppermute x19, starting transfers between devices: 26.2 us -> 38.9 us  [chip_shift(): return lax.ppermute(value, 'chip', pairs)]
    pallas_call x1, Pallas kernels: 42.2 us -> 31.5 us  [attention(): pl.pallas_call(attn_kernel, out_shape=(jax.ShapeDtypeStruct((features, to...]
    pallas_call x7 -> x5, Pallas kernels: 57.8 us -> 48.3 us  [the longest x2 37.8 us: feed_forward(): pl.pallas_call(functools.partial(kernel, parts), out_shape=shapes, grid=(...]
    ppermute x20 -> x17, waiting for transfers between devices: 10.8 us -> 20 us  [rows_swap(): return lax.ppermute(value, 'rows', [(r, r ^ bit) for r in range(4)])]
    ppermute x20 -> x17, starting transfers between devices: 24.8 us -> 16.4 us  [rows_swap(): return lax.ppermute(value, 'rows', [(r, r ^ bit) for r in range(4)])]
    concatenate x9 -> x2, other arithmetic: 4.82 us -> 1.11 us  [the longest x1 1.08 us: shards(): ff_rows = gather_rows(after(jnp.concatenate(ff_line), attn_rows))]
    ppermute x14, starting transfers between devices: 16 us -> 12.4 us  [core_swap(): return lax.ppermute(value, 'core', [(0, 1), (1, 0)])]
  transfers between devices with their start and end apart: 55 -> 52, of which waited for: 20 -> 17; matrix products, arithmetic and copies ran while one was open for 13% -> 10% of each run, Pallas kernels for 32% -> 32%
where the time goes in v3:
time: 254 us; the launch traced here: 249 us
  Pallas kernels  80.3 us (32%)
  starting transfers between devices  67.7 us (27%)
  waiting for transfers between devices  52.4 us (21%)
  local copies, waits for them, and re-layouts  23.9 us (9%)
  other arithmetic  23 us (9%)
    ppermute x19, starting transfers between devices, chip_shift(): return lax.ppermute(value, 'chip', pairs)  38.9 us
    pallas_call x2, Pallas kernels, feed_forward(): pl.pallas_call(functools.partial(kernel, parts), out_shape=shapes, grid=(...  37.8 us
    pallas_call x1, Pallas kernels, attention(): pl.pallas_call(attn_kernel, out_shape=(jax.ShapeDtypeStruct((features, to...  31.5 us
    ppermute x19, waiting for transfers between devices, chip_shift(): return lax.ppermute(value, 'chip', pairs)  30.4 us
    ppermute x17, waiting for transfers between devices, rows_swap(): return lax.ppermute(value, 'rows', [(r, r ^ bit) for r in range(4)])  20 us
    ppermute x17, starting transfers between devices, rows_swap(): return lax.ppermute(value, 'rows', [(r, r ^ bit) for r in range(4)])  16.4 us
    ppermute x14, starting transfers between devices, core_swap(): return lax.ppermute(value, 'core', [(0, 1), (1, 0)])  12.4 us
    unnamed x88, local copies, waits for them, and re-layouts  9.53 us
  transfers between devices with their start and end apart: 52, of which 17 were waited for; matrix products, arithmetic and copies ran while one was open for 10% of the time, Pallas kernels for 32%

profile of v3, /device:TPU:25, one launch (start us, length us, event | category | flops | bytes accessed | tf_op | source)
XLA Modules:
  0.0 249.1 jit_solution(12528793697666962066)
XLA Ops:
  7.6 3.1 %collective-permute-start.3 = (bf16[48,1024]{1,0:T(8,128)(2,1)S(1)}, bf16[48,1024]{1,0:T(8,128)(2,1)S(1)}, u32[]{:S(2)}, u32[]{:S(2)}) collective-permute-start(bf16[48,1024]{1,0:T(8,128)(2,1)S(1)} %maximum_select_fusion.3), channel_id=1, source_target_pairs={{0,2},{2,4},{4,6},{6,0},{1,3},{3,5},{5,7},{7,1},{8,10},{10,12},{12... | collective-permute-start | bytes 294920 | tf_op jit(solution)/shard_map/ppermute | solution.py:41
  19.7 5.9 %collective-permute-done.4.flat_ref = bf16[192,1024]{1,0:T(8,128)(2,1)S(1)} collective-permute-done((bf16[192,1024]{1,0:T(8,128)(2,1)S(1)}, bf16[192,1024]{1,0:T(8,128)(2,1)S(1)}, u32[]{:S(2)}, u32[]{:S(2)}) %collective-permute-start.4) | collective-permute-done | bytes 393248 | tf_op jit(solution)/shard_map/ppermute | solution.py:35
  25.6 3.1 %collective-permute-start.14 = (bf16[192,768]{1,0:T(8,128)(2,1)S(1)}, bf16[192,768]{1,0:T(8,128)(2,1)S(1)}, u32[]{:S(2)}, u32[]{:S(2)}) collective-permute-start(bf16[192,768]{1,0:T(8,128)(2,1)S(1)} %pad_maximum_fusion.7), channel_id=1, source_target_pairs={{0,6},{2,0},{4,2},{6,4},{1,7},{3,1},{5,3},{7,5},{8,14},{10,8},{12,... | collective-permute-start | bytes 884744 | tf_op jit(solution)/shard_map/ppermute | solution.py:41
  32.1 2.4 pad_maximum_fusion.grad_ref.g_ref
  35.0 7.0 %front.1 = (bf16[768,1024]{1,0:T(8,128)(2,1)}, f32[8,768]{1,0:T(8,128)S(1)}, f32[8,768]{1,0:T(8,128)S(1)}, bf16[1024,768]{1,0:T(8,128)(2,1)}, bf16[1024,768]{1,0...) custom-call(bf16[192,1024]{1,0:T(8,128)(2,1)S(1)} %pad_maximum_fusio, ...), custom_call_target="tpu_custom_call" | custom-call | flops 805306368 | bytes 6291456 | tf_op jit(solution)/shard_map/front/pallas_call | solution.py:274
  45.2 5.2 %collective-permute-done.15 = bf16[192,768]{1,0:T(8,128)(2,1)S(1)} collective-permute-done((bf16[192,768]{1,0:T(8,128)(2,1)S(1)}, bf16[192,768]{1,0:T(8,128)(2,1)S(1)}, u32[]{:S(2)}, u32[]{:S(2)}) %collective-permute-start.15) | collective-permute-done | bytes 294944 | tf_op jit(solution)/shard_map/ppermute | solution.py:41
  54.7 7.5 %collective-permute-done.10 = bf16[512,128]{1,0:T(8,128)(2,1)S(1)} collective-permute-done((bf16[512,128]{1,0:T(8,128)(2,1)S(1)}, bf16[512,128]{1,0:T(8,128)(2,1)S(1)}, u32[]{:S(2)}, u32[]{:S(2)}) %collective-permute-start.10) | collective-permute-done | bytes 131104 | tf_op jit(solution)/shard_map/ppermute | solution.py:41
  70.6 31.5 %attention.1 = (bf16[384,1024]{1,0:T(8,128)(2,1)S(1)}, bf16[384,1024]{1,0:T(8,128)(2,1)S(1)}, f32[1536,128]{1,0:T(8,128)S(1)}, f32[1536,128]{1,0:T(8,128)}) custom-call(s32[13]{0:T(128)S(1)} %pad_add_fusion.2.scal_ref, bf16[384,1024]{1,0:T(8,128)(2,1)S(1)} %copy-done.15, bf16[1024,768]{1,0:T(8,128)(2,1)} %pad_maximum_fusion.grad_ref.g_ref, ...), custom_call_target="tpu_custom_call" | custom-call | flops 7247757312 | bytes 3145728 | tf_op jit(solution)/shard_map/attention/pallas_call | solution.py:430
  102.2 2.3 collective-permute-done.18.rest_2_
  114.7 10.6 %collective-permute-start.25 = (bf16[512,128]{1,0:T(8,128)(2,1)}, bf16[512,128]{1,0:T(8,128)(2,1)S(1)}, u32[]{:S(2)}, u32[]{:S(2)}) collective-permute-start(bf16[512,128]{1,0:T(8,128)(2,1)} %get-tuple-element.251), channel_id=1, source_target_pairs={{2,0},{4,2},{6,4},{3,1},{5,3},{7,5},{10,8},{12,10},{14,12},{11,9},... | collective-permute-start | bytes 393224 | tf_op jit(solution)/shard_map/ppermute | solution.py:41
  125.3 5.0 %collective-permute-start.26 = (bf16[512,128]{1,0:T(8,128)(2,1)S(1)}, bf16[512,128]{1,0:T(8,128)(2,1)S(1)}, u32[]{:S(2)}, u32[]{:S(2)}) collective-permute-start(bf16[512,128]{1,0:T(8,128)(2,1)S(1)} %get-tuple-element.250), channel_id=1, source_target_pairs={{4,0},{6,2},{5,1},{7,3},{12,8},{14,10},{13,9},{15,11},{20,16},{22,... | collective-permute-start | bytes 393224 | tf_op jit(solution)/shard_map/ppermute | solution.py:41
  130.7 2.9 %collective-permute-start.23 = (bf16[4,48,768]{2,1,0:T(8,128)(2,1)S(1)}, bf16[4,48,768]{2,1,0:T(8,128)(2,1)S(1)}, u32[]{:S(2)}, u32[]{:S(2)}) collective-permute-start(bf16[4,48,768]{2,1,0:T(8,128)(2,1)S(1)} %get-tuple-element.246), channel_id=1, source_target_pairs={{0,8},{8,0},{16,24},{24,16},{1,9},{9,1},{17,25},{25,17},{2,10},{10... | collective-permute-start | bytes 884744 | tf_op jit(solution)/shard_map/ppermute | solution.py:35
  133.7 15.9 %ffn.2 = (f32[1024,768]{1,0:T(8,128)}, f32[1024,768]{1,0:T(8,128)}, bf16[768,1536]{1,0:T(8,128)(2,1)}, f32[1,768]{1,0:T(1,128)}) custom-call(bf16[1024,768]{1,0:T(8,128)(2,1)} %get-tuple-element.124.h_ref, bf16[768,1024]{1,0:T(8,128)(2,1)} %get-tuple-element.125.ht_ref, bf16[1024,768]{1,0:T(8,128)(2,1)} %pad_maximum_fusion.grad_ref.g_ref, ...), custom_call_target="tpu_custom_call" | custom-call | flops 7247757312 | bytes 20447232 | tf_op jit(solution)/shard_map/ffn/pallas_call | solution.py:721
  155.5 21.9 %ffn.3 = (f32[512,768]{1,0:T(8,128)}, f32[512,768]{1,0:T(8,128)}, f32[512,768]{1,0:T(8,128)}, f32[512,768]{1,0:T(8,128)}, bf16[768,1792]{1,0:T(8,128)(2,1)}) custom-call(bf16[1024,768]{1,0:T(8,128)(2,1)} %get-tuple-element.124.h_ref, bf16[768,1024]{1,0:T(8,128)(2,1)} %get-tuple-element.125.ht_ref, bf16[1024,768]{1,0:T(8,128)(2,1)} %pad_maximum_fusion.grad_ref.g_ref, ...), custom_call_target="tpu_custom_call" | custom-call | flops 7247757312 | bytes 20447232 | tf_op jit(solution)/shard_map/ffn/pallas_call | solution.py:721
  177.4 3.8 %collective-permute-done.29 = bf16[4,48,1536]{2,1,0:T(8,128)(2,1)S(1)} collective-permute-done((bf16[4,48,1536]{2,1,0:T(8,128)(2,1)S(1)}, bf16[4,48,1536]{2,1,0:T(8,128)(2,1)S(1)}, u32[]{:S(2)}, u32[]{:S(2)}) %collective-permute-start.29) | collective-permute-done | bytes 589856 | tf_op jit(solution)/shard_map/ppermute | solution.py:35
  189.5 2.2 fusion.35
  193.1 3.5 %collective-permute-start.34 = (bf16[48,1536]{1,0:T(8,128)(2,1)S(1)}, bf16[48,1536]{1,0:T(8,128)(2,1)S(1)}, u32[]{:S(2)}, u32[]{:S(2)}) collective-permute-start(bf16[48,1536]{1,0:T(8,128)(2,1)S(1)} %get-tuple-element.235), channel_id=1, source_target_pairs={{0,2},{2,4},{4,6},{6,0},{1,3},{3,5},{5,7},{7,1},{8,10},{10,12},{12... | collective-permute-start | bytes 442376 | tf_op jit(solution)/shard_map/ppermute | solution.py:41
  196.6 2.1 collective-permute-done.34
  201.0 6.5 %collective-permute-done.35 = bf16[48,1536]{1,0:T(8,128)(2,1)S(1)} collective-permute-done((bf16[48,1536]{1,0:T(8,128)(2,1)S(1)}, bf16[48,1536]{1,0:T(8,128)(2,1)S(1)}, u32[]{:S(2)}, u32[]{:S(2)}) %collective-permute-start.35) | collective-permute-done | bytes 147488 | tf_op jit(solution)/shard_map/ppermute | solution.py:41
  209.0 2.4 collective-permute-start.42
  213.8 5.3 %collective-permute-done.39 = bf16[4,48,1792]{2,1,0:T(8,128)(2,1)S(1)} collective-permute-done((bf16[4,48,1792]{2,1,0:T(8,128)(2,1)S(1)}, bf16[4,48,1792]{2,1,0:T(8,128)(2,1)S(1)}, u32[]{:S(2)}, u32[]{:S(2)}) %collective-permute-start.39) | collective-permute-done | bytes 688160 | tf_op jit(solution)/shard_map/ppermute | solution.py:35
  222.3 2.6 %collective-permute-start.45 = (bf16[48,1792]{1,0:T(8,128)(2,1)S(1)}, bf16[48,1792]{1,0:T(8,128)(2,1)S(1)}, u32[]{:S(2)}, u32[]{:S(2)}) collective-permute-start(bf16[48,1792]{1,0:T(8,128)(2,1)S(1)} %get-tuple-element.231), channel_id=1, source_target_pairs={{0,4},{2,6},{4,0},{6,2},{1,5},{3,7},{5,1},{7,3},{8,12},{10,14},{12... | collective-permute-start | bytes 516104 | tf_op jit(solution)/shard_map/ppermute | solution.py:41
  227.6 2.2 collective-permute-start.48
  231.7 8.1 %collective-permute-done.45 = bf16[48,1792]{1,0:T(8,128)(2,1)S(1)} collective-permute-done((bf16[48,1792]{1,0:T(8,128)(2,1)S(1)}, bf16[48,1792]{1,0:T(8,128)(2,1)S(1)}, u32[]{:S(2)}, u32[]{:S(2)}) %collective-permute-start.45) | collective-permute-done | bytes 172064 | tf_op jit(solution)/shard_map/ppermute | solution.py:41
  (277 shorter events, 84.2 us)
Async XLA Ops:
  5.1 23.6 %collective-permute-start.8 = (bf16[512,768]{1,0:T(8,128)(2,1)}, bf16[512,768]{1,0:T(8,128)(2,1)S(1)}, u32[]{:S(2)}, u32[]{:S(2)}) collective-permute-start(bf16[512,768]{1,0:T(8,128)(2,1)} %bitcast.234), channel_id=1, source_target_pairs={{0,1},{1,0},{2,3},{3,2},{4,5},{5,4},{6,7},{7,6},{8,9},{9,8},{10,11... | collective-permute-start | bytes 2359304 | tf_op jit(solution)/shard_map/ppermute | solution.py:31
  5.1 25.3 %collective-permute-start.7 = (bf16[512,768]{1,0:T(8,128)(2,1)}, bf16[512,768]{1,0:T(8,128)(2,1)}, u32[]{:S(2)}, u32[]{:S(2)}) collective-permute-start(bf16[512,768]{1,0:T(8,128)(2,1)} %bitcast.240), channel_id=1, source_target_pairs={{0,1},{1,0},{2,3},{3,2},{4,5},{5,4},{6,7},{7,6},{8,9},{9,8},{10,11... | collective-permute-start | bytes 2359304 | tf_op jit(solution)/shard_map/ppermute | solution.py:31
  18.1 16.3 %collective-permute-start.5 = (bf16[192,1024]{1,0:T(8,128)(2,1)S(1)}, bf16[192,1024]{1,0:T(8,128)(2,1)S(1)}, u32[]{:S(2)}, u32[]{:S(2)}) collective-permute-start(bf16[192,1024]{1,0:T(8,128)(2,1)S(1)} %pad_maximum_fusion.4.lines_ref), channel_id=1, source_target_pairs={{0,16},{8,24},{16,0},{24,8},{1,17},{9,25},{17,1},{25,9},{2,18},{10... | collective-permute-start | bytes 1179656 | tf_op jit(solution)/shard_map/ppermute | solution.py:35
  25.6 19.6 %collective-permute-start.14 = (bf16[192,768]{1,0:T(8,128)(2,1)S(1)}, bf16[192,768]{1,0:T(8,128)(2,1)S(1)}, u32[]{:S(2)}, u32[]{:S(2)}) collective-permute-start(bf16[192,768]{1,0:T(8,128)(2,1)S(1)} %pad_maximum_fusion.7), channel_id=1, source_target_pairs={{0,6},{2,0},{4,2},{6,4},{1,7},{3,1},{5,3},{7,5},{8,14},{10,8},{12,... | collective-permute-start | bytes 884744 | tf_op jit(solution)/shard_map/ppermute | solution.py:41
  28.7 21.6 %collective-permute-start.15 = (bf16[192,768]{1,0:T(8,128)(2,1)S(1)}, bf16[192,768]{1,0:T(8,128)(2,1)S(1)}, u32[]{:S(2)}, u32[]{:S(2)}) collective-permute-start(bf16[192,768]{1,0:T(8,128)(2,1)S(1)} %pad_maximum_fusion.7), channel_id=1, source_target_pairs={{0,4},{2,6},{4,0},{6,2},{1,5},{3,7},{5,1},{7,3},{8,12},{10,14},{12... | collective-permute-start | bytes 884744 | tf_op jit(solution)/shard_map/ppermute | solution.py:41
  30.5 19.9 %collective-permute-start.16 = (bf16[192,768]{1,0:T(8,128)(2,1)S(1)}, bf16[192,768]{1,0:T(8,128)(2,1)S(1)}, u32[]{:S(2)}, u32[]{:S(2)}) collective-permute-start(bf16[192,768]{1,0:T(8,128)(2,1)S(1)} %pad_maximum_fusion.7), channel_id=1, source_target_pairs={{0,2},{2,4},{4,6},{6,0},{1,3},{3,5},{5,7},{7,1},{8,10},{10,12},{12... | collective-permute-start | bytes 884744 | tf_op jit(solution)/shard_map/ppermute | solution.py:41
  42.0 20.2 %collective-permute-start.10 = (bf16[512,128]{1,0:T(8,128)(2,1)S(1)}, bf16[512,128]{1,0:T(8,128)(2,1)S(1)}, u32[]{:S(2)}, u32[]{:S(2)}) collective-permute-start(bf16[512,128]{1,0:T(8,128)(2,1)S(1)} %get-tuple-element.131), channel_id=1, source_target_pairs={{0,4},{2,6},{1,5},{3,7},{8,12},{10,14},{9,13},{11,15},{16,20},{18,... | collective-permute-start | bytes 393224 | tf_op jit(solution)/shard_map/ppermute | solution.py:41
  43.3 19.5 %collective-permute-start.11 = (bf16[512,128]{1,0:T(8,128)(2,1)S(1)}, bf16[512,128]{1,0:T(8,128)(2,1)S(1)}, u32[]{:S(2)}, u32[]{:S(2)}) collective-permute-start(bf16[512,128]{1,0:T(8,128)(2,1)S(1)} %get-tuple-element.131), channel_id=1, source_target_pairs={{0,2},{2,4},{4,6},{1,3},{3,5},{5,7},{8,10},{10,12},{12,14},{9,11},... | collective-permute-start | bytes 393224 | tf_op jit(solution)/shard_map/ppermute | solution.py:41
  51.4 50.7 %collective-permute-start.17 = (bf16[768,768]{1,0:T(8,128)(2,1)}, bf16[768,768]{1,0:T(8,128)(2,1)}, u32[]{:S(2)}, u32[]{:S(2)}) collective-permute-start(bf16[768,768]{1,0:T(8,128)(2,1)} %pad_maximum_fusion.2.rest_0_), channel_id=1, source_target_pairs={{0,8},{8,0},{16,24},{24,16},{1,9},{9,1},{17,25},{25,17},{2,10},{10... | collective-permute-start | bytes 3538952 | tf_op jit(solution)/shard_map/ppermute | solution.py:35
  52.6 51.8 %collective-permute-start.18 = (bf16[768,768]{1,0:T(8,128)(2,1)}, bf16[768,768]{1,0:T(8,128)(2,1)}, u32[]{:S(2)}, u32[]{:S(2)}) collective-permute-start(bf16[768,768]{1,0:T(8,128)(2,1)} %pad_maximum_fusion.2.rest_0_), channel_id=1, source_target_pairs={{0,16},{8,24},{16,0},{24,8},{1,17},{9,25},{17,1},{25,9},{2,18},{10... | collective-permute-start | bytes 3538952 | tf_op jit(solution)/shard_map/ppermute | solution.py:35
  54.7 50.9 %collective-permute-start.19 = (bf16[768,768]{1,0:T(8,128)(2,1)}, bf16[768,768]{1,0:T(8,128)(2,1)}, u32[]{:S(2)}, u32[]{:S(2)}) collective-permute-start(bf16[768,768]{1,0:T(8,128)(2,1)} %pad_maximum_fusion.2.rest_0_), channel_id=1, source_target_pairs={{0,24},{8,16},{16,8},{24,0},{1,25},{9,17},{17,9},{25,1},{2,26},{10... | collective-permute-start | bytes 3538952 | tf_op jit(solution)/shard_map/ppermute | solution.py:35
  114.7 34.9 %collective-permute-start.25 = (bf16[512,128]{1,0:T(8,128)(2,1)}, bf16[512,128]{1,0:T(8,128)(2,1)S(1)}, u32[]{:S(2)}, u32[]{:S(2)}) collective-permute-start(bf16[512,128]{1,0:T(8,128)(2,1)} %get-tuple-element.251), channel_id=1, source_target_pairs={{2,0},{4,2},{6,4},{3,1},{5,3},{7,5},{10,8},{12,10},{14,12},{11,9},... | collective-permute-start | bytes 393224 | tf_op jit(solution)/shard_map/ppermute | solution.py:41
  125.3 24.3 %collective-permute-start.26 = (bf16[512,128]{1,0:T(8,128)(2,1)S(1)}, bf16[512,128]{1,0:T(8,128)(2,1)S(1)}, u32[]{:S(2)}, u32[]{:S(2)}) collective-permute-start(bf16[512,128]{1,0:T(8,128)(2,1)S(1)} %get-tuple-element.250), channel_id=1, source_target_pairs={{4,0},{6,2},{5,1},{7,3},{12,8},{14,10},{13,9},{15,11},{20,16},{22,... | collective-permute-start | bytes 393224 | tf_op jit(solution)/shard_map/ppermute | solution.py:41
  130.7 20.9 %collective-permute-start.22 = (bf16[4,48,768]{2,1,0:T(8,128)(2,1)S(1)}, bf16[4,48,768]{2,1,0:T(8,128)(2,1)S(1)}, u32[]{:S(2)}, u32[]{:S(2)}) collective-permute-start(bf16[4,48,768]{2,1,0:T(8,128)(2,1)S(1)} %get-tuple-element.247), channel_id=1, source_target_pairs={{0,24},{8,16},{16,8},{24,0},{1,25},{9,17},{17,9},{25,1},{2,26},{10... | collective-permute-start | bytes 884744 | tf_op jit(solution)/shard_map/ppermute | solution.py:35
  130.7 20.8 %collective-permute-start.23 = (bf16[4,48,768]{2,1,0:T(8,128)(2,1)S(1)}, bf16[4,48,768]{2,1,0:T(8,128)(2,1)S(1)}, u32[]{:S(2)}, u32[]{:S(2)}) collective-permute-start(bf16[4,48,768]{2,1,0:T(8,128)(2,1)S(1)} %get-tuple-element.246), channel_id=1, source_target_pairs={{0,8},{8,0},{16,24},{24,16},{1,9},{9,1},{17,25},{25,17},{2,10},{10... | collective-permute-start | bytes 884744 | tf_op jit(solution)/shard_map/ppermute | solution.py:35
  133.7 17.9 %collective-permute-start.24 = (bf16[4,48,768]{2,1,0:T(8,128)(2,1)S(1)}, bf16[4,48,768]{2,1,0:T(8,128)(2,1)S(1)}, u32[]{:S(2)}, u32[]{:S(2)}) collective-permute-start(bf16[4,48,768]{2,1,0:T(8,128)(2,1)S(1)} %get-tuple-element.245), channel_id=1, source_target_pairs={{0,16},{8,24},{16,0},{24,8},{1,17},{9,25},{17,1},{25,9},{2,18},{10... | collective-permute-start | bytes 884744 | tf_op jit(solution)/shard_map/ppermute | solution.py:35
  152.3 25.1 %collective-permute-start.31 = (f32[64]{0:T(128)S(1)}, f32[64]{0:T(128)S(1)}, u32[]{:S(2)}, u32[]{:S(2)}) collective-permute-start(f32[64]{0:T(128)S(1)} %fusion.34), channel_id=1, source_target_pairs={{0,2},{2,0},{4,6},{6,4},{1,3},{3,1},{5,7},{7,5},{8,10},{10,8},{12,... | collective-permute-start | bytes 776 | tf_op jit(solution)/shard_map/ppermute | solution.py:131
  152.5 24.9 %collective-permute-start.28 = (bf16[4,48,1536]{2,1,0:T(8,128)(2,1)S(1)}, bf16[4,48,1536]{2,1,0:T(8,128)(2,1)S(1)}, u32[]{:S(2)}, u32[]{:S(2)}) collective-permute-start(bf16[4,48,1536]{2,1,0:T(8,128)(2,1)S(1)} %get-tuple-element.241), channel_id=1, source_target_pairs={{0,24},{8,16},{16,8},{24,0},{1,25},{9,17},{17,9},{25,1},{2,26},{10... | collective-permute-start | bytes 1769480 | tf_op jit(solution)/shard_map/ppermute | solution.py:35
  153.8 27.4 %collective-permute-start.29 = (bf16[4,48,1536]{2,1,0:T(8,128)(2,1)S(1)}, bf16[4,48,1536]{2,1,0:T(8,128)(2,1)S(1)}, u32[]{:S(2)}, u32[]{:S(2)}) collective-permute-start(bf16[4,48,1536]{2,1,0:T(8,128)(2,1)S(1)} %get-tuple-element.240), channel_id=1, source_target_pairs={{0,8},{8,0},{16,24},{24,16},{1,9},{9,1},{17,25},{25,17},{2,10},{10... | collective-permute-start | bytes 1769480 | tf_op jit(solution)/shard_map/ppermute | solution.py:35
  155.5 25.9 %collective-permute-start.30 = (bf16[4,48,1536]{2,1,0:T(8,128)(2,1)S(1)}, bf16[4,48,1536]{2,1,0:T(8,128)(2,1)S(1)}, u32[]{:S(2)}, u32[]{:S(2)}) collective-permute-start(bf16[4,48,1536]{2,1,0:T(8,128)(2,1)S(1)} %get-tuple-element.239), channel_id=1, source_target_pairs={{0,16},{8,24},{16,0},{24,8},{1,17},{9,25},{17,1},{25,9},{2,18},{10... | collective-permute-start | bytes 1769480 | tf_op jit(solution)/shard_map/ppermute | solution.py:35
  186.6 24.8 %collective-permute-start.38 = (bf16[4,48,1792]{2,1,0:T(8,128)(2,1)S(1)}, bf16[4,48,1792]{2,1,0:T(8,128)(2,1)S(1)}, u32[]{:S(2)}, u32[]{:S(2)}) collective-permute-start(bf16[4,48,1792]{2,1,0:T(8,128)(2,1)S(1)} %get-tuple-element.238), channel_id=1, source_target_pairs={{0,24},{8,16},{16,8},{24,0},{1,25},{9,17},{17,9},{25,1},{2,26},{10... | collective-permute-start | bytes 2064392 | tf_op jit(solution)/shard_map/ppermute | solution.py:35
  187.8 31.4 %collective-permute-start.39 = (bf16[4,48,1792]{2,1,0:T(8,128)(2,1)S(1)}, bf16[4,48,1792]{2,1,0:T(8,128)(2,1)S(1)}, u32[]{:S(2)}, u32[]{:S(2)}) collective-permute-start(bf16[4,48,1792]{2,1,0:T(8,128)(2,1)S(1)} %get-tuple-element.237), channel_id=1, source_target_pairs={{0,8},{8,0},{16,24},{24,16},{1,9},{9,1},{17,25},{25,17},{2,10},{10... | collective-permute-start | bytes 2064392 | tf_op jit(solution)/shard_map/ppermute | solution.py:35
  188.8 30.9 %collective-permute-start.40 = (bf16[4,48,1792]{2,1,0:T(8,128)(2,1)S(1)}, bf16[4,48,1792]{2,1,0:T(8,128)(2,1)S(1)}, u32[]{:S(2)}, u32[]{:S(2)}) collective-permute-start(bf16[4,48,1792]{2,1,0:T(8,128)(2,1)S(1)} %get-tuple-element.236), channel_id=1, source_target_pairs={{0,16},{8,24},{16,0},{24,8},{1,17},{9,25},{17,1},{25,9},{2,18},{10... | collective-permute-start | bytes 2064392 | tf_op jit(solution)/shard_map/ppermute | solution.py:35
  222.3 17.5 %collective-permute-start.45 = (bf16[48,1792]{1,0:T(8,128)(2,1)S(1)}, bf16[48,1792]{1,0:T(8,128)(2,1)S(1)}, u32[]{:S(2)}, u32[]{:S(2)}) collective-permute-start(bf16[48,1792]{1,0:T(8,128)(2,1)S(1)} %get-tuple-element.231), channel_id=1, source_target_pairs={{0,4},{2,6},{4,0},{6,2},{1,5},{3,7},{5,1},{7,3},{8,12},{10,14},{12... | collective-permute-start | bytes 516104 | tf_op jit(solution)/shard_map/ppermute | solution.py:41
  (72 other events, 527.8 us)
